TPU v7x, 32 devices: a whole 2x2x4 slice. The times are simulated.
32 devices in a mesh: groups: 2 (over x), seq: 16 (over z, y, core).
Axes of the slice: x: 2, y: 2, z: 4, core: 2. Of those that a mesh axis runs over, the one named last changes fastest.
Arguments:
- queries: bfloat16 [1024, 2048], P(('groups', 'seq')), parts along dimension 0, may hold values from -2048 to 2048
- new_keys: bfloat16 [1024, 512], P(('groups', 'seq')), parts along dimension 0, may hold values from -16 to 16
- new_values: bfloat16 [1024, 512], P(('groups', 'seq')), parts along dimension 0, may hold values from -6 to 6
- keys: bfloat16 [131072, 512], P(('groups', 'seq')), parts along dimension 0, may hold values from -16 to 16
- values: bfloat16 [131072, 512], P(('groups', 'seq')), parts along dimension 0, may hold values from -6 to 6
- page_list: int32 [256, 3], P(('groups', 'seq')), parts along dimension 0, may hold values from 0 to 15, as said below
- out_weight: bfloat16 [2048, 4096], P(None, 'seq'), may hold values from -0.125 to 0.125
Outputs:
- projected: bfloat16 [1024, 4096], P(('groups', 'seq')), parts along dimension 0
There are 2 independent parts, one for each index of `groups`. A program takes and returns all parts, laid end to end along the dimension named above; an argument that names none is the same for every part. Nothing has to cross between parts.
Inputs may be any that keep to these rules, and one draw needn't show every extreme that they name: `page_list`: the 3 pages of a tile are distinct. Among the 8 tiles of one index of seq (tiles 8 * i to 8 * (i + 1) - 1) no page is listed more than 3 times, and some page is listed exactly 3 times by the tiles of every index.
All inputs are finite; a program needn't handle non-finite values.
Results may differ from a plain program's by a relative error of at most 0.0058.
Values may be sent and summed in bfloat16 or wider, within the bound.
No kernel may reach another device: no remote copies, remote signals or barrier semaphores. Data moves between devices by JAX's collectives and lax.ppermute only.
A program may use at most 192 MiB of HBM per device.

v0:
```python
import math

import jax
import jax.numpy as jnp
from jax import lax
from jax.sharding import PartitionSpec as P

HQ = 16
KVH = 4
HD = 128


def shards(queries, new_keys, new_values, keys, values, page_list, out_weight):
    members = lax.axis_size("seq")
    tile_count, list_width = page_list.shape
    row_total, features = queries.shape
    tile_rows = row_total // tile_count
    per_group = HQ // KVH
    capacity = max(1, 2 * tile_count * list_width // members)
    slot_count = members * capacity
    order_ids = jnp.arange(tile_count)
    before = order_ids[None, :] < order_ids[:, None]
    matches = page_list[:, :, None, None] == page_list[None, None, :, :]
    ranking = jnp.sum(matches & before[:, None, :, None], axis=(2, 3))
    slot_index = page_list * capacity + ranking
    placing = jnp.any(
        slot_index[:, :, None] == jnp.arange(slot_count, dtype=jnp.int32)[None, None, :], axis=1
    )
    placing = placing.astype(jnp.bfloat16)
    outgoing = lax.dot_general(
        placing,
        queries.reshape(tile_count, tile_rows * features),
        (((0,), (0,)), ((), ())),
        preferred_element_type=jnp.float32,
    )
    outgoing = outgoing.astype(jnp.bfloat16).reshape(members, capacity, tile_rows, features)
    incoming = lax.all_to_all(outgoing, "seq", split_axis=0, concat_axis=0, tiled=True)
    layout = incoming.shape
    row_count = layout[0] * layout[1] * layout[2]
    flattened = incoming.reshape(row_count, features)
    pieces = []
    maxima = []
    totals = []
    for head_group in range(KVH):
        column_start = head_group * per_group * HD
        asked = flattened[:, column_start : column_start + per_group * HD].reshape(
            row_count * per_group, HD
        )
        cached_keys = keys[:, head_group * HD : (head_group + 1) * HD]
        cached_values = values[:, head_group * HD : (head_group + 1) * HD]
        scores = lax.dot_general(
            asked, cached_keys, (((1,), (1,)), ((), ())), preferred_element_type=jnp.float32
        ) / math.sqrt(HD)
        highest = jnp.max(scores, axis=1, keepdims=True)
        weights = jnp.exp(scores - highest)
        summed = jnp.sum(weights, axis=1, keepdims=True)
        mixed = (
            jnp.dot(weights.astype(jnp.bfloat16), cached_values, preferred_element_type=jnp.float32)
            / summed
        )
        pieces.append(mixed.reshape(row_count, per_group * HD))
        maxima.append(highest.reshape(row_count, per_group))
        totals.append(summed.reshape(row_count, per_group))
    partial_out = jnp.concatenate(pieces, axis=1).astype(jnp.bfloat16).reshape(layout)
    stat_shape = layout[:3] + (HQ,)
    maxima_all = jnp.concatenate(maxima, axis=1).reshape(stat_shape)
    totals_all = jnp.concatenate(totals, axis=1).reshape(stat_shape)
    returned = lax.all_to_all(partial_out, "seq", split_axis=0, concat_axis=0, tiled=True)
    returned_max = lax.all_to_all(maxima_all, "seq", split_axis=0, concat_axis=0, tiled=True)
    returned_total = lax.all_to_all(totals_all, "seq", split_axis=0, concat_axis=0, tiled=True)
    returned, returned_max, returned_total = (returned, returned_max, returned_total)
    asked_local = queries.reshape(tile_count, tile_rows, KVH, per_group, HD)
    fresh_keys = new_keys.reshape(tile_count, tile_rows, KVH, HD)
    fresh_values = new_values.reshape(tile_count, tile_rows, KVH, HD)
    own_scores = jnp.einsum(
        "tqgjd,tkgd->tqgjk", asked_local, fresh_keys, preferred_element_type=jnp.float32
    ) / math.sqrt(HD)
    causal = jnp.arange(tile_rows)[:, None] >= jnp.arange(tile_rows)[None, :]
    own_scores = jnp.where(causal[None, :, None, None, :], own_scores, -jnp.inf)
    own_max = jnp.max(own_scores, axis=-1)
    own_weights = jnp.exp(own_scores - own_max[..., None])
    own_total = jnp.sum(own_weights, axis=-1)
    own_out = (
        jnp.einsum(
            "tqgjk,tkgd->tqgjd",
            own_weights.astype(jnp.bfloat16),
            fresh_values,
            preferred_element_type=jnp.float32,
        )
        / own_total[..., None]
    )
    own_out = own_out.reshape(tile_count, tile_rows, HQ, HD)
    own_max = own_max.reshape(tile_count, tile_rows, HQ)
    own_total = own_total.reshape(tile_count, tile_rows, HQ)
    got_out = returned.reshape(slot_count, tile_rows, HQ, HD)
    got_max = returned_max.reshape(slot_count, tile_rows, HQ)
    got_total = returned_total.reshape(slot_count, tile_rows, HQ)
    chosen_out = got_out[slot_index].astype(jnp.float32)
    chosen_max = got_max[slot_index]
    chosen_total = got_total[slot_index]
    overall = jnp.maximum(own_max, jnp.max(chosen_max, axis=1))
    own_factor = own_total * jnp.exp(own_max - overall)
    page_factor = chosen_total * jnp.exp(chosen_max - overall[:, None])
    denom = own_factor + jnp.sum(page_factor, axis=1)
    numer = own_factor[..., None] * own_out + jnp.sum(page_factor[..., None] * chosen_out, axis=1)
    attended = (numer / denom[..., None]).reshape(row_total, features).astype(jnp.bfloat16)
    return jnp.dot(
        attended,
        lax.all_gather(out_weight, "seq", axis=1, tiled=True),
        preferred_element_type=jnp.float32,
    ).astype(jnp.bfloat16)


def solution(mesh):
    return jax.shard_map(
        shards,
        mesh=mesh,
        in_specs=(
            P(("groups", "seq"), None),
            P(("groups", "seq"), None),
            P(("groups", "seq"), None),
            P(("groups", "seq"), None),
            P(("groups", "seq"), None),
            P(("groups", "seq"), None),
            P(None, "seq"),
        ),
        out_specs=P(("groups", "seq"), None),
        check_vma=False,
    )
```

profile of v0, /device:TPU:0, one launch (start us, length us, event | category | flops | bytes accessed | tf_op | source)
XLA Modules:
  0.0 197.5 jit_solution(5072526256052859871)
XLA Ops:
  6.5 0.7 all-gather.2.cloned.1.call-update
  7.3 1.0 reshape.173
  8.3 1.0 convert_reduce_fusion
  9.3 0.7 compare_select_fusion
  11.0 44.2 %all_to_all.20 = bf16[16,3,4,2048]{3,2,1,0:T(4,128)(2,1)S(1)} all-to-all(bf16[16,3,4,2048]{3,2,1,0:T(4,128)(2,1)S(1)} %reshape.174), channel_id=1, replica_groups=mesh['groups'=2,'seq'=16] {'seq'}, dimensions={0} | all-to-all | bytes 1572864 | tf_op jit(solution)/shard_map/all_to_all | solution.py:37
  56.1 7.6 %multiply_reduce_fusion.2 = (f32[768]{0:T(1024)S(1)}, f32[768,4096]{1,0:T(8,128)}) fusion(bf16[768,128]{1,0:T(8,128)(2,1)S(1)} %reshape.177, bf16[4096,512]{1,0:T(8,128)(2,1)} %param.10), kind=kOutput, calls=%fused_computation.9 | convolution fusion | flops 811597056 | bytes 13831168 | tf_op jit(solution)/shard_map/dot_general | solution.py:51
  63.8 6.8 %fusion.3 = f32[768]{0:T(1024)S(1)} fusion(f32[768,4096]{1,0:T(8,128)} %get-tuple-element.20, f32[768]{0:T(1024)S(1)} %get-tuple-element.19), kind=kLoop, calls=%fused_computation.14 | loop fusion | flops 9436416 | bytes 12589056 | tf_op jit(solution)/shard_map/reduce_sum | solution.py:56
  70.8 7.5 %multiply_reduce_fusion.1 = (f32[768]{0:T(1024)S(1)}, f32[768,4096]{1,0:T(8,128)}) fusion(bf16[768,128]{1,0:T(8,128)(2,1)S(1)} %reshape.178, bf16[4096,512]{1,0:T(8,128)(2,1)} %param.10), kind=kOutput, calls=%fused_computation.8 | convolution fusion | flops 811597056 | bytes 13831168 | tf_op jit(solution)/shard_map/dot_general | solution.py:51
  78.4 8.4 %fusion.5 = f32[768]{0:T(1024)S(1)} fusion(f32[768,4096]{1,0:T(8,128)} %get-tuple-element.18, f32[768]{0:T(1024)S(1)} %get-tuple-element.17), kind=kLoop, calls=%fused_computation.16 | loop fusion | flops 9436416 | bytes 12589056 | tf_op jit(solution)/shard_map/reduce_sum | solution.py:56
  87.0 7.6 %multiply_reduce_fusion = (f32[768]{0:T(1024)S(1)}, f32[768,4096]{1,0:T(8,128)}) fusion(bf16[768,128]{1,0:T(8,128)(2,1)S(1)} %reshape.179, bf16[4096,512]{1,0:T(8,128)(2,1)} %param.10), kind=kOutput, calls=%fused_computation.7 | convolution fusion | flops 811597056 | bytes 13831168 | tf_op jit(solution)/shard_map/dot_general | solution.py:51
  94.8 7.0 %fusion.7 = f32[768]{0:T(1024)S(1)} fusion(f32[768,4096]{1,0:T(8,128)} %get-tuple-element.16, f32[768]{0:T(1024)S(1)} %get-tuple-element.15), kind=kLoop, calls=%fused_computation.18 | loop fusion | flops 9436416 | bytes 12589056 | tf_op jit(solution)/shard_map/reduce_sum | solution.py:56
  102.0 7.5 %multiply_reduce_fusion.3 = (f32[768]{0:T(1024)S(1)}, f32[768,4096]{1,0:T(8,128)}) fusion(bf16[768,128]{1,0:T(8,128)(2,1)S(1)} %reshape.176, bf16[4096,512]{1,0:T(8,128)(2,1)} %param.10), kind=kOutput, calls=%fused_computation.10 | convolution fusion | flops 811597056 | bytes 13831168 | tf_op jit(solution)/shard_map/dot_general | solution.py:51
  109.6 6.8 %fusion.1 = f32[768]{0:T(1024)S(1)} fusion(f32[768,4096]{1,0:T(8,128)} %get-tuple-element.22, f32[768]{0:T(1024)S(1)} %get-tuple-element.21), kind=kLoop, calls=%fused_computation.12 | loop fusion | flops 9436416 | bytes 12589056 | tf_op jit(solution)/shard_map/reduce_sum | solution.py:56
  116.8 0.7 reshape.220
  117.5 5.7 %all-to-all-start.2 = ((f32[16,1,192]{2,1,0:T(1,128)}), f32[16,1,192]{2,1,0:T(1,128)S(1)}, u32[]{:S(2)}, u32[]{:S(2)}) async-start(f32[16,1,192]{2,1,0:T(1,128)} %reshape.220), calls=%async_computation.2 | async-start | bytes 32768 | tf_op jit(solution)/shard_map/all_to_all | solution.py:70
  123.3 7.2 %fusion.46 = bf16[768,128]{1,0:T(8,128)(2,1)S(1)} fusion(bf16[4096,512]{1,0:T(8,128)(2,1)} %param.11, f32[768,4096]{1,0:T(8,128)} %get-tuple-element.20, f32[768]{0:T(1024)S(1)} %get-tuple-element.19, f32[768]{0:T(1024)S(1)} %fusion.3), kind=kOutput, calls=%fused_computation.45 | convolution fusion | flops 814940160 | bytes 13834240 | tf_op jit(solution)/shard_map/dot_general | solution.py:58
  130.6 7.6 %fusion.56 = bf16[768,128]{1,0:T(8,128)(2,1)S(1)} fusion(bf16[4096,512]{1,0:T(8,128)(2,1)S(1)} %copy-done.3, f32[768,4096]{1,0:T(8,128)} %get-tuple-element.18, f32[768]{0:T(1024)S(1)} %get-tuple-element.17, f32[768]{0:T(1024)S(1)} %fusion.5), kind=kOutput, calls=%fused_computation.47 | convolution fusion | flops 814940160 | bytes 13836288 | tf_op jit(solution)/shard_map/dot_general | solution.py:58
  138.3 2.1 %fusion.66 = bf16[768,128]{1,0:T(8,128)(2,1)S(1)} fusion(bf16[4096,512]{1,0:T(8,128)(2,1)S(1)} %copy-done.3, f32[768,4096]{1,0:T(8,128)S(1)} %bitcast.53, f32[768]{0:T(1024)S(1)} %get-tuple-element.15, f32[768]{0:T(1024)S(1)} %fusion.7), kind=kOutput, calls=%fused_computation.49 | convolution fusion | flops 814940160 | bytes 13836288 | tf_op jit(solution)/shard_map/dot_general | solution.py:58
  140.4 0.7 slice-done.5
  141.1 2.1 %fusion.36 = bf16[768,128]{1,0:T(8,128)(2,1)S(1)} fusion(bf16[4096,512]{1,0:T(8,128)(2,1)S(1)} %copy-done.3, f32[768,4096]{1,0:T(8,128)S(1)} %bitcast.55, f32[768]{0:T(1024)S(1)} %get-tuple-element.21, f32[768]{0:T(1024)S(1)} %fusion.1), kind=kOutput, calls=%fused_computation.43 | convolution fusion | flops 814940160 | bytes 13836288 | tf_op jit(solution)/shard_map/dot_general | solution.py:58
  143.8 0.7 reshape.218
  144.5 6.2 %all-to-all-start.1 = ((f32[16,1,192]{2,1,0:T(1,128)}), f32[16,1,192]{2,1,0:T(1,128)S(1)}, u32[]{:S(2)}, u32[]{:S(2)}) async-start(f32[16,1,192]{2,1,0:T(1,128)} %reshape.218), calls=%async_computation.1 | async-start | bytes 32768 | tf_op jit(solution)/shard_map/all_to_all | solution.py:69
  150.7 1.4 pad_maximum_fusion
  152.1 5.1 %all-to-all-done.1 = f32[16,1,192]{2,1,0:T(1,128)S(1)} async-done(((f32[16,1,192]{2,1,0:T(1,128)}), f32[16,1,192]{2,1,0:T(1,128)S(1)}, u32[]{:S(2)}, u32[]{:S(2)}) %all-to-all-start.1) | async-done | bytes 12320 | tf_op jit(solution)/shard_map/all_to_all | solution.py:69
  157.2 3.8 %all-to-all-start.3 = ((bf16[16,3,4,2048]{3,2,1,0:T(4,128)(2,1)}), bf16[16,3,4,2048]{3,2,1,0:T(4,128)(2,1)S(1)}, u32[]{:S(2)}, u32[]{:S(2)}) async-start(bf16[16,3,4,2048]{3,2,1,0:T(4,128)(2,1)} %pad_maximum_fusion), calls=%async_computation.3 | async-start | bytes 1572864 | tf_op jit(solution)/shard_map/all_to_all | solution.py:68
  161.4 1.3 fusion.89
  164.5 0.7 reduce.1
  165.3 0.7 reduce.2
  166.1 0.6 gather_fusion.1
  167.4 12.1 %all-to-all-done.3 = bf16[16,3,4,2048]{3,2,1,0:T(4,128)(2,1)S(1)} async-done(((bf16[16,3,4,2048]{3,2,1,0:T(4,128)(2,1)}), bf16[16,3,4,2048]{3,2,1,0:T(4,128)(2,1)S(1)}, u32[]{:S(2)}, u32[]{:S(2)}) %all-to-all-start.3) | async-done | bytes 786464 | tf_op jit(solution)/shard_map/all_to_all | solution.py:68
  180.0 0.6 gather_fusion.2
  181.2 9.5 %convolution_convert_fusion.1 = bf16[32,4096]{1,0:T(8,128)(2,1)} fusion(bf16[2048,4096]{1,0:T(8,128)(2,1)} %all-gather.2.cloned.1.call-done, f32[4,8,16,128]{3,2,1,0:T(8,128)S(1)} %bitcast.57, f32[4,8,16,128]{3,2,1,0:T(8,128)S(1)} %bitcast.59, f32[32,2048]{1,0:T(8,128)S(1)} %reshape.182, f32[4,8,16,128]{3,2,1,0:T(8,128)S(1)} %bitcast.58), kind=kOutput, calls=%fused_computation.24 | convolution fusion | flops 537264128 | bytes 18087936 | tf_op jit(solution)/shard_map/dot_general | solution.py:107
  (75 shorter events, 7.9 us)
Async XLA Ops:
  6.5 174.4 %all-gather.2.cloned.1.call-start = ((), (), s32[]{:S(2)}) async-start(), calls=%async_computation.4 | async-start | bytes 17825792 | tf_op jit(solution)/shard_map/all_gather | solution.py:109
  117.5 27.0 %all-to-all-start.2 = ((f32[16,1,192]{2,1,0:T(1,128)}), f32[16,1,192]{2,1,0:T(1,128)S(1)}, u32[]{:S(2)}, u32[]{:S(2)}) async-start(f32[16,1,192]{2,1,0:T(1,128)} %reshape.220), calls=%async_computation.2 | async-start | bytes 32768 | tf_op jit(solution)/shard_map/all_to_all | solution.py:70
  123.3 7.3 %copy-start.3 = (bf16[4096,512]{1,0:T(8,128)(2,1)S(1)}, bf16[4096,512]{1,0:T(8,128)(2,1)}, u32[]{:S(2)}) copy-start(bf16[4096,512]{1,0:T(8,128)(2,1)} %param.11) | copy-start | bytes 12582916
  123.3 14.9 %slice-start = ((s8[12582912]{0:T(1024)(128)(4,1)}), s8[4194304]{0:T(1024)(128)(4,1)S(1)}, s32[]{:S(2)}) async-start(s8[12582912]{0:T(1024)(128)(4,1)} %bitcast.52), calls=%async_computation.5 | async-start | bytes 8388608
  123.3 14.9 %slice-start.1 = ((s8[12582912]{0:T(1024)(128)(4,1)}), s8[4194304]{0:T(1024)(128)(4,1)S(1)}, s32[]{:S(2)}) async-start(s8[12582912]{0:T(1024)(128)(4,1)} %bitcast.52), calls=%async_computation.6 | async-start | bytes 8388608
  130.6 7.7 %slice-start.2 = ((s8[12582912]{0:T(1024)(128)(4,1)}), s8[4194304]{0:T(1024)(128)(4,1)S(1)}, s32[]{:S(2)}) async-start(s8[12582912]{0:T(1024)(128)(4,1)} %bitcast.52), calls=%async_computation.7 | async-start | bytes 8388608
  130.6 9.8 %slice-start.3 = ((s8[12582912]{0:T(1024)(128)(4,1)}), s8[4194304]{0:T(1024)(128)(4,1)S(1)}, s32[]{:S(2)}) async-start(s8[12582912]{0:T(1024)(128)(4,1)} %bitcast.54), calls=%async_computation.8 | async-start | bytes 8388608
  130.6 9.8 %slice-start.4 = ((s8[12582912]{0:T(1024)(128)(4,1)}), s8[4194304]{0:T(1024)(128)(4,1)S(1)}, s32[]{:S(2)}) async-start(s8[12582912]{0:T(1024)(128)(4,1)} %bitcast.54), calls=%async_computation.9 | async-start | bytes 8388608
  138.3 2.9 %slice-start.5 = ((s8[12582912]{0:T(1024)(128)(4,1)}), s8[4194304]{0:T(1024)(128)(4,1)S(1)}, s32[]{:S(2)}) async-start(s8[12582912]{0:T(1024)(128)(4,1)} %bitcast.54), calls=%async_computation.10 | async-start | bytes 8388608
  141.1 19.9 %copy-start = (bf16[32,2048]{1,0:T(8,128)(2,1)S(1)}, bf16[32,2048]{1,0:T(8,128)(2,1)}, u32[]{:S(2)}) copy-start(bf16[32,2048]{1,0:T(8,128)(2,1)} %param.7) | copy-start | bytes 393220
  141.1 20.2 %copy-start.1 = (bf16[32,512]{1,0:T(8,128)(2,1)S(1)}, bf16[32,512]{1,0:T(8,128)(2,1)}, u32[]{:S(2)}) copy-start(bf16[32,512]{1,0:T(8,128)(2,1)} %param.8) | copy-start | bytes 98308
  141.1 20.2 %copy-start.2 = (bf16[32,512]{1,0:T(8,128)(2,1)S(1)}, bf16[32,512]{1,0:T(8,128)(2,1)}, u32[]{:S(2)}) copy-start(bf16[32,512]{1,0:T(8,128)(2,1)} %param.9) | copy-start | bytes 98308
  144.5 12.7 %all-to-all-start.1 = ((f32[16,1,192]{2,1,0:T(1,128)}), f32[16,1,192]{2,1,0:T(1,128)S(1)}, u32[]{:S(2)}, u32[]{:S(2)}) async-start(f32[16,1,192]{2,1,0:T(1,128)} %reshape.218), calls=%async_computation.1 | async-start | bytes 32768 | tf_op jit(solution)/shard_map/all_to_all | solution.py:69
  157.2 22.3 %all-to-all-start.3 = ((bf16[16,3,4,2048]{3,2,1,0:T(4,128)(2,1)}), bf16[16,3,4,2048]{3,2,1,0:T(4,128)(2,1)S(1)}, u32[]{:S(2)}, u32[]{:S(2)}) async-start(bf16[16,3,4,2048]{3,2,1,0:T(4,128)(2,1)} %pad_maximum_fusion), calls=%async_computation.3 | async-start | bytes 1572864 | tf_op jit(solution)/shard_map/all_to_all | solution.py:68
Sparse Core Ops, SparseCore 0:
  9.5 147.8 all-gather.1
where the time goes:
time: 198 us; the launch traced here: 197 us
  matrix products  60.7 us (31%)
  blocking collectives  44.2 us (22%)
  other arithmetic  34.6 us (17%)
  waiting for transfers between devices  17.9 us (9%)
  starting transfers between devices  15.7 us (8%)
  between operations  13.9 us (7%)
  local copies, waits for them, and re-layouts  10.4 us (5%)
    all_to_all x1, blocking collectives, shards(): lax.all_to_all(outgoing, 'seq', split_axis=0, concat_axis=0, tiled=True)  44.2 us
    dot_general x4, matrix products, shards(): lax.dot_general(asked, cached_keys, (((1,), (1,)), ((), ())), preferred_e...  30.2 us
    reduce_sum x4, other arithmetic, shards(): summed = jnp.sum(weights, axis=1, keepdims=True)  29 us
    dot_general x4, matrix products, shards(): jnp.dot(weights.astype(jnp.bfloat16), cached_values, preferred_element_ty...  19 us
    all_to_all x1, waiting for transfers between devices, shards(): lax.all_to_all(partial_out, 'seq', split_axis=0, concat_axis=0, tiled=True)  12.1 us
    dot_general x1, matrix products, shards(): jnp.dot(attended, lax.all_gather(out_weight, 'seq', axis=1, tiled=True),...  9.49 us
    all_to_all x1, starting transfers between devices, shards(): lax.all_to_all(maxima_all, 'seq', split_axis=0, concat_axis=0, tiled=True)  6.17 us
    all_to_all x1, starting transfers between devices, shards(): lax.all_to_all(totals_all, 'seq', split_axis=0, concat_axis=0, tiled=True)  5.73 us
  transfers between devices with their start and end apart: 4, of which 2 were waited for; matrix products, arithmetic and copies ran while one was open for 48% of the time, Pallas kernels for 0%

commit v1 on v0

v1 whole, which is shorter than its diff:
```python
import functools
import math

import jax
import jax.numpy as jnp
from jax import lax
from jax.experimental import pallas as pl
from jax.experimental.pallas import tpu as pltpu
from jax.sharding import PartitionSpec as P

HQ = 16
KVH = 4
HD = 128
GROUP = HQ // KVH
LANES = 128
PARTS = 4
STAT_ROWS = KVH * PARTS
SCALE2 = math.log2(math.e) / math.sqrt(HD)
CHUNK = 512


def iota(shape, axis):
    return lax.broadcasted_iota(jnp.int32, shape, axis)


def fill_slots(page_list, base, members, capacity, source, count):
    tiles, width = page_list.shape

    def clear(i, carry):
        source[i] = -1
        return carry

    lax.fori_loop(0, members * capacity, clear, 0)

    def clear_count(i, carry):
        count[i] = 0
        return carry

    lax.fori_loop(0, members, clear_count, 0)
    for tile in range(tiles):
        for item in range(width):
            page = page_list[tile, item] - base

            @pl.when((page >= 0) & (page < members))
            def _():
                slot = count[page]
                source[page * capacity + slot] = tile
                count[page] = slot + 1


def pack_kernel(members, capacity, page_list, queries, packed, source, count):
    tiles = page_list.shape[0]
    rows = queries.shape[0]
    tile_rows = rows // tiles
    slot_rows = capacity * tile_rows
    block = GROUP * slot_rows
    fill_slots(page_list, 0, members, capacity, source, count)
    row = iota((block, GROUP * rows), 0)
    col = iota((block, GROUP * rows), 1)
    fixed = (row // slot_rows == col // rows) & (row % tile_rows == col % tile_rows)
    slot = row % slot_rows // tile_rows
    tile = col % rows // tile_rows
    pieces = []
    for page in range(members):
        wanted = jnp.full((block, GROUP * rows), -1, jnp.int32)
        for k in range(capacity):
            wanted = jnp.where(slot == k, source[page * capacity + k], wanted)
        pieces.append((fixed & (tile == wanted)).astype(jnp.bfloat16))
    chosen = jnp.concatenate(pieces, axis=0)
    for group in range(KVH):
        stacked = jnp.concatenate(
            [
                queries[:, (group * GROUP + j) * HD : (group * GROUP + j + 1) * HD]
                for j in range(GROUP)
            ],
            axis=0,
        )
        sent = jnp.dot(chosen, stacked, preferred_element_type=jnp.float32).astype(jnp.bfloat16)
        packed[:, group * block : (group + 1) * block, :] = sent.reshape(members, block, HD)


def attend_kernel(queries, keys, values, partial, stats):
    members, block, _ = queries.shape
    rows = members * block
    group = pl.program_id(0)
    asked = queries[...].reshape(rows, HD)
    page = keys.shape[0]
    chunk = min(CHUNK, page)
    ones = jnp.ones((chunk, HD), jnp.bfloat16)
    highest = None
    total = None
    for start in range(0, page, chunk):
        scores = lax.dot_general(
            asked,
            keys[start : start + chunk, :],
            (((1,), (1,)), ((), ())),
            preferred_element_type=jnp.float32,
        )
        here = jnp.max(scores, axis=1, keepdims=True)
        new = here if highest is None else jnp.maximum(highest, here)
        weights = jnp.exp2((scores - new) * SCALE2).astype(jnp.bfloat16)
        extended = jnp.concatenate([values[start : start + chunk, :], ones], axis=1)
        mixed = jnp.dot(weights, extended, preferred_element_type=jnp.float32)
        if total is None:
            total = mixed
        else:
            total = total * jnp.exp2((highest - new) * SCALE2) + mixed
        highest = new
    summed = total[:, HD:]
    result = (total[:, :HD] / summed).astype(jnp.bfloat16).reshape(members, block, HD)
    partial[:, pl.ds(pl.multiple_of(group * block, block), block), :] = result
    peak = jnp.broadcast_to(highest * SCALE2, (rows, LANES))
    peak_high = peak.astype(jnp.bfloat16).astype(jnp.float32)
    peak_low = (peak - peak_high).astype(jnp.bfloat16).astype(jnp.float32)
    moved = summed * jnp.exp2(peak - peak_high - peak_low)
    moved_high = moved.astype(jnp.bfloat16).astype(jnp.float32)
    moved_low = moved - moved_high
    part = iota((rows, LANES), 1) % PARTS
    mixed = jnp.where(
        part == 0,
        peak_high,
        jnp.where(part == 1, peak_low, jnp.where(part == 2, moved_high, moved_low)),
    )
    turned = mixed.T[:STAT_ROWS, :]
    mine = iota((STAT_ROWS, rows), 0) // PARTS == group

    @pl.when(group == 0)
    def _():
        stats[...] = turned

    @pl.when(group > 0)
    def _():
        stats[...] = jnp.where(mine, turned, stats[...])

    @pl.when(group == KVH - 1)
    def _():
        padded = jnp.concatenate(
            [stats[...], jnp.zeros((STAT_ROWS, LANES), jnp.float32)], axis=1
        )
        for member in range(members):
            partial[member, KVH * block :, :] = padded[
                :, member * block : member * block + LANES
            ].astype(jnp.bfloat16)


def merge_kernel(
    members, capacity, page_list, queries, new_keys, new_values, returned, attended, source, count
):
    tiles = page_list.shape[0]
    rows = queries.shape[0]
    tile_rows = rows // tiles
    slot_rows = capacity * tile_rows
    block = GROUP * slot_rows
    width = members * block
    tall = GROUP * rows
    fill_slots(page_list, 0, members, capacity, source, count)
    lane = iota((8, width), 1)
    lane_slot = lane // block * capacity + lane % slot_rows // tile_rows
    wanted = jnp.full((8, width), -1, jnp.int32)
    for slot in range(members * capacity):
        wanted = jnp.where(lane_slot == slot, source[slot], wanted)
    lane_code = (wanted * tile_rows + lane % tile_rows) + (lane % block // slot_rows) * rows
    lane_code = jnp.where(wanted < 0, -1, lane_code)[:1, :]
    chosen = iota((tall, width), 0) == lane_code
    bias = jnp.where(chosen, 0.0, -jnp.inf)
    stat_pieces = [
        returned[member, KVH * block :, :].astype(jnp.float32)[:, :block]
        for member in range(members)
    ]
    stats = jnp.concatenate(stat_pieces, axis=1)
    own_row = iota((tall, rows), 0) % rows
    own_col = iota((tall, rows), 1)
    causal = (own_row // tile_rows == own_col // tile_rows) & (own_col <= own_row)
    for group in range(KVH):
        stacked = jnp.concatenate(
            [
                queries[:, (group * GROUP + j) * HD : (group * GROUP + j + 1) * HD]
                for j in range(GROUP)
            ],
            axis=0,
        )
        fresh_keys = new_keys[:, group * HD : (group + 1) * HD]
        fresh_values = new_values[:, group * HD : (group + 1) * HD]
        scores = lax.dot_general(
            stacked, fresh_keys, (((1,), (1,)), ((), ())), preferred_element_type=jnp.float32
        )
        scores = jnp.where(causal, scores, -jnp.inf)
        own_max = jnp.max(scores, axis=1, keepdims=True)
        own_weights = jnp.exp2((scores - own_max) * SCALE2)
        own_total = jnp.sum(own_weights, axis=1, keepdims=True)
        own_sum = jnp.dot(
            own_weights.astype(jnp.bfloat16), fresh_values, preferred_element_type=jnp.float32
        )
        base = group * PARTS
        peak = bias + (stats[base : base + 1, :] + stats[base + 1 : base + 2, :])
        moved = stats[base + 2 : base + 3, :] + stats[base + 3 : base + 4, :]
        own_peak = own_max * SCALE2
        top = jnp.maximum(jnp.max(peak, axis=1, keepdims=True), own_peak)
        factor = jnp.exp2(peak - top) * moved
        own_factor = jnp.exp2(own_peak - top)
        denom = jnp.sum(factor, axis=1, keepdims=True) + own_factor * own_total
        factor = factor / denom
        high = factor.astype(jnp.bfloat16)
        low = (factor - high.astype(jnp.float32)).astype(jnp.bfloat16)
        outs = returned[:, group * block : (group + 1) * block, :].reshape(width, HD)
        numer = (
            jnp.dot(high, outs, preferred_element_type=jnp.float32)
            + jnp.dot(low, outs, preferred_element_type=jnp.float32)
            + own_factor / denom * own_sum
        )
        numer = numer.astype(jnp.bfloat16)
        for j in range(GROUP):
            head = group * GROUP + j
            attended[:, head * HD : (head + 1) * HD] = numer[j * rows : (j + 1) * rows, :]


def project_kernel(count, own, other, place, *refs):
    weights = refs[:count]
    own_out, other_out = refs[count : count + 2]
    held, sems = refs[count + 2 :]
    width = weights[0].shape[1]
    copies = [pltpu.make_async_copy(weights[k], held.at[k], sems.at[k]) for k in range(count)]
    for copy in copies:
        copy.start()
    rows = own.shape[0]
    left = jnp.concatenate([own[...], other[...]], axis=0)
    for k in range(count):
        copies[k].wait()
        made = jnp.dot(left, held[k], preferred_element_type=jnp.float32).astype(jnp.bfloat16)
        at = pl.ds(pl.multiple_of((place[0] ^ k) * width, width), width)
        own_out[:, at] = made[:rows, :]
        other_out[:, at] = made[rows:, :]


VMEM = pl.BlockSpec(memory_space=pltpu.VMEM)
SMEM = pl.BlockSpec(memory_space=pltpu.SMEM)
ANY = pl.BlockSpec(memory_space=pl.ANY)


def slot_scratch(members, capacity):
    return [
        pltpu.SMEM((members * capacity,), jnp.int32),
        pltpu.SMEM((members,), jnp.int32),
    ]


def shards(queries, new_keys, new_values, keys, values, page_list, out_weight):
    members = lax.axis_size("seq")
    me = lax.axis_index("seq")
    tile_count, list_width = page_list.shape
    row_total, features = queries.shape
    tile_rows = row_total // tile_count
    capacity = max(1, 2 * tile_count * list_width // members)
    block = GROUP * capacity * tile_rows
    half = members // 2
    mirror = [(i, (i + half) % members) for i in range(members)]

    packed = pl.pallas_call(
        functools.partial(pack_kernel, members, capacity),
        out_shape=jax.ShapeDtypeStruct((members, KVH * block, HD), jnp.bfloat16),
        in_specs=[SMEM, VMEM],
        out_specs=VMEM,
        scratch_shapes=slot_scratch(members, capacity),
        name="pack",
    )(page_list, queries)
    incoming = lax.all_to_all(packed, "seq", split_axis=0, concat_axis=0, tiled=True)

    page = keys.shape[0]
    rows = members * block
    partial = pl.pallas_call(
        attend_kernel,
        out_shape=jax.ShapeDtypeStruct((members, KVH * block + STAT_ROWS, HD), jnp.bfloat16),
        grid=(KVH,),
        in_specs=[
            pl.BlockSpec((members, block, HD), lambda g: (0, g, 0)),
            pl.BlockSpec((page, HD), lambda g: (0, g)),
            pl.BlockSpec((page, HD), lambda g: (0, g)),
        ],
        out_specs=pl.BlockSpec((members, KVH * block + STAT_ROWS, HD), lambda g: (0, 0, 0)),
        scratch_shapes=[pltpu.VMEM((STAT_ROWS, rows), jnp.float32)],
        compiler_params=pltpu.CompilerParams(
            dimension_semantics=("arbitrary",), vmem_limit_bytes=56 << 20
        ),
        cost_estimate=pl.CostEstimate(
            flops=4 * rows * KVH * page * HD,
            bytes_accessed=4 * page * KVH * HD,
            transcendentals=rows * KVH * page,
        ),
        name="attend",
    )(incoming, keys, values)
    returned = lax.all_to_all(partial, "seq", split_axis=0, concat_axis=0, tiled=True)

    attended = pl.pallas_call(
        functools.partial(merge_kernel, members, capacity),
        out_shape=jax.ShapeDtypeStruct((row_total, features), jnp.bfloat16),
        in_specs=[SMEM] + [VMEM] * 4,
        out_specs=VMEM,
        scratch_shapes=slot_scratch(members, capacity),
        name="merge",
    )(page_list, queries, new_keys, new_values, returned)

    width = out_weight.shape[1]
    if width % LANES or members & (members - 1):
        return jnp.dot(
            attended,
            lax.all_gather(out_weight, "seq", axis=1, tiled=True),
            preferred_element_type=jnp.float32,
        ).astype(jnp.bfloat16)

    def exchanged(array, step):
        return lax.ppermute(array, "seq", [(i, i ^ step) for i in range(members)])

    same_core = [out_weight] + [exchanged(out_weight, step) for step in range(2, half, 2)]
    gathered = []
    for array in same_core:
        gathered += [array, exchanged(array, 1)]
    other = lax.ppermute(attended, "seq", mirror)
    own_out, other_out = pl.pallas_call(
        functools.partial(project_kernel, half),
        out_shape=[jax.ShapeDtypeStruct((row_total, half * width), jnp.bfloat16)] * 2,
        in_specs=[VMEM, VMEM, SMEM] + [ANY] * half,
        out_specs=[VMEM, VMEM],
        scratch_shapes=[
            pltpu.VMEM((half, features, width), jnp.bfloat16),
            pltpu.SemaphoreType.DMA((half,)),
        ],
        name="project",
    )(attended, other, (me % half).reshape(1), *gathered)
    received = lax.ppermute(other_out, "seq", mirror)
    first = me < half
    return jnp.concatenate(
        [jnp.where(first, own_out, received), jnp.where(first, received, own_out)], axis=1
    )


def solution(mesh):
    return jax.shard_map(
        shards,
        mesh=mesh,
        in_specs=(
            P(("groups", "seq"), None),
            P(("groups", "seq"), None),
            P(("groups", "seq"), None),
            P(("groups", "seq"), None),
            P(("groups", "seq"), None),
            P(("groups", "seq"), None),
            P(None, "seq"),
        ),
        out_specs=P(("groups", "seq"), None),
        check_vma=False,
    )
```

time: 198 us -> 119 us (0.60)
  matrix products: 60.7 us -> 0 us
  waiting for transfers between devices: 17.9 us -> 63.4 us
  blocking collectives: 44.2 us -> 0 us
  other arithmetic: 34.6 us -> 1.65 us
  Pallas kernels: 0 us -> 32.7 us
  between operations: 13.9 us -> 0.1 us
  local copies, waits for them, and re-layouts: 10.4 us -> 3.84 us
    dot_general x12 -> x0, matrix products: 60.7 us -> none  [the longest x4 30.2 us: shards(): lax.dot_general(asked, cached_keys, (((1,), (1,)), ((), ())), preferred_e...]
    all_to_all x1 -> x0, blocking collectives: 44.2 us -> none  [shards(): lax.all_to_all(outgoing, 'seq', split_axis=0, concat_axis=0, tiled=True)]
    ppermute x0 -> x9, waiting for transfers between devices: none -> 36.3 us  [the longest x7 22.5 us: exchanged(): return lax.ppermute(array, 'seq', [(i, i ^ step) for i in range(members)])]
    pallas_call x0 -> x4, Pallas kernels: none -> 32.7 us  [the longest x1 19.4 us: shards(): pl.pallas_call(attend_kernel, out_shape=jax.ShapeDtypeStruct((members, KV...]
    reduce_sum x8 -> x0, other arithmetic: 30.6 us -> none  [the longest x4 29 us: shards(): summed = jnp.sum(weights, axis=1, keepdims=True)]
    all_to_all x3 -> x2, waiting for transfers between devices: 17.2 us -> 27.1 us  [the longest x1 15.6 us: shards(): lax.all_to_all(packed, 'seq', split_axis=0, concat_axis=0, tiled=True)]
    ppermute x0 -> x9, starting transfers between devices: none -> 4.61 us  [the longest x7 4.54 us: exchanged(): return lax.ppermute(array, 'seq', [(i, i ^ step) for i in range(members)])]
    all_to_all x3 -> x2, starting transfers between devices: 15.7 us -> 12.6 us  [the longest x1 7.41 us: shards(): lax.all_to_all(packed, 'seq', split_axis=0, concat_axis=0, tiled=True)]
  transfers between devices with their start and end apart: 4 -> 11, of which waited for: 2 -> 5; matrix products, arithmetic and copies ran while one was open for 48% -> 0% of each run, Pallas kernels for 0% -> 20%
where the time goes in v1:
time: 119 us
  waiting for transfers between devices  63.4 us (53%)
  Pallas kernels  32.7 us (27%)
  starting transfers between devices  17.2 us (14%)
  local copies, waits for them, and re-layouts  3.84 us (3%)
  other arithmetic  1.65 us (1%)
    ppermute x7, waiting for transfers between devices, exchanged(): return lax.ppermute(array, 'seq', [(i, i ^ step) for i in range(members)])  22.5 us
    pallas_call x1, Pallas kernels, shards(): pl.pallas_call(attend_kernel, out_shape=jax.ShapeDtypeStruct((members, KV...  19.4 us
    all_to_all x1, waiting for transfers between devices, shards(): lax.all_to_all(packed, 'seq', split_axis=0, concat_axis=0, tiled=True)  15.6 us
    all_to_all x1, waiting for transfers between devices, shards(): lax.all_to_all(partial, 'seq', split_axis=0, concat_axis=0, tiled=True)  11.5 us
    all_to_all x1, starting transfers between devices, shards(): lax.all_to_all(packed, 'seq', split_axis=0, concat_axis=0, tiled=True)  7.41 us
    ppermute x1, waiting for transfers between devices, shards(): other = lax.ppermute(attended, 'seq', mirror)  6.95 us
    ppermute x1, waiting for transfers between devices, shards(): received = lax.ppermute(other_out, 'seq', mirror)  6.86 us
    pallas_call x1, Pallas kernels, shards(): pl.pallas_call(functools.partial(project_kernel, half), out_shape=[jax.Sh...  6.35 us
  transfers between devices with their start and end apart: 11, of which 5 were waited for; matrix products, arithmetic and copies ran while one was open for 0% of the time, Pallas kernels for 20%

profile of v1, /device:TPU:0, one launch (start us, length us, event | category | flops | bytes accessed | tf_op | source)
XLA Modules:
  0.0 118.8 jit_solution(11829662225444882764)
XLA Ops:
  0.0 1.3 %copy.9.page_list = s32[8,3]{1,0:T(8,128)} copy(s32[8,3]{0,1:T(4,128)} %param.12) | data formatting | bytes 192 | tf_op args[5]
  1.3 2.7 %pack.1 = bf16[16,192,128]{2,1,0:T(8,128)(2,1)} custom-call(s32[8,3]{1,0:T(8,128)} %copy.9.page_list, bf16[32,2048]{1,0:T(8,128)(2,1)} %queries.3), custom_call_target="tpu_custom_call" | custom-call | tf_op jit(solution)/shard_map/pack/pallas_call | solution.py:258
  4.0 7.4 %all-to-all-start = ((bf16[16,192,128]{2,1,0:T(8,128)(2,1)}), bf16[16,192,128]{2,1,0:T(8,128)(2,1)S(1)}, u32[]{:S(2)}, u32[]{:S(2)}) async-start(bf16[16,192,128]{2,1,0:T(8,128)(2,1)} %pack.1), calls=%async_computation | async-start | bytes 1572864 | tf_op jit(solution)/shard_map/all_to_all | solution.py:266
  11.4 0.0 copy-start.1
  11.5 2.0 %collective-permute-start.4 = (bf16[2048,256]{1,0:T(8,128)(2,1)}, bf16[2048,256]{1,0:T(8,128)(2,1)S(1)}, u32[]{:S(2)}, u32[]{:S(2)}) collective-permute-start(bf16[2048,256]{1,0:T(8,128)(2,1)} %refs_0_.1), channel_id=1, source_target_pairs={{0,4},{1,5},{2,6},{3,7},{4,0},{5,1},{6,2},{7,3},{8,12},{9,13},{10,... | collective-permute-start | bytes 3145736 | tf_op jit(solution)/shard_map/ppermute | solution.py:311
  13.4 1.5 %collective-permute-start.2 = (bf16[2048,256]{1,0:T(8,128)(2,1)}, bf16[2048,256]{1,0:T(8,128)(2,1)}, u32[]{:S(2)}, u32[]{:S(2)}) collective-permute-start(bf16[2048,256]{1,0:T(8,128)(2,1)} %refs_0_.1), channel_id=1, source_target_pairs={{0,2},{1,3},{2,0},{3,1},{4,6},{5,7},{6,4},{7,5},{8,10},{9,11},{10,... | collective-permute-start | bytes 3145736 | tf_op jit(solution)/shard_map/ppermute | solution.py:311
  14.9 0.1 collective-permute-start.6
  15.0 15.6 %all-to-all-done.queries = bf16[16,192,128]{2,1,0:T(8,128)(2,1)S(1)} async-done(((bf16[16,192,128]{2,1,0:T(8,128)(2,1)}), bf16[16,192,128]{2,1,0:T(8,128)(2,1)S(1)}, u32[]{:S(2)}, u32[]{:S(2)}) %all-to-all-start) | async-done | bytes 786464 | tf_op jit(solution)/shard_map/all_to_all | solution.py:266
  30.6 0.9 copy-done.3
  31.5 19.4 %attend.1 = bf16[16,208,128]{2,1,0:T(8,128)(2,1)} custom-call(bf16[16,192,128]{2,1,0:T(8,128)(2,1)} %copy-done.3, bf16[4096,512]{1,0:T(8,128)(2,1)} %keys.1, bf16[4096,512]{1,0:T(8,128)(2,1)} %values.1), custom_call_target="tpu_custom_call" | custom-call | flops 6442450944 | bytes 8388608 | tf_op jit(solution)/shard_map/attend/pallas_call | solution.py:270
  50.9 5.1 %all-to-all-start.1 = ((bf16[16,208,128]{2,1,0:T(8,128)(2,1)}), bf16[16,208,128]{2,1,0:T(8,128)(2,1)S(1)}, u32[]{:S(2)}, u32[]{:S(2)}) async-start(bf16[16,208,128]{2,1,0:T(8,128)(2,1)} %attend.1), calls=%async_computation.1 | async-start | bytes 1703936 | tf_op jit(solution)/shard_map/all_to_all | solution.py:291
  56.0 0.5 collective-permute-start.1
  56.5 0.0 collective-permute-done.4.refs_4_
  56.5 0.1 collective-permute-start.5
  56.6 0.0 collective-permute-done.2.refs_2_
  56.6 0.4 collective-permute-start.3
  57.0 22.4 %collective-permute-done.6.refs_6_ = bf16[2048,256]{1,0:T(8,128)(2,1)} collective-permute-done((bf16[2048,256]{1,0:T(8,128)(2,1)}, bf16[2048,256]{1,0:T(8,128)(2,1)}, u32[]{:S(2)}, u32[]{:S(2)}) %collective-permute-start.6) | collective-permute-done | bytes 1048608 | tf_op jit(solution)/shard_map/ppermute | solution.py:311
  79.4 0.0 collective-permute-start.7
  79.4 11.5 %all-to-all-done.1.returned = bf16[16,208,128]{2,1,0:T(8,128)(2,1)S(1)} async-done(((bf16[16,208,128]{2,1,0:T(8,128)(2,1)}), bf16[16,208,128]{2,1,0:T(8,128)(2,1)S(1)}, u32[]{:S(2)}, u32[]{:S(2)}) %all-to-all-start.1) | async-done | bytes 852000 | tf_op jit(solution)/shard_map/all_to_all | solution.py:291
  91.0 0.9 copy-done
  91.9 4.3 %merge.1.own = bf16[32,2048]{1,0:T(8,128)(2,1)} custom-call(s32[8,3]{1,0:T(8,128)} %copy.9.page_list, bf16[32,2048]{1,0:T(8,128)(2,1)} %queries.3, bf16[32,512]{1,0:T(8,128)(2,1)} %new_keys.1, bf16[32,512]{1,0:T(8,128)(2,1)} %new_values.1, bf16[16,208,128]{2,1,0:T(8,128)(2,1)} %copy-done), custom_call_target="tpu_custom_call" | custom-call | tf_op jit(solution)/shard_map/merge/pallas_call | solution.py:293
  96.3 0.0 collective-permute-start
  96.3 0.0 collective-permute-done.1.refs_1_
  96.3 0.0 collective-permute-done.5.refs_5_
  96.3 0.0 collective-permute-done.3.refs_3_
  96.3 6.9 %collective-permute-done.other = bf16[32,2048]{1,0:T(8,128)(2,1)S(1)} collective-permute-done((bf16[32,2048]{1,0:T(8,128)(2,1)}, bf16[32,2048]{1,0:T(8,128)(2,1)S(1)}, u32[]{:S(2)}, u32[]{:S(2)}) %collective-permute-start) | collective-permute-done | bytes 131104 | tf_op jit(solution)/shard_map/ppermute | solution.py:317
  103.2 0.6 copy-done.4
  103.9 6.3 %project.1 = (bf16[32,2048]{1,0:T(8,128)(2,1)}, bf16[32,2048]{1,0:T(8,128)(2,1)}) custom-call(bf16[32,2048]{1,0:T(8,128)(2,1)} %merge.1.own, bf16[32,2048]{1,0:T(8,128)(2,1)} %copy-done.4, s32[1]{0:T(128)} %bitcast.place, bf16[2048,256]{1,0:T(8,128)(2,1)} %refs_0_.1, bf16[2048,256]{1,0:T(8,128)(2,1)} %collective-permute-done.1.refs_1_, ...), custom_call_target="tpu_custom_call" | custom-call | tf_op jit(solution)/shard_map/project/pallas_call | solution.py:318
  110.2 0.1 collective-permute-start.8
  110.3 6.9 %collective-permute-done.8 = bf16[32,2048]{1,0:T(8,128)(2,1)S(1)} collective-permute-done((bf16[32,2048]{1,0:T(8,128)(2,1)}, bf16[32,2048]{1,0:T(8,128)(2,1)S(1)}, u32[]{:S(2)}, u32[]{:S(2)}) %collective-permute-start.8) | collective-permute-done | bytes 131104 | tf_op jit(solution)/shard_map/ppermute | solution.py:329
  117.2 0.9 broadcast_select_fusion.1
  118.1 0.7 pad_maximum_fusion
  (7 shorter events, 0.0 us)
Async XLA Ops:
  4.0 26.6 %all-to-all-start = ((bf16[16,192,128]{2,1,0:T(8,128)(2,1)}), bf16[16,192,128]{2,1,0:T(8,128)(2,1)S(1)}, u32[]{:S(2)}, u32[]{:S(2)}) async-start(bf16[16,192,128]{2,1,0:T(8,128)(2,1)} %pack.1), calls=%async_computation | async-start | bytes 1572864 | tf_op jit(solution)/shard_map/all_to_all | solution.py:266
  11.4 44.6 %copy-start.1 = (bf16[2048,256]{1,0:T(8,128)(2,1)S(1)}, bf16[2048,256]{1,0:T(8,128)(2,1)}, u32[]{:S(2)}) copy-start(bf16[2048,256]{1,0:T(8,128)(2,1)} %refs_0_.1) | copy-start | bytes 3145732
  11.5 45.0 %collective-permute-start.4 = (bf16[2048,256]{1,0:T(8,128)(2,1)}, bf16[2048,256]{1,0:T(8,128)(2,1)S(1)}, u32[]{:S(2)}, u32[]{:S(2)}) collective-permute-start(bf16[2048,256]{1,0:T(8,128)(2,1)} %refs_0_.1), channel_id=1, source_target_pairs={{0,4},{1,5},{2,6},{3,7},{4,0},{5,1},{6,2},{7,3},{8,12},{9,13},{10,... | collective-permute-start | bytes 3145736 | tf_op jit(solution)/shard_map/ppermute | solution.py:311
  13.4 43.2 %collective-permute-start.2 = (bf16[2048,256]{1,0:T(8,128)(2,1)}, bf16[2048,256]{1,0:T(8,128)(2,1)}, u32[]{:S(2)}, u32[]{:S(2)}) collective-permute-start(bf16[2048,256]{1,0:T(8,128)(2,1)} %refs_0_.1), channel_id=1, source_target_pairs={{0,2},{1,3},{2,0},{3,1},{4,6},{5,7},{6,4},{7,5},{8,10},{9,11},{10,... | collective-permute-start | bytes 3145736 | tf_op jit(solution)/shard_map/ppermute | solution.py:311
  14.9 64.5 %collective-permute-start.6 = (bf16[2048,256]{1,0:T(8,128)(2,1)}, bf16[2048,256]{1,0:T(8,128)(2,1)}, u32[]{:S(2)}, u32[]{:S(2)}) collective-permute-start(bf16[2048,256]{1,0:T(8,128)(2,1)} %refs_0_.1), channel_id=1, source_target_pairs={{0,6},{1,7},{2,4},{3,5},{4,2},{5,3},{6,0},{7,1},{8,14},{9,15},{10,... | collective-permute-start | bytes 3145736 | tf_op jit(solution)/shard_map/ppermute | solution.py:311
  30.6 0.9 copy-start.3
  50.9 40.1 %all-to-all-start.1 = ((bf16[16,208,128]{2,1,0:T(8,128)(2,1)}), bf16[16,208,128]{2,1,0:T(8,128)(2,1)S(1)}, u32[]{:S(2)}, u32[]{:S(2)}) async-start(bf16[16,208,128]{2,1,0:T(8,128)(2,1)} %attend.1), calls=%async_computation.1 | async-start | bytes 1703936 | tf_op jit(solution)/shard_map/all_to_all | solution.py:291
  56.0 40.2 %collective-permute-start.1 = (bf16[2048,256]{1,0:T(8,128)(2,1)S(1)}, bf16[2048,256]{1,0:T(8,128)(2,1)}, u32[]{:S(2)}, u32[]{:S(2)}) collective-permute-start(bf16[2048,256]{1,0:T(8,128)(2,1)S(1)} %copy-done.1), channel_id=1, source_target_pairs={{0,1},{1,0},{2,3},{3,2},{4,5},{5,4},{6,7},{7,6},{8,9},{9,8},{10,11... | collective-permute-start | bytes 3145736 | tf_op jit(solution)/shard_map/ppermute | solution.py:311
  56.5 46.8 %copy-start.2 = (bf16[2048,256]{1,0:T(8,128)(2,1)}, bf16[2048,256]{1,0:T(8,128)(2,1)S(1)}, u32[]{:S(2)}) copy-start(bf16[2048,256]{1,0:T(8,128)(2,1)S(1)} %collective-permute-done.4.refs_4_) | copy-start | bytes 3145732
  56.5 39.8 %collective-permute-start.5 = (bf16[2048,256]{1,0:T(8,128)(2,1)S(1)}, bf16[2048,256]{1,0:T(8,128)(2,1)}, u32[]{:S(2)}, u32[]{:S(2)}) collective-permute-start(bf16[2048,256]{1,0:T(8,128)(2,1)S(1)} %collective-permute-done.4.refs_4_), channel_id=1, source_target_pairs={{0,1},{1,0},{2,3},{3,2},{4,5},{5,4},{6,7},{7,6},{8,9},{9,8},{10,11... | collective-permute-start | bytes 3145736 | tf_op jit(solution)/shard_map/ppermute | solution.py:311
  56.6 39.7 %collective-permute-start.3 = (bf16[2048,256]{1,0:T(8,128)(2,1)}, bf16[2048,256]{1,0:T(8,128)(2,1)}, u32[]{:S(2)}, u32[]{:S(2)}) collective-permute-start(bf16[2048,256]{1,0:T(8,128)(2,1)} %collective-permute-done.2.refs_2_), channel_id=1, source_target_pairs={{0,1},{1,0},{2,3},{3,2},{4,5},{5,4},{6,7},{7,6},{8,9},{9,8},{10,11... | collective-permute-start | bytes 3145736 | tf_op jit(solution)/shard_map/ppermute | solution.py:311
  79.4 16.8 %collective-permute-start.7 = (bf16[2048,256]{1,0:T(8,128)(2,1)}, bf16[2048,256]{1,0:T(8,128)(2,1)}, u32[]{:S(2)}, u32[]{:S(2)}) collective-permute-start(bf16[2048,256]{1,0:T(8,128)(2,1)} %collective-permute-done.6.refs_6_), channel_id=1, source_target_pairs={{0,1},{1,0},{2,3},{3,2},{4,5},{5,4},{6,7},{7,6},{8,9},{9,8},{10,11... | collective-permute-start | bytes 3145736 | tf_op jit(solution)/shard_map/ppermute | solution.py:311
  91.0 0.9 copy-start
  96.3 7.0 %collective-permute-start = (bf16[32,2048]{1,0:T(8,128)(2,1)}, bf16[32,2048]{1,0:T(8,128)(2,1)S(1)}, u32[]{:S(2)}, u32[]{:S(2)}) collective-permute-start(bf16[32,2048]{1,0:T(8,128)(2,1)} %merge.1.own), channel_id=1, source_target_pairs={{0,8},{1,9},{2,10},{3,11},{4,12},{5,13},{6,14},{7,15},{8,0},{9,1},... | collective-permute-start | bytes 393224 | tf_op jit(solution)/shard_map/ppermute | solution.py:317
  103.2 0.7 copy-start.4
  110.2 6.9 %collective-permute-start.8 = (bf16[32,2048]{1,0:T(8,128)(2,1)}, bf16[32,2048]{1,0:T(8,128)(2,1)S(1)}, u32[]{:S(2)}, u32[]{:S(2)}) collective-permute-start(bf16[32,2048]{1,0:T(8,128)(2,1)} %get-tuple-element.8), channel_id=1, source_target_pairs={{0,8},{1,9},{2,10},{3,11},{4,12},{5,13},{6,14},{7,15},{8,0},{9,1},... | collective-permute-start | bytes 393224 | tf_op jit(solution)/shard_map/ppermute | solution.py:329

commit v2 on v1

v2 whole, which is shorter than its diff:
```python
import functools
import math

import jax
import jax.numpy as jnp
from jax import lax
from jax.experimental import pallas as pl
from jax.experimental.pallas import tpu as pltpu
from jax.sharding import PartitionSpec as P


HQ = 16
KVH = 4
HD = 128
GROUP = HQ // KVH
LANES = 128
PARTS = 4
STAT_ROWS = KVH * PARTS
SCALE2 = math.log2(math.e) / math.sqrt(HD)
CHUNK = 512
FLOOR = -(2.0**100)


def iota(shape, axis):
    return lax.broadcasted_iota(jnp.int32, shape, axis)


def fill_slots(page_list, base, members, capacity, source, count):
    tiles, width = page_list.shape

    def clear(i, carry):
        source[i] = -1
        return carry

    lax.fori_loop(0, members * capacity, clear, 0)

    def clear_count(i, carry):
        count[i] = 0
        return carry

    lax.fori_loop(0, members, clear_count, 0)
    for tile in range(tiles):
        for item in range(width):
            page = page_list[tile, item] - base

            @pl.when((page >= 0) & (page < members))
            def _():
                slot = count[page]
                source[page * capacity + slot] = tile
                count[page] = slot + 1


def pack_kernel(members, capacity, base, page_list, queries, packed, source, count):
    tiles = page_list.shape[0]
    rows = queries.shape[0]
    tile_rows = rows // tiles
    slot_rows = capacity * tile_rows
    block = GROUP * slot_rows
    fill_slots(page_list, base[0], members, capacity, source, count)
    row = iota((block, GROUP * rows), 0)
    col = iota((block, GROUP * rows), 1)
    fixed = (row // slot_rows == col // rows) & (row % tile_rows == col % tile_rows)
    slot = row % slot_rows // tile_rows
    tile = col % rows // tile_rows
    pieces = []
    for page in range(members):
        wanted = jnp.full((block, GROUP * rows), -1, jnp.int32)
        for k in range(capacity):
            wanted = jnp.where(slot == k, source[page * capacity + k], wanted)
        pieces.append((fixed & (tile == wanted)).astype(jnp.bfloat16))
    chosen = jnp.concatenate(pieces, axis=0)
    for group in range(KVH):
        stacked = jnp.concatenate(
            [
                queries[:, (group * GROUP + j) * HD : (group * GROUP + j + 1) * HD]
                for j in range(GROUP)
            ],
            axis=0,
        )
        sent = jnp.dot(chosen, stacked, preferred_element_type=jnp.float32).astype(jnp.bfloat16)
        packed[:, group * block : (group + 1) * block, :] = sent.reshape(members, block, HD)


def attend_kernel(queries, keys, values, partial, stats):
    members, block, _ = queries.shape
    rows = members * block
    group = pl.program_id(0)
    asked = queries[...].reshape(rows, HD)
    page = keys.shape[0]
    chunk = min(CHUNK, page)
    ones = jnp.ones((chunk, HD), jnp.bfloat16)
    highest = None
    total = None
    for start in range(0, page, chunk):
        scores = lax.dot_general(
            asked,
            keys[start : start + chunk, :],
            (((1,), (1,)), ((), ())),
            preferred_element_type=jnp.float32,
        )
        here = jnp.max(scores, axis=1, keepdims=True)
        new = here if highest is None else jnp.maximum(highest, here)
        weights = jnp.exp2((scores - new) * SCALE2).astype(jnp.bfloat16)
        extended = jnp.concatenate([values[start : start + chunk, :], ones], axis=1)
        mixed = jnp.dot(weights, extended, preferred_element_type=jnp.float32)
        if total is None:
            total = mixed
        else:
            total = total * jnp.exp2((highest - new) * SCALE2) + mixed
        highest = new
    summed = total[:, HD:]
    result = (total[:, :HD] / summed).astype(jnp.bfloat16).reshape(members, block, HD)
    partial[:, pl.ds(pl.multiple_of(group * block, block), block), :] = result
    peak = jnp.broadcast_to(highest * SCALE2, (rows, LANES))
    peak_high = peak.astype(jnp.bfloat16).astype(jnp.float32)
    peak_low = (peak - peak_high).astype(jnp.bfloat16).astype(jnp.float32)
    moved = summed * jnp.exp2(peak - peak_high - peak_low)
    moved_high = moved.astype(jnp.bfloat16).astype(jnp.float32)
    moved_low = moved - moved_high
    part = iota((rows, LANES), 1) % PARTS
    mixed = jnp.where(
        part == 0,
        peak_high,
        jnp.where(part == 1, peak_low, jnp.where(part == 2, moved_high, moved_low)),
    )
    turned = mixed.T[:STAT_ROWS, :]
    mine = iota((STAT_ROWS, rows), 0) // PARTS == group

    @pl.when(group == 0)
    def _():
        stats[...] = turned

    @pl.when(group > 0)
    def _():
        stats[...] = jnp.where(mine, turned, stats[...])

    @pl.when(group == KVH - 1)
    def _():
        padded = jnp.concatenate(
            [stats[...], jnp.zeros((STAT_ROWS, LANES), jnp.float32)], axis=1
        )
        for member in range(members):
            partial[member, KVH * block :, :] = padded[
                :, member * block : member * block + LANES
            ].astype(jnp.bfloat16)


def split(value):
    high = value.astype(jnp.bfloat16).astype(jnp.float32)
    return high, (value - high).astype(jnp.bfloat16).astype(jnp.float32)


def stacked_heads(queries, group):
    return jnp.concatenate(
        [
            queries[:, (group * GROUP + j) * HD : (group * GROUP + j + 1) * HD]
            for j in range(GROUP)
        ],
        axis=0,
    )


def own_partial(queries, new_keys, new_values, causal, group):
    scores = lax.dot_general(
        stacked_heads(queries, group),
        new_keys[:, group * HD : (group + 1) * HD],
        (((1,), (1,)), ((), ())),
        preferred_element_type=jnp.float32,
    )
    scores = jnp.where(causal, scores, -jnp.inf)
    peak = jnp.max(scores, axis=1, keepdims=True)
    weights = jnp.exp2((scores - peak) * SCALE2)
    total = jnp.sum(weights, axis=1, keepdims=True)
    mixed = jnp.dot(
        weights.astype(jnp.bfloat16),
        new_values[:, group * HD : (group + 1) * HD],
        preferred_element_type=jnp.float32,
    )
    return peak * SCALE2, total, mixed


def merge_kernel(members, capacity, with_own, base, page_list, *refs):
    own_refs = refs[:3] if with_own else ()
    returned, merged, source, count = refs[len(own_refs) :]
    tiles = page_list.shape[0]
    tall = (merged.shape[0] - STAT_ROWS) // KVH
    rows = tall // GROUP
    tile_rows = rows // tiles
    slot_rows = capacity * tile_rows
    block = GROUP * slot_rows
    width = members * block
    fill_slots(page_list, base[0], members, capacity, source, count)
    lane = iota((8, width), 1)
    lane_slot = lane // block * capacity + lane % slot_rows // tile_rows
    wanted = jnp.full((8, width), -1, jnp.int32)
    for slot in range(members * capacity):
        wanted = jnp.where(lane_slot == slot, source[slot], wanted)
    lane_code = (wanted * tile_rows + lane % tile_rows) + (lane % block // slot_rows) * rows
    lane_code = jnp.where(wanted < 0, -1, lane_code)[:1, :]
    bias = jnp.where(iota((tall, width), 0) == lane_code, 0.0, -jnp.inf)
    stat_pieces = [
        returned[member, KVH * block :, :].astype(jnp.float32)[:, :block]
        for member in range(members)
    ]
    stats = jnp.concatenate(stat_pieces, axis=1)
    if with_own:
        own_row = iota((tall, rows), 0) % rows
        own_col = iota((tall, rows), 1)
        causal = (own_row // tile_rows == own_col // tile_rows) & (own_col <= own_row)
    part = iota((tall, LANES), 1)
    columns = jnp.zeros((tall, LANES), jnp.float32)
    for group in range(KVH):
        at = group * PARTS
        peak = bias + (stats[at : at + 1, :] + stats[at + 1 : at + 2, :])
        moved = stats[at + 2 : at + 3, :] + stats[at + 3 : at + 4, :]
        top = jnp.maximum(jnp.max(peak, axis=1, keepdims=True), FLOOR)
        if with_own:
            own_peak, own_total, own_sum = own_partial(*own_refs, causal, group)
            top = jnp.maximum(top, own_peak)
        factor = jnp.exp2(peak - top) * moved
        denom = jnp.sum(factor, axis=1, keepdims=True)
        if with_own:
            own_factor = jnp.exp2(own_peak - top)
            denom = denom + own_factor * own_total
        inverse = 1.0 / jnp.where(denom > 0.0, denom, 1.0)
        factor = factor * inverse
        high = factor.astype(jnp.bfloat16)
        low = (factor - high.astype(jnp.float32)).astype(jnp.bfloat16)
        outs = returned[:, group * block : (group + 1) * block, :].reshape(width, HD)
        numer = jnp.dot(high, outs, preferred_element_type=jnp.float32) + jnp.dot(
            low, outs, preferred_element_type=jnp.float32
        )
        if with_own:
            numer = numer + own_factor * inverse * own_sum
        merged[group * tall : (group + 1) * tall, :] = numer.astype(jnp.bfloat16)
        peak_high, peak_low = split(top)
        moved_high, moved_low = split(denom * jnp.exp2(top - peak_high - peak_low))
        for i, value in enumerate((peak_high, peak_low, moved_high, moved_low)):
            columns = jnp.where(part == at + i, value, columns)
    merged[KVH * tall :, :tall] = columns.T[:STAT_ROWS, :].astype(jnp.bfloat16)


def combine(tall, first, second):
    rows = tall // GROUP
    a = first[KVH * tall :, :].astype(jnp.float32)
    b = second[KVH * tall :, :].astype(jnp.float32)
    shares = []
    for group in range(KVH):
        at = group * PARTS
        a_peak = a[at : at + 1, :] + a[at + 1 : at + 2, :]
        b_peak = b[at : at + 1, :] + b[at + 1 : at + 2, :]
        a_total = a[at + 2 : at + 3, :] + a[at + 3 : at + 4, :]
        b_total = b[at + 2 : at + 3, :] + b[at + 3 : at + 4, :]
        top = jnp.maximum(a_peak, b_peak)
        a_factor = a_total * jnp.exp2(a_peak - top)
        b_factor = b_total * jnp.exp2(b_peak - top)
        denom = a_factor + b_factor
        shares += [a_factor / denom, b_factor / denom]
    shares = jnp.concatenate(
        shares + [jnp.zeros((LANES - len(shares), LANES), jnp.float32)], axis=0
    ).T
    heads = []
    for group in range(KVH):
        rows_at = slice(group * tall, (group + 1) * tall)
        mixed = (
            first[rows_at, :].astype(jnp.float32) * shares[:tall, 2 * group : 2 * group + 1]
            + second[rows_at, :].astype(jnp.float32)
            * shares[:tall, 2 * group + 1 : 2 * group + 2]
        ).astype(jnp.bfloat16)
        heads += [mixed[j * rows : (j + 1) * rows, :] for j in range(GROUP)]
    return jnp.concatenate(heads, axis=1)


def attended_kernel(first, second, attended):
    tall = (first.shape[0] - STAT_ROWS) // KVH
    attended[...] = combine(tall, first, second)


def project_kernel(count, places, own_a, own_b, other_a, other_b, me, *refs):
    weights = refs[: len(places)]
    own_out, other_out = refs[len(places) : len(places) + 2]
    held, sems = refs[len(places) + 2 :]
    width = weights[0].shape[1]
    copies = {k: [] for k in range(count)}
    for i, (k, start) in enumerate(places):
        copy = pltpu.make_async_copy(
            weights[i], held.at[k, start : start + weights[i].shape[0], :], sems.at[i]
        )
        copy.start()
        copies[k].append(copy)
    tall = (own_a.shape[0] - STAT_ROWS) // KVH
    rows = tall // GROUP
    left = jnp.concatenate(
        [combine(tall, own_a, own_b), combine(tall, other_a, other_b)], axis=0
    )
    for k in range(count):
        for copy in copies[k]:
            copy.wait()
        made = jnp.dot(left, held[k], preferred_element_type=jnp.float32).astype(jnp.bfloat16)
        at = pl.ds(pl.multiple_of((me[0] ^ k) * width, width), width)
        own_out[:, at] = made[:rows, :]
        other_out[:, at] = made[rows:, :]


VMEM = pl.BlockSpec(memory_space=pltpu.VMEM)
SMEM = pl.BlockSpec(memory_space=pltpu.SMEM)
ANY = pl.BlockSpec(memory_space=pl.ANY)
SMALL = pltpu.CompilerParams(vmem_limit_bytes=16 << 20)


def slot_scratch(members, capacity):
    return [
        pltpu.SMEM((members * capacity,), jnp.int32),
        pltpu.SMEM((members,), jnp.int32),
    ]


def shards(queries, new_keys, new_values, keys, values, page_list, out_weight):
    members = lax.axis_size("seq")
    me = lax.axis_index("seq")
    tile_count, list_width = page_list.shape
    row_total, features = queries.shape
    tile_rows = row_total // tile_count
    capacity = max(1, 2 * tile_count * list_width // members)
    block = GROUP * capacity * tile_rows
    half = members // 2
    tall = GROUP * row_total
    halves = [list(range(half)), list(range(half, members))]
    base = (me // half * half).reshape(1)
    page = keys.shape[0]
    rows = half * block

    def mirrored(array):
        return lax.ppermute(array, "seq", [(i, (i + half) % members) for i in range(members)])

    def pack(tiles, listed):
        return pl.pallas_call(
            functools.partial(pack_kernel, half, capacity),
            out_shape=jax.ShapeDtypeStruct((half, KVH * block, HD), jnp.bfloat16),
            in_specs=[SMEM, SMEM, VMEM],
            out_specs=VMEM,
            scratch_shapes=slot_scratch(half, capacity),
            compiler_params=SMALL,
            name="pack",
        )(base, listed, tiles)

    def spread(array):
        return lax.all_to_all(
            array, "seq", split_axis=0, concat_axis=0, tiled=True, axis_index_groups=halves
        )

    def attend(incoming):
        return pl.pallas_call(
            attend_kernel,
            out_shape=jax.ShapeDtypeStruct((half, KVH * block + STAT_ROWS, HD), jnp.bfloat16),
            grid=(KVH,),
            in_specs=[
                pl.BlockSpec((half, block, HD), lambda g: (0, g, 0)),
                pl.BlockSpec((page, HD), lambda g: (0, g)),
                pl.BlockSpec((page, HD), lambda g: (0, g)),
            ],
            out_specs=pl.BlockSpec((half, KVH * block + STAT_ROWS, HD), lambda g: (0, 0, 0)),
            scratch_shapes=[pltpu.VMEM((STAT_ROWS, rows), jnp.float32)],
            compiler_params=pltpu.CompilerParams(
                dimension_semantics=("arbitrary",), vmem_limit_bytes=58 << 20
            ),
            cost_estimate=pl.CostEstimate(
                flops=4 * rows * KVH * page * HD,
                bytes_accessed=4 * page * KVH * HD,
                transcendentals=rows * KVH * page,
            ),
            name="attend",
        )(incoming, keys, values)

    def merge(listed, returned, own):
        return pl.pallas_call(
            functools.partial(merge_kernel, half, capacity, bool(own)),
            out_shape=jax.ShapeDtypeStruct((KVH * tall + STAT_ROWS, HD), jnp.bfloat16),
            in_specs=[SMEM, SMEM] + [VMEM] * (len(own) + 1),
            out_specs=VMEM,
            scratch_shapes=slot_scratch(half, capacity),
            compiler_params=SMALL,
            name="merge",
        )(base, listed, *own, returned)

    other_queries = mirrored(queries)
    other_list = mirrored(page_list)
    packed_near = pack(queries, page_list)
    near = spread(packed_near)
    packed_far = pack(other_queries, other_list)
    far = spread(packed_far)
    near_partial = attend(near)
    near_back = spread(near_partial)
    far_partial = attend(far)
    far_back = spread(far_partial)
    own_a = merge(page_list, near_back, (queries, new_keys, new_values))
    other_b = merge(other_list, far_back, ())
    other_a = mirrored(own_a)
    own_b = mirrored(other_b)

    width = out_weight.shape[1]
    if width % LANES or members & (members - 1):
        attended = pl.pallas_call(
            attended_kernel,
            out_shape=jax.ShapeDtypeStruct((row_total, features), jnp.bfloat16),
            in_specs=[VMEM, VMEM],
            out_specs=VMEM,
            name="combine",
        )(own_a, own_b)
        return jnp.dot(
            attended,
            lax.all_gather(out_weight, "seq", axis=1, tiled=True),
            preferred_element_type=jnp.float32,
        ).astype(jnp.bfloat16)

    def exchanged(array, step):
        return lax.ppermute(array, "seq", [(i, i ^ step) for i in range(members)])

    middle = features // 2

    def upper(pieces):
        return pieces[0] if len(pieces) > 1 else pieces[0][:middle, :]

    def lower(pieces):
        return pieces[1] if len(pieces) > 1 else pieces[0][middle:, :]

    same_core = {0: [out_weight]}
    for step in range(2, half, 2):
        low = step & -step
        if low == step:
            same_core[step] = [exchanged(out_weight, step)]
    for step in range(2, half, 2):
        low = step & -step
        if low != step:
            same_core[step] = [
                exchanged(upper(same_core[step ^ low]), low),
                exchanged(lower(same_core[low]), step ^ low),
            ]
    gathered = []
    places = []
    for step, pieces in same_core.items():
        for i, piece in enumerate(pieces):
            gathered += [piece, exchanged(piece, 1)]
            places += [(step, i * middle), (step + 1, i * middle)]
    own_out, other_out = pl.pallas_call(
        functools.partial(project_kernel, half, tuple(places)),
        out_shape=[jax.ShapeDtypeStruct((row_total, half * width), jnp.bfloat16)] * 2,
        in_specs=[VMEM] * 4 + [SMEM] + [ANY] * len(places),
        out_specs=[VMEM, VMEM],
        scratch_shapes=[
            pltpu.VMEM((half, features, width), jnp.bfloat16),
            pltpu.SemaphoreType.DMA((len(places),)),
        ],
        compiler_params=pltpu.CompilerParams(vmem_limit_bytes=60 << 20),
        name="project",
    )(own_a, own_b, other_a, other_b, (me % half).reshape(1), *gathered)
    received = mirrored(other_out)
    first = me < half
    return jnp.concatenate(
        [jnp.where(first, own_out, received), jnp.where(first, received, own_out)], axis=1
    )


def solution(mesh):
    return jax.shard_map(
        shards,
        mesh=mesh,
        in_specs=(
            P(("groups", "seq"), None),
            P(("groups", "seq"), None),
            P(("groups", "seq"), None),
            P(("groups", "seq"), None),
            P(("groups", "seq"), None),
            P(("groups", "seq"), None),
            P(None, "seq"),
        ),
        out_specs=P(("groups", "seq"), None),
        check_vma=False,
    )
```

time: 119 us -> 115 us (0.966)
  waiting for transfers between devices: 63.4 us -> 40.2 us
  starting transfers between devices: 17.2 us -> 30.3 us
  Pallas kernels: 32.7 us -> 37.6 us
    all_to_all x2 -> x4, waiting for transfers between devices: 27.1 us -> 4.89 us  [spread(): lax.all_to_all(array, 'seq', split_axis=0, concat_axis=0, tiled=True, axi...]
    ppermute x7 -> x9, waiting for transfers between devices: 22.5 us -> 11.5 us  [exchanged(): return lax.ppermute(array, 'seq', [(i, i ^ step) for i in range(members)])]
    ppermute x2 -> x5, waiting for transfers between devices: 13.8 us -> 23.8 us  [mirrored(): lax.ppermute(array, 'seq', [(i, (i + half) % members) for i in range(memb...]
    all_to_all x2 -> x4, starting transfers between devices: 12.6 us -> 19 us  [spread(): lax.all_to_all(array, 'seq', split_axis=0, concat_axis=0, tiled=True, axi...]
    pallas_call x4 -> x7, Pallas kernels: 32.7 us -> 37.6 us  [the longest x2 23.2 us: attend(): pl.pallas_call(attend_kernel, out_shape=jax.ShapeDtypeStruct((half, KVH *...]
    ppermute x2 -> x5, starting transfers between devices: 0.07 us -> 4.39 us  [mirrored(): lax.ppermute(array, 'seq', [(i, (i + half) % members) for i in range(memb...]
    ppermute x7 -> x9, starting transfers between devices: 4.54 us -> 6.95 us  [exchanged(): return lax.ppermute(array, 'seq', [(i, i ^ step) for i in range(members)])]
    slice x0 -> x2, local copies, waits for them, and re-layouts: none -> 1.8 us  [the longest x1 0.92 us: lower(): return pieces[1] if len(pieces) > 1 else pieces[0][middle:, :]]
  transfers between devices with their start and end apart: 11 -> 18, of which waited for: 5 -> 6; matrix products, arithmetic and copies ran while one was open for 0% -> 2% of each run, Pallas kernels for 20% -> 26%
where the time goes in v2:
time: 115 us; the launch traced here: 114 us
  waiting for transfers between devices  40.2 us (35%)
  Pallas kernels  37.6 us (33%)
  starting transfers between devices  30.3 us (26%)
  local copies, waits for them, and re-layouts  4.1 us (4%)
  other arithmetic  1.65 us (1%)
    ppermute x5, waiting for transfers between devices, mirrored(): lax.ppermute(array, 'seq', [(i, (i + half) % members) for i in range(memb...  23.8 us
    pallas_call x2, Pallas kernels, attend(): pl.pallas_call(attend_kernel, out_shape=jax.ShapeDtypeStruct((half, KVH *...  23.2 us
    all_to_all x4, starting transfers between devices, spread(): lax.all_to_all(array, 'seq', split_axis=0, concat_axis=0, tiled=True, axi...  19 us
    ppermute x9, waiting for transfers between devices, exchanged(): return lax.ppermute(array, 'seq', [(i, i ^ step) for i in range(members)])  11.5 us
    ppermute x9, starting transfers between devices, exchanged(): return lax.ppermute(array, 'seq', [(i, i ^ step) for i in range(members)])  6.95 us
    pallas_call x1, Pallas kernels, shards(): pl.pallas_call(functools.partial(project_kernel, half, tuple(places)), ou...  6.52 us
    all_to_all x4, waiting for transfers between devices, spread(): lax.all_to_all(array, 'seq', split_axis=0, concat_axis=0, tiled=True, axi...  4.89 us
    ppermute x5, starting transfers between devices, mirrored(): lax.ppermute(array, 'seq', [(i, (i + half) % members) for i in range(memb...  4.39 us
  transfers between devices with their start and end apart: 18, of which 6 were waited for; matrix products, arithmetic and copies ran while one was open for 2% of the time, Pallas kernels for 26%

profile of v2, /device:TPU:0, one launch (start us, length us, event | category | flops | bytes accessed | tf_op | source)
XLA Modules:
  0.0 114.1 jit_solution(3123895828906415700)
XLA Ops:
  0.0 0.8 copy.9.page_list
  0.8 0.9 copy-done.2
  1.7 1.9 %pack.2 = bf16[8,192,128]{2,1,0:T(8,128)(2,1)} custom-call(s32[1]{0:T(128)} %bitcast.base, s32[8,3]{1,0:T(8,128)S(1)} %copy.9.page_list, bf16[32,2048]{1,0:T(8,128)(2,1)S(1)} %copy-done.2), custom_call_target="tpu_custom_call" | custom-call | tf_op jit(solution)/shard_map/pack/pallas_call | solution.py:337
  3.6 5.3 %all-to-all-start = ((bf16[8,192,128]{2,1,0:T(8,128)(2,1)}), bf16[8,192,128]{2,1,0:T(8,128)(2,1)S(1)}, u32[]{:S(2)}, u32[]{:S(2)}) async-start(bf16[8,192,128]{2,1,0:T(8,128)(2,1)} %pack.2), calls=%async_computation | async-start | bytes 786432 | tf_op jit(solution)/shard_map/all_to_all | solution.py:348
  8.9 2.6 %collective-permute-start.1 = (bf16[32,2048]{1,0:T(8,128)(2,1)}, bf16[32,2048]{1,0:T(8,128)(2,1)S(1)}, u32[]{:S(2)}, u32[]{:S(2)}) collective-permute-start(bf16[32,2048]{1,0:T(8,128)(2,1)} %refs_0_.2), channel_id=1, source_target_pairs={{0,8},{1,9},{2,10},{3,11},{4,12},{5,13},{6,14},{7,15},{8,0},{9,1},... | collective-permute-start | bytes 393224 | tf_op jit(solution)/shard_map/ppermute | solution.py:334
  11.8 5.4 %collective-permute-done.page_list = s32[8,3]{1,0:T(8,128)S(1)} collective-permute-done((s32[8,3]{1,0:T(8,128)S(1)}, s32[8,3]{1,0:T(8,128)S(1)}, u32[]{:S(2)}, u32[]{:S(2)}) %collective-permute-start) | collective-permute-done | bytes 128 | tf_op jit(solution)/shard_map/ppermute | solution.py:334
  17.2 1.9 %pack.3 = bf16[8,192,128]{2,1,0:T(8,128)(2,1)} custom-call(s32[1]{0:T(128)} %bitcast.base, s32[8,3]{1,0:T(8,128)S(1)} %collective-permute-done.page_list, bf16[32,2048]{1,0:T(8,128)(2,1)S(1)} %collective-permute-done.1.queries), custom_call_target="tpu_custom_call" | custom-call | tf_op jit(solution)/shard_map/pack/pallas_call | solution.py:337
  19.2 6.7 %all-to-all-start.2 = ((bf16[8,192,128]{2,1,0:T(8,128)(2,1)}), bf16[8,192,128]{2,1,0:T(8,128)(2,1)S(1)}, u32[]{:S(2)}, u32[]{:S(2)}) async-start(bf16[8,192,128]{2,1,0:T(8,128)(2,1)} %pack.3), calls=%async_computation.2 | async-start | bytes 786432 | tf_op jit(solution)/shard_map/all_to_all | solution.py:348
  25.9 2.0 %collective-permute-start.5 = (bf16[2048,256]{1,0:T(8,128)(2,1)}, bf16[2048,256]{1,0:T(8,128)(2,1)S(1)}, u32[]{:S(2)}, u32[]{:S(2)}) collective-permute-start(bf16[2048,256]{1,0:T(8,128)(2,1)} %refs_0_.3), channel_id=1, source_target_pairs={{0,2},{1,3},{2,0},{3,1},{4,6},{5,7},{6,4},{7,5},{8,10},{9,11},{10,... | collective-permute-start | bytes 3145736 | tf_op jit(solution)/shard_map/ppermute | solution.py:417
  27.9 1.5 %collective-permute-start.7 = (bf16[2048,256]{1,0:T(8,128)(2,1)}, bf16[2048,256]{1,0:T(8,128)(2,1)S(1)}, u32[]{:S(2)}, u32[]{:S(2)}) collective-permute-start(bf16[2048,256]{1,0:T(8,128)(2,1)} %refs_0_.3), channel_id=1, source_target_pairs={{0,4},{1,5},{2,6},{3,7},{4,0},{5,1},{6,2},{7,3},{8,12},{9,13},{10,... | collective-permute-start | bytes 3145736 | tf_op jit(solution)/shard_map/ppermute | solution.py:417
  29.4 11.6 %attend.2 = bf16[8,208,128]{2,1,0:T(8,128)(2,1)} custom-call(bf16[8,192,128]{2,1,0:T(8,128)(2,1)} %copy-done.9, bf16[4096,512]{1,0:T(8,128)(2,1)} %keys.3, bf16[4096,512]{1,0:T(8,128)(2,1)} %values.3), custom_call_target="tpu_custom_call" | custom-call | flops 3221225472 | bytes 8388608 | tf_op jit(solution)/shard_map/attend/pallas_call | solution.py:353
  41.0 3.5 %all-to-all-start.1 = ((bf16[8,208,128]{2,1,0:T(8,128)(2,1)}), bf16[8,208,128]{2,1,0:T(8,128)(2,1)S(1)}, u32[]{:S(2)}, u32[]{:S(2)}) async-start(bf16[8,208,128]{2,1,0:T(8,128)(2,1)} %attend.2), calls=%async_computation.1 | async-start | bytes 851968 | tf_op jit(solution)/shard_map/all_to_all | solution.py:348
  44.4 0.4 collective-permute-start.4
  44.9 11.5 %collective-permute-done.5.refs_2_ = bf16[2048,256]{1,0:T(8,128)(2,1)S(1)} collective-permute-done((bf16[2048,256]{1,0:T(8,128)(2,1)}, bf16[2048,256]{1,0:T(8,128)(2,1)S(1)}, u32[]{:S(2)}, u32[]{:S(2)}) %collective-permute-start.5) | collective-permute-done | bytes 1048608 | tf_op jit(solution)/shard_map/ppermute | solution.py:417
  56.3 0.9 slice.9
  57.3 1.5 %collective-permute-start.11 = (bf16[1024,256]{1,0:T(8,128)(2,1)}, bf16[1024,256]{1,0:T(8,128)(2,1)}, u32[]{:S(2)}, u32[]{:S(2)}) collective-permute-start(bf16[1024,256]{1,0:T(8,128)(2,1)} %slice.9), channel_id=1, source_target_pairs={{0,4},{1,5},{2,6},{3,7},{4,0},{5,1},{6,2},{7,3},{8,12},{9,13},{10,... | collective-permute-start | bytes 1572872 | tf_op jit(solution)/shard_map/ppermute | solution.py:417
  58.7 0.9 slice.8
  59.6 0.5 collective-permute-start.9
  60.1 0.5 collective-permute-start.8
  60.6 11.6 %attend.3 = bf16[8,208,128]{2,1,0:T(8,128)(2,1)} custom-call(bf16[8,192,128]{2,1,0:T(8,128)(2,1)} %copy-done.8, bf16[4096,512]{1,0:T(8,128)(2,1)} %keys.3, bf16[4096,512]{1,0:T(8,128)(2,1)} %values.3), custom_call_target="tpu_custom_call" | custom-call | flops 3221225472 | bytes 8388608 | tf_op jit(solution)/shard_map/attend/pallas_call | solution.py:353
  72.3 3.5 %all-to-all-start.3 = ((bf16[8,208,128]{2,1,0:T(8,128)(2,1)}), bf16[8,208,128]{2,1,0:T(8,128)(2,1)S(1)}, u32[]{:S(2)}, u32[]{:S(2)}) async-start(bf16[8,208,128]{2,1,0:T(8,128)(2,1)} %attend.3), calls=%async_computation.3 | async-start | bytes 851968 | tf_op jit(solution)/shard_map/all_to_all | solution.py:348
  76.3 2.4 %merge.2.own_a = bf16[528,128]{1,0:T(8,128)(2,1)S(1)} custom-call(s32[1]{0:T(128)} %bitcast.base, s32[8,3]{1,0:T(8,128)S(1)} %copy.9.page_list, bf16[32,2048]{1,0:T(8,128)(2,1)S(1)} %copy-done.3, bf16[32,512]{1,0:T(8,128)(2,1)S(1)} %copy-done.4, bf16[32,512]{1,0:T(8,128)(2,1)S(1)} %copy-done.5, bf16[8,208,128]{2,1,0:T(8,128)(2,1)S(1)} %all-to-all-done.1.refs_3_), custom_call_target="tpu_custom_call" | custom-call | tf_op jit(solution)/shard_map/merge/pallas_call | solution.py:376
  78.8 1.4 %collective-permute-start.3 = (bf16[528,128]{1,0:T(8,128)(2,1)S(1)}, bf16[528,128]{1,0:T(8,128)(2,1)S(1)}, u32[]{:S(2)}, u32[]{:S(2)}) collective-permute-start(bf16[528,128]{1,0:T(8,128)(2,1)S(1)} %merge.2.own_a), channel_id=1, source_target_pairs={{0,8},{1,9},{2,10},{3,11},{4,12},{5,13},{6,14},{7,15},{8,0},{9,1},... | collective-permute-start | bytes 405512 | tf_op jit(solution)/shard_map/ppermute | solution.py:334
  80.2 4.9 %all-to-all-done.3.refs_0_ = bf16[8,208,128]{2,1,0:T(8,128)(2,1)S(1)} async-done(((bf16[8,208,128]{2,1,0:T(8,128)(2,1)}), bf16[8,208,128]{2,1,0:T(8,128)(2,1)S(1)}, u32[]{:S(2)}, u32[]{:S(2)}) %all-to-all-start.3) | async-done | bytes 426016 | tf_op jit(solution)/shard_map/all_to_all | solution.py:348
  85.1 1.7 %merge.3.other_b = bf16[528,128]{1,0:T(8,128)(2,1)S(1)} custom-call(s32[1]{0:T(128)} %bitcast.base, s32[8,3]{1,0:T(8,128)S(1)} %collective-permute-done.page_list, bf16[8,208,128]{2,1,0:T(8,128)(2,1)S(1)} %all-to-all-done.3.refs_0_), custom_call_target="tpu_custom_call" | custom-call | tf_op jit(solution)/shard_map/merge/pallas_call | solution.py:376
  86.8 1.8 %collective-permute-done.3.other_a = bf16[528,128]{1,0:T(8,128)(2,1)S(1)} collective-permute-done((bf16[528,128]{1,0:T(8,128)(2,1)S(1)}, bf16[528,128]{1,0:T(8,128)(2,1)S(1)}, u32[]{:S(2)}, u32[]{:S(2)}) %collective-permute-start.3) | collective-permute-done | bytes 135200 | tf_op jit(solution)/shard_map/ppermute | solution.py:334
  88.6 8.5 %collective-permute-done.2.own_b = bf16[528,128]{1,0:T(8,128)(2,1)S(1)} collective-permute-done((bf16[528,128]{1,0:T(8,128)(2,1)S(1)}, bf16[528,128]{1,0:T(8,128)(2,1)S(1)}, u32[]{:S(2)}, u32[]{:S(2)}) %collective-permute-start.2) | collective-permute-done | bytes 135200 | tf_op jit(solution)/shard_map/ppermute | solution.py:334
  97.1 0.6 copy-done.11
  97.7 6.5 %project.1 = (bf16[32,2048]{1,0:T(8,128)(2,1)}, bf16[32,2048]{1,0:T(8,128)(2,1)}) custom-call(bf16[528,128]{1,0:T(8,128)(2,1)} %copy-done.1, bf16[528,128]{1,0:T(8,128)(2,1)} %copy-done.11, bf16[528,128]{1,0:T(8,128)(2,1)} %copy-done.10, bf16[528,128]{1,0:T(8,128)(2,1)} %copy-done, s32[1]{0:T(128)} %bitcast.1.me, bf16[2048,256]{1,0:T(8,128)(2,1)} %refs_0_.3, ...), custom_call_target="tpu_custom_call" | custom-call | tf_op jit(solution)/shard_map/project/pallas_call | solution.py:445
  104.4 8.1 %collective-permute-done.13 = bf16[32,2048]{1,0:T(8,128)(2,1)S(1)} collective-permute-done((bf16[32,2048]{1,0:T(8,128)(2,1)}, bf16[32,2048]{1,0:T(8,128)(2,1)S(1)}, u32[]{:S(2)}, u32[]{:S(2)}) %collective-permute-start.13) | collective-permute-done | bytes 131104 | tf_op jit(solution)/shard_map/ppermute | solution.py:334
  112.4 0.9 broadcast_select_fusion.1
  113.4 0.7 pad_maximum_fusion
  (40 shorter events, 1.1 us)
Async XLA Ops:
  0.8 0.9 copy-start.2
  3.6 15.6 %all-to-all-start = ((bf16[8,192,128]{2,1,0:T(8,128)(2,1)}), bf16[8,192,128]{2,1,0:T(8,128)(2,1)S(1)}, u32[]{:S(2)}, u32[]{:S(2)}) async-start(bf16[8,192,128]{2,1,0:T(8,128)(2,1)} %pack.2), calls=%async_computation | async-start | bytes 786432 | tf_op jit(solution)/shard_map/all_to_all | solution.py:348
  8.9 8.4 %collective-permute-start.1 = (bf16[32,2048]{1,0:T(8,128)(2,1)}, bf16[32,2048]{1,0:T(8,128)(2,1)S(1)}, u32[]{:S(2)}, u32[]{:S(2)}) collective-permute-start(bf16[32,2048]{1,0:T(8,128)(2,1)} %refs_0_.2), channel_id=1, source_target_pairs={{0,8},{1,9},{2,10},{3,11},{4,12},{5,13},{6,14},{7,15},{8,0},{9,1},... | collective-permute-start | bytes 393224 | tf_op jit(solution)/shard_map/ppermute | solution.py:334
  11.5 5.8 %collective-permute-start = (s32[8,3]{1,0:T(8,128)S(1)}, s32[8,3]{1,0:T(8,128)S(1)}, u32[]{:S(2)}, u32[]{:S(2)}) collective-permute-start(s32[8,3]{1,0:T(8,128)S(1)} %copy.9.page_list), channel_id=1, source_target_pairs={{0,8},{1,9},{2,10},{3,11},{4,12},{5,13},{6,14},{7,15},{8,0},{9,1},... | collective-permute-start | bytes 296 | tf_op jit(solution)/shard_map/ppermute | solution.py:334
  19.2 10.2 %copy-start.9 = (bf16[8,192,128]{2,1,0:T(8,128)(2,1)}, bf16[8,192,128]{2,1,0:T(8,128)(2,1)S(1)}, u32[]{:S(2)}) copy-start(bf16[8,192,128]{2,1,0:T(8,128)(2,1)S(1)} %all-to-all-done.queries) | copy-start | bytes 1179652
  19.2 21.8 %all-to-all-start.2 = ((bf16[8,192,128]{2,1,0:T(8,128)(2,1)}), bf16[8,192,128]{2,1,0:T(8,128)(2,1)S(1)}, u32[]{:S(2)}, u32[]{:S(2)}) async-start(bf16[8,192,128]{2,1,0:T(8,128)(2,1)} %pack.3), calls=%async_computation.2 | async-start | bytes 786432 | tf_op jit(solution)/shard_map/all_to_all | solution.py:348
  25.9 30.4 %collective-permute-start.5 = (bf16[2048,256]{1,0:T(8,128)(2,1)}, bf16[2048,256]{1,0:T(8,128)(2,1)S(1)}, u32[]{:S(2)}, u32[]{:S(2)}) collective-permute-start(bf16[2048,256]{1,0:T(8,128)(2,1)} %refs_0_.3), channel_id=1, source_target_pairs={{0,2},{1,3},{2,0},{3,1},{4,6},{5,7},{6,4},{7,5},{8,10},{9,11},{10,... | collective-permute-start | bytes 3145736 | tf_op jit(solution)/shard_map/ppermute | solution.py:417
  27.9 30.8 %collective-permute-start.7 = (bf16[2048,256]{1,0:T(8,128)(2,1)}, bf16[2048,256]{1,0:T(8,128)(2,1)S(1)}, u32[]{:S(2)}, u32[]{:S(2)}) collective-permute-start(bf16[2048,256]{1,0:T(8,128)(2,1)} %refs_0_.3), channel_id=1, source_target_pairs={{0,4},{1,5},{2,6},{3,7},{4,0},{5,1},{6,2},{7,3},{8,12},{9,13},{10,... | collective-permute-start | bytes 3145736 | tf_op jit(solution)/shard_map/ppermute | solution.py:417
  41.0 19.7 %copy-start.8 = (bf16[8,192,128]{2,1,0:T(8,128)(2,1)}, bf16[8,192,128]{2,1,0:T(8,128)(2,1)S(1)}, u32[]{:S(2)}) copy-start(bf16[8,192,128]{2,1,0:T(8,128)(2,1)S(1)} %all-to-all-done.2.queries) | copy-start | bytes 1179652
  41.0 31.3 %all-to-all-start.1 = ((bf16[8,208,128]{2,1,0:T(8,128)(2,1)}), bf16[8,208,128]{2,1,0:T(8,128)(2,1)S(1)}, u32[]{:S(2)}, u32[]{:S(2)}) async-start(bf16[8,208,128]{2,1,0:T(8,128)(2,1)} %attend.2), calls=%async_computation.1 | async-start | bytes 851968 | tf_op jit(solution)/shard_map/all_to_all | solution.py:348
  44.4 34.4 %collective-permute-start.4 = (bf16[2048,256]{1,0:T(8,128)(2,1)}, bf16[2048,256]{1,0:T(8,128)(2,1)}, u32[]{:S(2)}, u32[]{:S(2)}) collective-permute-start(bf16[2048,256]{1,0:T(8,128)(2,1)} %refs_0_.3), channel_id=1, source_target_pairs={{0,1},{1,0},{2,3},{3,2},{4,5},{5,4},{6,7},{7,6},{8,9},{9,8},{10,11... | collective-permute-start | bytes 3145736 | tf_op jit(solution)/shard_map/ppermute | solution.py:417
  56.3 15.9 %copy-start.6 = (bf16[2048,256]{1,0:T(8,128)(2,1)}, bf16[2048,256]{1,0:T(8,128)(2,1)S(1)}, u32[]{:S(2)}) copy-start(bf16[2048,256]{1,0:T(8,128)(2,1)S(1)} %collective-permute-done.5.refs_2_) | copy-start | bytes 3145732
  57.3 18.5 %collective-permute-start.11 = (bf16[1024,256]{1,0:T(8,128)(2,1)}, bf16[1024,256]{1,0:T(8,128)(2,1)}, u32[]{:S(2)}, u32[]{:S(2)}) collective-permute-start(bf16[1024,256]{1,0:T(8,128)(2,1)} %slice.9), channel_id=1, source_target_pairs={{0,4},{1,5},{2,6},{3,7},{4,0},{5,1},{6,2},{7,3},{8,12},{9,13},{10,... | collective-permute-start | bytes 1572872 | tf_op jit(solution)/shard_map/ppermute | solution.py:417
  58.7 13.5 %copy-start.7 = (bf16[2048,256]{1,0:T(8,128)(2,1)}, bf16[2048,256]{1,0:T(8,128)(2,1)S(1)}, u32[]{:S(2)}) copy-start(bf16[2048,256]{1,0:T(8,128)(2,1)S(1)} %collective-permute-done.7.refs_4_) | copy-start | bytes 3145732
  59.6 16.7 %copy-start.3 = (bf16[32,2048]{1,0:T(8,128)(2,1)S(1)}, bf16[32,2048]{1,0:T(8,128)(2,1)}, u32[]{:S(2)}) copy-start(bf16[32,2048]{1,0:T(8,128)(2,1)} %refs_0_.2) | copy-start | bytes 393220
  59.6 16.7 %copy-start.4 = (bf16[32,512]{1,0:T(8,128)(2,1)S(1)}, bf16[32,512]{1,0:T(8,128)(2,1)}, u32[]{:S(2)}) copy-start(bf16[32,512]{1,0:T(8,128)(2,1)} %refs_1_.1) | copy-start | bytes 98308
  59.6 16.7 %copy-start.5 = (bf16[32,512]{1,0:T(8,128)(2,1)S(1)}, bf16[32,512]{1,0:T(8,128)(2,1)}, u32[]{:S(2)}) copy-start(bf16[32,512]{1,0:T(8,128)(2,1)} %refs_2_.1) | copy-start | bytes 98308
  59.6 16.6 %collective-permute-start.9 = (bf16[1024,256]{1,0:T(8,128)(2,1)}, bf16[1024,256]{1,0:T(8,128)(2,1)}, u32[]{:S(2)}, u32[]{:S(2)}) collective-permute-start(bf16[1024,256]{1,0:T(8,128)(2,1)} %slice.8), channel_id=1, source_target_pairs={{0,2},{1,3},{2,0},{3,1},{4,6},{5,7},{6,4},{7,5},{8,10},{9,11},{10,... | collective-permute-start | bytes 1572872 | tf_op jit(solution)/shard_map/ppermute | solution.py:417
  60.1 37.0 %collective-permute-start.6 = (bf16[2048,256]{1,0:T(8,128)(2,1)S(1)}, bf16[2048,256]{1,0:T(8,128)(2,1)}, u32[]{:S(2)}, u32[]{:S(2)}) collective-permute-start(bf16[2048,256]{1,0:T(8,128)(2,1)S(1)} %collective-permute-done.5.refs_2_), channel_id=1, source_target_pairs={{0,1},{1,0},{2,3},{3,2},{4,5},{5,4},{6,7},{7,6},{8,9},{9,8},{10,11... | collective-permute-start | bytes 3145736 | tf_op jit(solution)/shard_map/ppermute | solution.py:417
  60.1 37.0 %collective-permute-start.8 = (bf16[2048,256]{1,0:T(8,128)(2,1)S(1)}, bf16[2048,256]{1,0:T(8,128)(2,1)}, u32[]{:S(2)}, u32[]{:S(2)}) collective-permute-start(bf16[2048,256]{1,0:T(8,128)(2,1)S(1)} %collective-permute-done.7.refs_4_), channel_id=1, source_target_pairs={{0,1},{1,0},{2,3},{3,2},{4,5},{5,4},{6,7},{7,6},{8,9},{9,8},{10,11... | collective-permute-start | bytes 3145736 | tf_op jit(solution)/shard_map/ppermute | solution.py:417
  72.3 12.8 %all-to-all-start.3 = ((bf16[8,208,128]{2,1,0:T(8,128)(2,1)}), bf16[8,208,128]{2,1,0:T(8,128)(2,1)S(1)}, u32[]{:S(2)}, u32[]{:S(2)}) async-start(bf16[8,208,128]{2,1,0:T(8,128)(2,1)} %attend.3), calls=%async_computation.3 | async-start | bytes 851968 | tf_op jit(solution)/shard_map/all_to_all | solution.py:348
  75.8 21.3 %collective-permute-start.12 = (bf16[1024,256]{1,0:T(8,128)(2,1)}, bf16[1024,256]{1,0:T(8,128)(2,1)}, u32[]{:S(2)}, u32[]{:S(2)}) collective-permute-start(bf16[1024,256]{1,0:T(8,128)(2,1)} %collective-permute-done.11.refs_8_), channel_id=1, source_target_pairs={{0,1},{1,0},{2,3},{3,2},{4,5},{5,4},{6,7},{7,6},{8,9},{9,8},{10,11... | collective-permute-start | bytes 1572872 | tf_op jit(solution)/shard_map/ppermute | solution.py:417
  76.2 20.9 %collective-permute-start.10 = (bf16[1024,256]{1,0:T(8,128)(2,1)}, bf16[1024,256]{1,0:T(8,128)(2,1)}, u32[]{:S(2)}, u32[]{:S(2)}) collective-permute-start(bf16[1024,256]{1,0:T(8,128)(2,1)} %collective-permute-done.9.refs_6_), channel_id=1, source_target_pairs={{0,1},{1,0},{2,3},{3,2},{4,5},{5,4},{6,7},{7,6},{8,9},{9,8},{10,11... | collective-permute-start | bytes 1572872 | tf_op jit(solution)/shard_map/ppermute | solution.py:417
  78.8 18.3 %copy-start.1 = (bf16[528,128]{1,0:T(8,128)(2,1)}, bf16[528,128]{1,0:T(8,128)(2,1)S(1)}, u32[]{:S(2)}) copy-start(bf16[528,128]{1,0:T(8,128)(2,1)S(1)} %merge.2.own_a) | copy-start | bytes 405508
  78.8 9.7 %collective-permute-start.3 = (bf16[528,128]{1,0:T(8,128)(2,1)S(1)}, bf16[528,128]{1,0:T(8,128)(2,1)S(1)}, u32[]{:S(2)}, u32[]{:S(2)}) collective-permute-start(bf16[528,128]{1,0:T(8,128)(2,1)S(1)} %merge.2.own_a), channel_id=1, source_target_pairs={{0,8},{1,9},{2,10},{3,11},{4,12},{5,13},{6,14},{7,15},{8,0},{9,1},... | collective-permute-start | bytes 405512 | tf_op jit(solution)/shard_map/ppermute | solution.py:334
  86.8 10.4 %copy-start = (bf16[528,128]{1,0:T(8,128)(2,1)}, bf16[528,128]{1,0:T(8,128)(2,1)S(1)}, u32[]{:S(2)}) copy-start(bf16[528,128]{1,0:T(8,128)(2,1)S(1)} %merge.3.other_b) | copy-start | bytes 405508
  88.5 8.6 %copy-start.10 = (bf16[528,128]{1,0:T(8,128)(2,1)}, bf16[528,128]{1,0:T(8,128)(2,1)S(1)}, u32[]{:S(2)}) copy-start(bf16[528,128]{1,0:T(8,128)(2,1)S(1)} %collective-permute-done.3.other_a) | copy-start | bytes 405508
  88.6 8.5 %collective-permute-start.2 = (bf16[528,128]{1,0:T(8,128)(2,1)S(1)}, bf16[528,128]{1,0:T(8,128)(2,1)S(1)}, u32[]{:S(2)}, u32[]{:S(2)}) collective-permute-start(bf16[528,128]{1,0:T(8,128)(2,1)S(1)} %merge.3.other_b), channel_id=1, source_target_pairs={{0,8},{1,9},{2,10},{3,11},{4,12},{5,13},{6,14},{7,15},{8,0},{9,1},... | collective-permute-start | bytes 405512 | tf_op jit(solution)/shard_map/ppermute | solution.py:334
  97.1 0.7 copy-start.11
  104.3 8.2 %collective-permute-start.13 = (bf16[32,2048]{1,0:T(8,128)(2,1)}, bf16[32,2048]{1,0:T(8,128)(2,1)S(1)}, u32[]{:S(2)}, u32[]{:S(2)}) collective-permute-start(bf16[32,2048]{1,0:T(8,128)(2,1)} %get-tuple-element.8), channel_id=1, source_target_pairs={{0,8},{1,9},{2,10},{3,11},{4,12},{5,13},{6,14},{7,15},{8,0},{9,1},... | collective-permute-start | bytes 393224 | tf_op jit(solution)/shard_map/ppermute | solution.py:334

commit v3 on v2

--- a/solution.py
+++ b/solution.py
@@ -18,6 +18,7 @@
 STAT_ROWS = KVH * PARTS
 SCALE2 = math.log2(math.e) / math.sqrt(HD)
 CHUNK = 512
+AHEAD = 3
 FLOOR = -(2.0**100)
 
 
@@ -283,11 +284,16 @@
     width = weights[0].shape[1]
     copies = {k: [] for k in range(count)}
     for i, (k, start) in enumerate(places):
-        copy = pltpu.make_async_copy(
-            weights[i], held.at[k, start : start + weights[i].shape[0], :], sems.at[i]
-        )
-        copy.start()
-        copies[k].append(copy)
+        copies[k].append(
+            pltpu.make_async_copy(
+                weights[i], held.at[k, start : start + weights[i].shape[0], :], sems.at[i]
+            )
+        )
+    order = [copies[k] for k in range(count)]
+    ahead = min(AHEAD, count)
+    for group in order[:ahead]:
+        for copy in group:
+            copy.start()
     tall = (own_a.shape[0] - STAT_ROWS) // KVH
     rows = tall // GROUP
     left = jnp.concatenate(
@@ -296,15 +302,25 @@
     for k in range(count):
         for copy in copies[k]:
             copy.wait()
+        if k + ahead < count:
+            for copy in order[k + ahead]:
+                copy.start()
         made = jnp.dot(left, held[k], preferred_element_type=jnp.float32).astype(jnp.bfloat16)
         at = pl.ds(pl.multiple_of((me[0] ^ k) * width, width), width)
         own_out[:, at] = made[:rows, :]
         other_out[:, at] = made[rows:, :]
 
 
+def place_kernel(first, own, received, out):
+    width = own.shape[1]
+    out[:, pl.ds(pl.multiple_of(first[0] * width, width), width)] = own[...]
+    out[:, pl.ds(pl.multiple_of((1 - first[0]) * width, width), width)] = received[...]
+
+
 VMEM = pl.BlockSpec(memory_space=pltpu.VMEM)
 SMEM = pl.BlockSpec(memory_space=pltpu.SMEM)
 ANY = pl.BlockSpec(memory_space=pl.ANY)
+LARGE = pltpu.CompilerParams(vmem_limit_bytes=60 << 20)
 SMALL = pltpu.CompilerParams(vmem_limit_bytes=16 << 20)
 
 
@@ -313,6 +329,10 @@
         pltpu.SMEM((members * capacity,), jnp.int32),
         pltpu.SMEM((members,), jnp.int32),
     ]
+
+
+def early_first(step):
+    return (1, 0) if step == 2 else (0, 1)
 
 
 def shards(queries, new_keys, new_values, keys, values, page_list, out_weight):
@@ -333,14 +353,14 @@
     def mirrored(array):
         return lax.ppermute(array, "seq", [(i, (i + half) % members) for i in range(members)])
 
-    def pack(tiles, listed):
+    def pack(tiles, listed, params):
         return pl.pallas_call(
             functools.partial(pack_kernel, half, capacity),
             out_shape=jax.ShapeDtypeStruct((half, KVH * block, HD), jnp.bfloat16),
             in_specs=[SMEM, SMEM, VMEM],
             out_specs=VMEM,
             scratch_shapes=slot_scratch(half, capacity),
-            compiler_params=SMALL,
+            compiler_params=params,
             name="pack",
         )(base, listed, tiles)
 
@@ -385,9 +405,9 @@
 
     other_queries = mirrored(queries)
     other_list = mirrored(page_list)
-    packed_near = pack(queries, page_list)
+    packed_near = pack(queries, page_list, LARGE)
     near = spread(packed_near)
-    packed_far = pack(other_queries, other_list)
+    packed_far = pack(other_queries, other_list, SMALL)
     far = spread(packed_far)
     near_partial = attend(near)
     near_back = spread(near_partial)
@@ -417,30 +437,24 @@
         return lax.ppermute(array, "seq", [(i, i ^ step) for i in range(members)])
 
     middle = features // 2
-
-    def upper(pieces):
-        return pieces[0] if len(pieces) > 1 else pieces[0][:middle, :]
-
-    def lower(pieces):
-        return pieces[1] if len(pieces) > 1 else pieces[0][middle:, :]
-
-    same_core = {0: [out_weight]}
+    halves_of = [out_weight[:middle, :], out_weight[middle:, :]]
+    pieces = {0: [out_weight]}
     for step in range(2, half, 2):
         low = step & -step
         if low == step:
-            same_core[step] = [exchanged(out_weight, step)]
+            pieces[step] = [None, None]
+            for i in early_first(step):
+                pieces[step][i] = exchanged(halves_of[i], step)
     for step in range(2, half, 2):
         low = step & -step
         if low != step:
-            same_core[step] = [
-                exchanged(upper(same_core[step ^ low]), low),
-                exchanged(lower(same_core[low]), step ^ low),
-            ]
+            first_piece = exchanged(pieces[step ^ low][0], low)
+            pieces[step] = [first_piece, exchanged(pieces[low][1], step ^ low)]
     gathered = []
     places = []
-    for step, pieces in same_core.items():
-        for i, piece in enumerate(pieces):
-            gathered += [piece, exchanged(piece, 1)]
+    for step, parts in pieces.items():
+        for i, part in enumerate(parts):
+            gathered += [part, exchanged(part, 1)]
             places += [(step, i * middle), (step + 1, i * middle)]
     own_out, other_out = pl.pallas_call(
         functools.partial(project_kernel, half, tuple(places)),
@@ -451,14 +465,18 @@
             pltpu.VMEM((half, features, width), jnp.bfloat16),
             pltpu.SemaphoreType.DMA((len(places),)),
         ],
-        compiler_params=pltpu.CompilerParams(vmem_limit_bytes=60 << 20),
+        compiler_params=LARGE,
         name="project",
     )(own_a, own_b, other_a, other_b, (me % half).reshape(1), *gathered)
     received = mirrored(other_out)
-    first = me < half
-    return jnp.concatenate(
-        [jnp.where(first, own_out, received), jnp.where(first, received, own_out)], axis=1
-    )
+    return pl.pallas_call(
+        place_kernel,
+        out_shape=jax.ShapeDtypeStruct((row_total, members * width), jnp.bfloat16),
+        in_specs=[SMEM, VMEM, VMEM],
+        out_specs=VMEM,
+        compiler_params=SMALL,
+        name="place",
+    )((me // half).reshape(1), own_out, received)
 
 
 def solution(mesh):

time: 115 us -> 111 us (0.965)
  waiting for transfers between devices: 40.2 us -> 31.6 us
  starting transfers between devices: 30.3 us -> 34.4 us
  local copies, waits for them, and re-layouts: 4.1 us -> 5.82 us
  other arithmetic: 1.65 us -> 0 us
  Pallas kernels: 37.6 us -> 38.9 us
    ppermute x9 -> x13, waiting for transfers between devices: 11.5 us -> 6.36 us  [exchanged(): return lax.ppermute(array, 'seq', [(i, i ^ step) for i in range(members)])]
    all_to_all x4, waiting for transfers between devices: 4.89 us -> 1.98 us  [spread(): lax.all_to_all(array, 'seq', split_axis=0, concat_axis=0, tiled=True, axi...]
    ppermute x9 -> x13, starting transfers between devices: 6.95 us -> 8.98 us  [exchanged(): return lax.ppermute(array, 'seq', [(i, i ^ step) for i in range(members)])]
    unnamed x25 -> x31, local copies, waits for them, and re-layouts: 2.3 us -> 3.77 us
    ppermute x5, starting transfers between devices: 4.39 us -> 5.72 us  [mirrored(): lax.ppermute(array, 'seq', [(i, (i + half) % members) for i in range(memb...]
  transfers between devices with their start and end apart: 18 -> 22, of which waited for: 6 -> 6; matrix products, arithmetic and copies ran while one was open for 2% -> 2% of each run, Pallas kernels for 26% -> 26%
where the time goes in v3:
time: 111 us
  Pallas kernels  38.9 us (35%)
  starting transfers between devices  34.4 us (31%)
  waiting for transfers between devices  31.6 us (28%)
  local copies, waits for them, and re-layouts  5.82 us (5%)
    ppermute x5, waiting for transfers between devices, mirrored(): lax.ppermute(array, 'seq', [(i, (i + half) % members) for i in range(memb...  23.2 us
    pallas_call x2, Pallas kernels, attend(): pl.pallas_call(attend_kernel, out_shape=jax.ShapeDtypeStruct((half, KVH *...  23.2 us
    all_to_all x4, starting transfers between devices, spread(): lax.all_to_all(array, 'seq', split_axis=0, concat_axis=0, tiled=True, axi...  19.7 us
    ppermute x13, starting transfers between devices, exchanged(): return lax.ppermute(array, 'seq', [(i, i ^ step) for i in range(members)])  8.98 us
    pallas_call x1, Pallas kernels, shards(): pl.pallas_call(functools.partial(project_kernel, half, tuple(places)), ou...  6.72 us
    ppermute x13, waiting for transfers between devices, exchanged(): return lax.ppermute(array, 'seq', [(i, i ^ step) for i in range(members)])  6.36 us
    ppermute x5, starting transfers between devices, mirrored(): lax.ppermute(array, 'seq', [(i, (i + half) % members) for i in range(memb...  5.72 us
    pallas_call x2, Pallas kernels, pack(): pl.pallas_call(functools.partial(pack_kernel, half, capacity), out_shape=...  4.14 us
  transfers between devices with their start and end apart: 22, of which 6 were waited for; matrix products, arithmetic and copies ran while one was open for 2% of the time, Pallas kernels for 26%

profile of v3, /device:TPU:0, one launch (start us, length us, event | category | flops | bytes accessed | tf_op | source)
XLA Modules:
  0.0 110.8 jit_solution(13120352130228242589)
XLA Ops:
  0.0 1.3 %copy.9.page_list = s32[8,3]{1,0:T(8,128)} copy(s32[8,3]{0,1:T(4,128)} %param.12) | data formatting | bytes 192 | tf_op args[5]
  1.3 2.2 %pack.2 = bf16[8,192,128]{2,1,0:T(8,128)(2,1)} custom-call(s32[1]{0:T(128)} %bitcast.1.base, s32[8,3]{1,0:T(8,128)} %copy.9.page_list, bf16[32,2048]{1,0:T(8,128)(2,1)} %refs_0_.2), custom_call_target="tpu_custom_call" | custom-call | tf_op jit(solution)/shard_map/pack/pallas_call | solution.py:357
  3.6 5.3 %all-to-all-start = ((bf16[8,192,128]{2,1,0:T(8,128)(2,1)}), bf16[8,192,128]{2,1,0:T(8,128)(2,1)S(1)}, u32[]{:S(2)}, u32[]{:S(2)}) async-start(bf16[8,192,128]{2,1,0:T(8,128)(2,1)} %pack.2), calls=%async_computation | async-start | bytes 786432 | tf_op jit(solution)/shard_map/all_to_all | solution.py:368
  8.9 2.6 %collective-permute-start.1 = (bf16[32,2048]{1,0:T(8,128)(2,1)}, bf16[32,2048]{1,0:T(8,128)(2,1)S(1)}, u32[]{:S(2)}, u32[]{:S(2)}) collective-permute-start(bf16[32,2048]{1,0:T(8,128)(2,1)} %refs_0_.2), channel_id=1, source_target_pairs={{0,8},{1,9},{2,10},{3,11},{4,12},{5,13},{6,14},{7,15},{8,0},{9,1},... | collective-permute-start | bytes 393224 | tf_op jit(solution)/shard_map/ppermute | solution.py:354
  11.8 5.4 %collective-permute-done.page_list = s32[8,3]{1,0:T(8,128)S(1)} collective-permute-done((s32[8,3]{1,0:T(8,128)}, s32[8,3]{1,0:T(8,128)S(1)}, u32[]{:S(2)}, u32[]{:S(2)}) %collective-permute-start) | collective-permute-done | bytes 128 | tf_op jit(solution)/shard_map/ppermute | solution.py:354
  17.2 1.9 %pack.3 = bf16[8,192,128]{2,1,0:T(8,128)(2,1)} custom-call(s32[1]{0:T(128)} %bitcast.1.base, s32[8,3]{1,0:T(8,128)S(1)} %collective-permute-done.page_list, bf16[32,2048]{1,0:T(8,128)(2,1)S(1)} %collective-permute-done.1.queries), custom_call_target="tpu_custom_call" | custom-call | tf_op jit(solution)/shard_map/pack/pallas_call | solution.py:357
  19.2 6.7 %all-to-all-start.2 = ((bf16[8,192,128]{2,1,0:T(8,128)(2,1)}), bf16[8,192,128]{2,1,0:T(8,128)(2,1)S(1)}, u32[]{:S(2)}, u32[]{:S(2)}) async-start(bf16[8,192,128]{2,1,0:T(8,128)(2,1)} %pack.3), calls=%async_computation.2 | async-start | bytes 786432 | tf_op jit(solution)/shard_map/all_to_all | solution.py:368
  25.9 2.0 %fusion = (bf16[1024,256]{1,0:T(8,128)(2,1)S(1)}, bf16[1024,256]{1,0:T(8,128)(2,1)}) fusion(bf16[2048,256]{1,0:T(8,128)(2,1)} %refs_0_.3), kind=kLoop, calls=%fused_computation | loop fusion | bytes 2097152 | tf_op jit(solution)/shard_map/slice | solution.py:440
  27.9 2.0 %collective-permute-start.11 = (bf16[1024,256]{1,0:T(8,128)(2,1)S(1)}, bf16[1024,256]{1,0:T(8,128)(2,1)}, u32[]{:S(2)}, u32[]{:S(2)}) collective-permute-start(bf16[1024,256]{1,0:T(8,128)(2,1)S(1)} %get-tuple-element.9), channel_id=1, source_target_pairs={{0,4},{1,5},{2,6},{3,7},{4,0},{5,1},{6,2},{7,3},{8,12},{9,13},{10,... | collective-permute-start | bytes 1572872 | tf_op jit(solution)/shard_map/ppermute | solution.py:437
  30.0 1.5 %collective-permute-start.7 = (bf16[1024,256]{1,0:T(8,128)(2,1)S(1)}, bf16[1024,256]{1,0:T(8,128)(2,1)}, u32[]{:S(2)}, u32[]{:S(2)}) collective-permute-start(bf16[1024,256]{1,0:T(8,128)(2,1)S(1)} %get-tuple-element.9), channel_id=1, source_target_pairs={{0,2},{1,3},{2,0},{3,1},{4,6},{5,7},{6,4},{7,5},{8,10},{9,11},{10,... | collective-permute-start | bytes 1572872 | tf_op jit(solution)/shard_map/ppermute | solution.py:437
  31.4 0.6 collective-permute-start.9
  32.0 11.6 %attend.2 = bf16[8,208,128]{2,1,0:T(8,128)(2,1)} custom-call(bf16[8,192,128]{2,1,0:T(8,128)(2,1)} %copy-done.12, bf16[4096,512]{1,0:T(8,128)(2,1)} %keys.3, bf16[4096,512]{1,0:T(8,128)(2,1)} %values.3), custom_call_target="tpu_custom_call" | custom-call | flops 3221225472 | bytes 8388608 | tf_op jit(solution)/shard_map/attend/pallas_call | solution.py:373
  43.6 4.2 %all-to-all-start.1 = ((bf16[8,208,128]{2,1,0:T(8,128)(2,1)}), bf16[8,208,128]{2,1,0:T(8,128)(2,1)S(1)}, u32[]{:S(2)}, u32[]{:S(2)}) async-start(bf16[8,208,128]{2,1,0:T(8,128)(2,1)} %attend.2), calls=%async_computation.1 | async-start | bytes 851968 | tf_op jit(solution)/shard_map/all_to_all | solution.py:368
  47.9 0.6 collective-permute-start.12
  48.4 1.6 %collective-permute-start.15 = (bf16[1024,256]{1,0:T(8,128)(2,1)}, bf16[1024,256]{1,0:T(8,128)(2,1)}, u32[]{:S(2)}, u32[]{:S(2)}) collective-permute-start(bf16[1024,256]{1,0:T(8,128)(2,1)} %collective-permute-done.7.refs_4_), channel_id=1, source_target_pairs={{0,4},{1,5},{2,6},{3,7},{4,0},{5,1},{6,2},{7,3},{8,12},{9,13},{10,... | collective-permute-start | bytes 1572872 | tf_op jit(solution)/shard_map/ppermute | solution.py:437
  50.2 6.3 %collective-permute-done.9.refs_6_ = bf16[1024,256]{1,0:T(8,128)(2,1)} collective-permute-done((bf16[1024,256]{1,0:T(8,128)(2,1)}, bf16[1024,256]{1,0:T(8,128)(2,1)}, u32[]{:S(2)}, u32[]{:S(2)}) %collective-permute-start.9) | collective-permute-done | bytes 524320 | tf_op jit(solution)/shard_map/ppermute | solution.py:437
  56.5 1.5 %collective-permute-start.13 = (bf16[1024,256]{1,0:T(8,128)(2,1)}, bf16[1024,256]{1,0:T(8,128)(2,1)}, u32[]{:S(2)}, u32[]{:S(2)}) collective-permute-start(bf16[1024,256]{1,0:T(8,128)(2,1)} %collective-permute-done.9.refs_6_), channel_id=1, source_target_pairs={{0,2},{1,3},{2,0},{3,1},{4,6},{5,7},{6,4},{7,5},{8,10},{9,11},{10,... | collective-permute-start | bytes 1572872 | tf_op jit(solution)/shard_map/ppermute | solution.py:437
  58.0 11.6 %attend.3 = bf16[8,208,128]{2,1,0:T(8,128)(2,1)} custom-call(bf16[8,192,128]{2,1,0:T(8,128)(2,1)} %copy-done.11, bf16[4096,512]{1,0:T(8,128)(2,1)} %keys.3, bf16[4096,512]{1,0:T(8,128)(2,1)} %values.3), custom_call_target="tpu_custom_call" | custom-call | flops 3221225472 | bytes 8388608 | tf_op jit(solution)/shard_map/attend/pallas_call | solution.py:373
  69.6 3.5 %all-to-all-start.3 = ((bf16[8,208,128]{2,1,0:T(8,128)(2,1)}), bf16[8,208,128]{2,1,0:T(8,128)(2,1)S(1)}, u32[]{:S(2)}, u32[]{:S(2)}) async-start(bf16[8,208,128]{2,1,0:T(8,128)(2,1)} %attend.3), calls=%async_computation.3 | async-start | bytes 851968 | tf_op jit(solution)/shard_map/all_to_all | solution.py:368
  74.2 2.4 %merge.2.own_a = bf16[528,128]{1,0:T(8,128)(2,1)S(1)} custom-call(s32[1]{0:T(128)} %bitcast.1.base, s32[8,3]{1,0:T(8,128)S(1)} %copy-done.4, bf16[32,2048]{1,0:T(8,128)(2,1)S(1)} %copy-done.2, bf16[32,512]{1,0:T(8,128)(2,1)S(1)} %copy-done.5, bf16[32,512]{1,0:T(8,128)(2,1)S(1)} %copy-done.6, bf16[8,208,128]{2,1,0:T(8,128)(2,1)S(1)} %all-to-all-done.1.refs_3_), custom_call_target="tpu_custom_call" | custom-call | tf_op jit(solution)/shard_map/merge/pallas_call | solution.py:396
  76.7 0.8 copy-done.10
  77.5 1.3 %collective-permute-start.3 = (bf16[528,128]{1,0:T(8,128)(2,1)S(1)}, bf16[528,128]{1,0:T(8,128)(2,1)S(1)}, u32[]{:S(2)}, u32[]{:S(2)}) collective-permute-start(bf16[528,128]{1,0:T(8,128)(2,1)S(1)} %merge.2.own_a), channel_id=1, source_target_pairs={{0,8},{1,9},{2,10},{3,11},{4,12},{5,13},{6,14},{7,15},{8,0},{9,1},... | collective-permute-start | bytes 405512 | tf_op jit(solution)/shard_map/ppermute | solution.py:354
  78.9 2.0 %all-to-all-done.3.refs_0_ = bf16[8,208,128]{2,1,0:T(8,128)(2,1)S(1)} async-done(((bf16[8,208,128]{2,1,0:T(8,128)(2,1)}), bf16[8,208,128]{2,1,0:T(8,128)(2,1)S(1)}, u32[]{:S(2)}, u32[]{:S(2)}) %all-to-all-start.3) | async-done | bytes 426016 | tf_op jit(solution)/shard_map/all_to_all | solution.py:368
  80.8 1.7 %merge.3.other_b = bf16[528,128]{1,0:T(8,128)(2,1)S(1)} custom-call(s32[1]{0:T(128)} %bitcast.1.base, s32[8,3]{1,0:T(8,128)S(1)} %collective-permute-done.page_list, bf16[8,208,128]{2,1,0:T(8,128)(2,1)S(1)} %all-to-all-done.3.refs_0_), custom_call_target="tpu_custom_call" | custom-call | tf_op jit(solution)/shard_map/merge/pallas_call | solution.py:396
  82.5 1.4 %collective-permute-start.2 = (bf16[528,128]{1,0:T(8,128)(2,1)S(1)}, bf16[528,128]{1,0:T(8,128)(2,1)S(1)}, u32[]{:S(2)}, u32[]{:S(2)}) collective-permute-start(bf16[528,128]{1,0:T(8,128)(2,1)S(1)} %merge.3.other_b), channel_id=1, source_target_pairs={{0,8},{1,9},{2,10},{3,11},{4,12},{5,13},{6,14},{7,15},{8,0},{9,1},... | collective-permute-start | bytes 405512 | tf_op jit(solution)/shard_map/ppermute | solution.py:354
  83.9 6.8 %collective-permute-done.3.other_a = bf16[528,128]{1,0:T(8,128)(2,1)S(1)} collective-permute-done((bf16[528,128]{1,0:T(8,128)(2,1)S(1)}, bf16[528,128]{1,0:T(8,128)(2,1)S(1)}, u32[]{:S(2)}, u32[]{:S(2)}) %collective-permute-start.3) | collective-permute-done | bytes 135200 | tf_op jit(solution)/shard_map/ppermute | solution.py:354
  90.7 2.2 %collective-permute-done.2.own_b = bf16[528,128]{1,0:T(8,128)(2,1)S(1)} collective-permute-done((bf16[528,128]{1,0:T(8,128)(2,1)S(1)}, bf16[528,128]{1,0:T(8,128)(2,1)S(1)}, u32[]{:S(2)}, u32[]{:S(2)}) %collective-permute-start.2) | collective-permute-done | bytes 135200 | tf_op jit(solution)/shard_map/ppermute | solution.py:354
  93.0 0.6 copy-done.14
  93.6 6.7 %project.1 = (bf16[32,2048]{1,0:T(8,128)(2,1)}, bf16[32,2048]{1,0:T(8,128)(2,1)}) custom-call(bf16[528,128]{1,0:T(8,128)(2,1)} %copy-done.1, bf16[528,128]{1,0:T(8,128)(2,1)} %copy-done.14, bf16[528,128]{1,0:T(8,128)(2,1)} %copy-done.13, bf16[528,128]{1,0:T(8,128)(2,1)} %copy-done, s32[1]{0:T(128)} %bitcast.2.me, bf16[2048,256]{1,0:T(8,128)(2,1)} %refs_0_.3, ...), custom_call_target="tpu_custom_call" | custom-call | tf_op jit(solution)/shard_map/project/pallas_call | solution.py:459
  100.4 8.8 %collective-permute-done.17.received = bf16[32,2048]{1,0:T(8,128)(2,1)S(1)} collective-permute-done((bf16[32,2048]{1,0:T(8,128)(2,1)}, bf16[32,2048]{1,0:T(8,128)(2,1)S(1)}, u32[]{:S(2)}, u32[]{:S(2)}) %collective-permute-start.17) | collective-permute-done | bytes 131104 | tf_op jit(solution)/shard_map/ppermute | solution.py:354
  109.2 0.9 copy-done.3
  110.1 0.7 place.1
  (52 shorter events, 1.7 us)
Async XLA Ops:
  3.6 15.6 %all-to-all-start = ((bf16[8,192,128]{2,1,0:T(8,128)(2,1)}), bf16[8,192,128]{2,1,0:T(8,128)(2,1)S(1)}, u32[]{:S(2)}, u32[]{:S(2)}) async-start(bf16[8,192,128]{2,1,0:T(8,128)(2,1)} %pack.2), calls=%async_computation | async-start | bytes 786432 | tf_op jit(solution)/shard_map/all_to_all | solution.py:368
  8.9 8.4 %collective-permute-start.1 = (bf16[32,2048]{1,0:T(8,128)(2,1)}, bf16[32,2048]{1,0:T(8,128)(2,1)S(1)}, u32[]{:S(2)}, u32[]{:S(2)}) collective-permute-start(bf16[32,2048]{1,0:T(8,128)(2,1)} %refs_0_.2), channel_id=1, source_target_pairs={{0,8},{1,9},{2,10},{3,11},{4,12},{5,13},{6,14},{7,15},{8,0},{9,1},... | collective-permute-start | bytes 393224 | tf_op jit(solution)/shard_map/ppermute | solution.py:354
  11.4 5.8 %collective-permute-start = (s32[8,3]{1,0:T(8,128)}, s32[8,3]{1,0:T(8,128)S(1)}, u32[]{:S(2)}, u32[]{:S(2)}) collective-permute-start(s32[8,3]{1,0:T(8,128)} %copy.9.page_list), channel_id=1, source_target_pairs={{0,8},{1,9},{2,10},{3,11},{4,12},{5,13},{6,14},{7,15},{8,0},{9,1},... | collective-permute-start | bytes 296 | tf_op jit(solution)/shard_map/ppermute | solution.py:354
  19.2 12.8 %copy-start.12 = (bf16[8,192,128]{2,1,0:T(8,128)(2,1)}, bf16[8,192,128]{2,1,0:T(8,128)(2,1)S(1)}, u32[]{:S(2)}) copy-start(bf16[8,192,128]{2,1,0:T(8,128)(2,1)S(1)} %all-to-all-done.queries) | copy-start | bytes 1179652
  19.2 24.4 %all-to-all-start.2 = ((bf16[8,192,128]{2,1,0:T(8,128)(2,1)}), bf16[8,192,128]{2,1,0:T(8,128)(2,1)S(1)}, u32[]{:S(2)}, u32[]{:S(2)}) async-start(bf16[8,192,128]{2,1,0:T(8,128)(2,1)} %pack.3), calls=%async_computation.2 | async-start | bytes 786432 | tf_op jit(solution)/shard_map/all_to_all | solution.py:368
  27.9 19.9 %collective-permute-start.11 = (bf16[1024,256]{1,0:T(8,128)(2,1)S(1)}, bf16[1024,256]{1,0:T(8,128)(2,1)}, u32[]{:S(2)}, u32[]{:S(2)}) collective-permute-start(bf16[1024,256]{1,0:T(8,128)(2,1)S(1)} %get-tuple-element.9), channel_id=1, source_target_pairs={{0,4},{1,5},{2,6},{3,7},{4,0},{5,1},{6,2},{7,3},{8,12},{9,13},{10,... | collective-permute-start | bytes 1572872 | tf_op jit(solution)/shard_map/ppermute | solution.py:437
  30.0 18.4 %collective-permute-start.7 = (bf16[1024,256]{1,0:T(8,128)(2,1)S(1)}, bf16[1024,256]{1,0:T(8,128)(2,1)}, u32[]{:S(2)}, u32[]{:S(2)}) collective-permute-start(bf16[1024,256]{1,0:T(8,128)(2,1)S(1)} %get-tuple-element.9), channel_id=1, source_target_pairs={{0,2},{1,3},{2,0},{3,1},{4,6},{5,7},{6,4},{7,5},{8,10},{9,11},{10,... | collective-permute-start | bytes 1572872 | tf_op jit(solution)/shard_map/ppermute | solution.py:437
  31.4 18.6 %copy-start.7 = (bf16[2048,256]{1,0:T(8,128)(2,1)S(1)}, bf16[2048,256]{1,0:T(8,128)(2,1)}, u32[]{:S(2)}) copy-start(bf16[2048,256]{1,0:T(8,128)(2,1)} %refs_0_.3) | copy-start | bytes 3145732
  31.4 25.1 %collective-permute-start.9 = (bf16[1024,256]{1,0:T(8,128)(2,1)}, bf16[1024,256]{1,0:T(8,128)(2,1)}, u32[]{:S(2)}, u32[]{:S(2)}) collective-permute-start(bf16[1024,256]{1,0:T(8,128)(2,1)} %get-tuple-element.10), channel_id=1, source_target_pairs={{0,4},{1,5},{2,6},{3,7},{4,0},{5,1},{6,2},{7,3},{8,12},{9,13},{10,... | collective-permute-start | bytes 1572872 | tf_op jit(solution)/shard_map/ppermute | solution.py:437
  32.0 24.5 %collective-permute-start.5 = (bf16[1024,256]{1,0:T(8,128)(2,1)}, bf16[1024,256]{1,0:T(8,128)(2,1)S(1)}, u32[]{:S(2)}, u32[]{:S(2)}) collective-permute-start(bf16[1024,256]{1,0:T(8,128)(2,1)} %get-tuple-element.10), channel_id=1, source_target_pairs={{0,2},{1,3},{2,0},{3,1},{4,6},{5,7},{6,4},{7,5},{8,10},{9,11},{10,... | collective-permute-start | bytes 1572872 | tf_op jit(solution)/shard_map/ppermute | solution.py:437
  43.6 26.0 %all-to-all-start.1 = ((bf16[8,208,128]{2,1,0:T(8,128)(2,1)}), bf16[8,208,128]{2,1,0:T(8,128)(2,1)S(1)}, u32[]{:S(2)}, u32[]{:S(2)}) async-start(bf16[8,208,128]{2,1,0:T(8,128)(2,1)} %attend.2), calls=%async_computation.1 | async-start | bytes 851968 | tf_op jit(solution)/shard_map/all_to_all | solution.py:368
  47.8 26.4 %copy-start.2 = (bf16[32,2048]{1,0:T(8,128)(2,1)S(1)}, bf16[32,2048]{1,0:T(8,128)(2,1)}, u32[]{:S(2)}) copy-start(bf16[32,2048]{1,0:T(8,128)(2,1)} %refs_0_.2) | copy-start | bytes 393220
  47.8 26.4 %copy-start.4 = (s32[8,3]{1,0:T(8,128)S(1)}, s32[8,3]{1,0:T(8,128)}, u32[]{:S(2)}) copy-start(s32[8,3]{1,0:T(8,128)} %copy.9.page_list) | copy-start | bytes 292
  47.8 26.4 %copy-start.5 = (bf16[32,512]{1,0:T(8,128)(2,1)S(1)}, bf16[32,512]{1,0:T(8,128)(2,1)}, u32[]{:S(2)}) copy-start(bf16[32,512]{1,0:T(8,128)(2,1)} %refs_1_.1) | copy-start | bytes 98308
  47.8 26.4 %copy-start.6 = (bf16[32,512]{1,0:T(8,128)(2,1)S(1)}, bf16[32,512]{1,0:T(8,128)(2,1)}, u32[]{:S(2)}) copy-start(bf16[32,512]{1,0:T(8,128)(2,1)} %refs_2_.1) | copy-start | bytes 98308
  47.9 25.2 %collective-permute-start.12 = (bf16[1024,256]{1,0:T(8,128)(2,1)}, bf16[1024,256]{1,0:T(8,128)(2,1)}, u32[]{:S(2)}, u32[]{:S(2)}) collective-permute-start(bf16[1024,256]{1,0:T(8,128)(2,1)} %collective-permute-done.11.refs_8_), channel_id=1, source_target_pairs={{0,1},{1,0},{2,3},{3,2},{4,5},{5,4},{6,7},{7,6},{8,9},{9,8},{10,11... | collective-permute-start | bytes 1572872 | tf_op jit(solution)/shard_map/ppermute | solution.py:437
  48.4 25.1 %collective-permute-start.15 = (bf16[1024,256]{1,0:T(8,128)(2,1)}, bf16[1024,256]{1,0:T(8,128)(2,1)}, u32[]{:S(2)}, u32[]{:S(2)}) collective-permute-start(bf16[1024,256]{1,0:T(8,128)(2,1)} %collective-permute-done.7.refs_4_), channel_id=1, source_target_pairs={{0,4},{1,5},{2,6},{3,7},{4,0},{5,1},{6,2},{7,3},{8,12},{9,13},{10,... | collective-permute-start | bytes 1572872 | tf_op jit(solution)/shard_map/ppermute | solution.py:437
  50.0 33.9 %collective-permute-start.4 = (bf16[2048,256]{1,0:T(8,128)(2,1)S(1)}, bf16[2048,256]{1,0:T(8,128)(2,1)S(1)}, u32[]{:S(2)}, u32[]{:S(2)}) collective-permute-start(bf16[2048,256]{1,0:T(8,128)(2,1)S(1)} %copy-done.7), channel_id=1, source_target_pairs={{0,1},{1,0},{2,3},{3,2},{4,5},{5,4},{6,7},{7,6},{8,9},{9,8},{10,11... | collective-permute-start | bytes 3145736 | tf_op jit(solution)/shard_map/ppermute | solution.py:437
  56.5 17.2 %collective-permute-start.8 = (bf16[1024,256]{1,0:T(8,128)(2,1)}, bf16[1024,256]{1,0:T(8,128)(2,1)}, u32[]{:S(2)}, u32[]{:S(2)}) collective-permute-start(bf16[1024,256]{1,0:T(8,128)(2,1)} %collective-permute-done.7.refs_4_), channel_id=1, source_target_pairs={{0,1},{1,0},{2,3},{3,2},{4,5},{5,4},{6,7},{7,6},{8,9},{9,8},{10,11... | collective-permute-start | bytes 1572872 | tf_op jit(solution)/shard_map/ppermute | solution.py:437
  56.5 13.1 %copy-start.9 = (bf16[1024,256]{1,0:T(8,128)(2,1)}, bf16[1024,256]{1,0:T(8,128)(2,1)S(1)}, u32[]{:S(2)}) copy-start(bf16[1024,256]{1,0:T(8,128)(2,1)S(1)} %collective-permute-done.5.refs_2_) | copy-start | bytes 1572868
  56.5 17.5 %collective-permute-start.13 = (bf16[1024,256]{1,0:T(8,128)(2,1)}, bf16[1024,256]{1,0:T(8,128)(2,1)}, u32[]{:S(2)}, u32[]{:S(2)}) collective-permute-start(bf16[1024,256]{1,0:T(8,128)(2,1)} %collective-permute-done.9.refs_6_), channel_id=1, source_target_pairs={{0,2},{1,3},{2,0},{3,1},{4,6},{5,7},{6,4},{7,5},{8,10},{9,11},{10,... | collective-permute-start | bytes 1572872 | tf_op jit(solution)/shard_map/ppermute | solution.py:437
  69.6 11.2 %all-to-all-start.3 = ((bf16[8,208,128]{2,1,0:T(8,128)(2,1)}), bf16[8,208,128]{2,1,0:T(8,128)(2,1)S(1)}, u32[]{:S(2)}, u32[]{:S(2)}) async-start(bf16[8,208,128]{2,1,0:T(8,128)(2,1)} %attend.3), calls=%async_computation.3 | async-start | bytes 851968 | tf_op jit(solution)/shard_map/all_to_all | solution.py:368
  73.1 3.6 %collective-permute-start.10 = (bf16[1024,256]{1,0:T(8,128)(2,1)}, bf16[1024,256]{1,0:T(8,128)(2,1)S(1)}, u32[]{:S(2)}, u32[]{:S(2)}) collective-permute-start(bf16[1024,256]{1,0:T(8,128)(2,1)} %collective-permute-done.9.refs_6_), channel_id=1, source_target_pairs={{0,1},{1,0},{2,3},{3,2},{4,5},{5,4},{6,7},{7,6},{8,9},{9,8},{10,11... | collective-permute-start | bytes 1572872 | tf_op jit(solution)/shard_map/ppermute | solution.py:437
  73.5 9.0 %collective-permute-start.6 = (bf16[1024,256]{1,0:T(8,128)(2,1)}, bf16[1024,256]{1,0:T(8,128)(2,1)}, u32[]{:S(2)}, u32[]{:S(2)}) collective-permute-start(bf16[1024,256]{1,0:T(8,128)(2,1)} %copy-done.9), channel_id=1, source_target_pairs={{0,1},{1,0},{2,3},{3,2},{4,5},{5,4},{6,7},{7,6},{8,9},{9,8},{10,11... | collective-permute-start | bytes 1572872 | tf_op jit(solution)/shard_map/ppermute | solution.py:437
  73.7 17.0 %collective-permute-start.16 = (bf16[1024,256]{1,0:T(8,128)(2,1)}, bf16[1024,256]{1,0:T(8,128)(2,1)}, u32[]{:S(2)}, u32[]{:S(2)}) collective-permute-start(bf16[1024,256]{1,0:T(8,128)(2,1)} %collective-permute-done.15.refs_12_), channel_id=1, source_target_pairs={{0,1},{1,0},{2,3},{3,2},{4,5},{5,4},{6,7},{7,6},{8,9},{9,8},{10,11... | collective-permute-start | bytes 1572872 | tf_op jit(solution)/shard_map/ppermute | solution.py:437
  74.0 16.7 %collective-permute-start.14 = (bf16[1024,256]{1,0:T(8,128)(2,1)}, bf16[1024,256]{1,0:T(8,128)(2,1)}, u32[]{:S(2)}, u32[]{:S(2)}) collective-permute-start(bf16[1024,256]{1,0:T(8,128)(2,1)} %collective-permute-done.13.refs_10_), channel_id=1, source_target_pairs={{0,1},{1,0},{2,3},{3,2},{4,5},{5,4},{6,7},{7,6},{8,9},{9,8},{10,11... | collective-permute-start | bytes 1572872 | tf_op jit(solution)/shard_map/ppermute | solution.py:437
  76.7 16.3 %copy-start.1 = (bf16[528,128]{1,0:T(8,128)(2,1)}, bf16[528,128]{1,0:T(8,128)(2,1)S(1)}, u32[]{:S(2)}) copy-start(bf16[528,128]{1,0:T(8,128)(2,1)S(1)} %merge.2.own_a) | copy-start | bytes 405508
  77.5 13.2 %collective-permute-start.3 = (bf16[528,128]{1,0:T(8,128)(2,1)S(1)}, bf16[528,128]{1,0:T(8,128)(2,1)S(1)}, u32[]{:S(2)}, u32[]{:S(2)}) collective-permute-start(bf16[528,128]{1,0:T(8,128)(2,1)S(1)} %merge.2.own_a), channel_id=1, source_target_pairs={{0,8},{1,9},{2,10},{3,11},{4,12},{5,13},{6,14},{7,15},{8,0},{9,1},... | collective-permute-start | bytes 405512 | tf_op jit(solution)/shard_map/ppermute | solution.py:354
  82.5 10.4 %copy-start = (bf16[528,128]{1,0:T(8,128)(2,1)}, bf16[528,128]{1,0:T(8,128)(2,1)S(1)}, u32[]{:S(2)}) copy-start(bf16[528,128]{1,0:T(8,128)(2,1)S(1)} %merge.3.other_b) | copy-start | bytes 405508
  82.5 10.4 %collective-permute-start.2 = (bf16[528,128]{1,0:T(8,128)(2,1)S(1)}, bf16[528,128]{1,0:T(8,128)(2,1)S(1)}, u32[]{:S(2)}, u32[]{:S(2)}) collective-permute-start(bf16[528,128]{1,0:T(8,128)(2,1)S(1)} %merge.3.other_b), channel_id=1, source_target_pairs={{0,8},{1,9},{2,10},{3,11},{4,12},{5,13},{6,14},{7,15},{8,0},{9,1},... | collective-permute-start | bytes 405512 | tf_op jit(solution)/shard_map/ppermute | solution.py:354
  83.9 9.0 %copy-start.8 = (bf16[2048,256]{1,0:T(8,128)(2,1)}, bf16[2048,256]{1,0:T(8,128)(2,1)S(1)}, u32[]{:S(2)}) copy-start(bf16[2048,256]{1,0:T(8,128)(2,1)S(1)} %collective-permute-done.4.refs_1_) | copy-start | bytes 3145732
  100.3 8.9 %collective-permute-start.17 = (bf16[32,2048]{1,0:T(8,128)(2,1)}, bf16[32,2048]{1,0:T(8,128)(2,1)S(1)}, u32[]{:S(2)}, u32[]{:S(2)}) collective-permute-start(bf16[32,2048]{1,0:T(8,128)(2,1)} %get-tuple-element.8), channel_id=1, source_target_pairs={{0,8},{1,9},{2,10},{3,11},{4,12},{5,13},{6,14},{7,15},{8,0},{9,1},... | collective-permute-start | bytes 393224 | tf_op jit(solution)/shard_map/ppermute | solution.py:354
  (5 other events, 9.5 us)

commit v4 on v3

--- a/solution.py
+++ b/solution.py
@@ -18,7 +18,6 @@
 STAT_ROWS = KVH * PARTS
 SCALE2 = math.log2(math.e) / math.sqrt(HD)
 CHUNK = 512
-AHEAD = 3
 FLOOR = -(2.0**100)
 
 
@@ -279,33 +278,23 @@
 
 def project_kernel(count, places, own_a, own_b, other_a, other_b, me, *refs):
     weights = refs[: len(places)]
-    own_out, other_out = refs[len(places) : len(places) + 2]
-    held, sems = refs[len(places) + 2 :]
+    own_out, other_out = refs[len(places) :]
     width = weights[0].shape[1]
-    copies = {k: [] for k in range(count)}
-    for i, (k, start) in enumerate(places):
-        copies[k].append(
-            pltpu.make_async_copy(
-                weights[i], held.at[k, start : start + weights[i].shape[0], :], sems.at[i]
-            )
-        )
-    order = [copies[k] for k in range(count)]
-    ahead = min(AHEAD, count)
-    for group in order[:ahead]:
-        for copy in group:
-            copy.start()
     tall = (own_a.shape[0] - STAT_ROWS) // KVH
     rows = tall // GROUP
     left = jnp.concatenate(
         [combine(tall, own_a, own_b), combine(tall, other_a, other_b)], axis=0
     )
     for k in range(count):
-        for copy in copies[k]:
-            copy.wait()
-        if k + ahead < count:
-            for copy in order[k + ahead]:
-                copy.start()
-        made = jnp.dot(left, held[k], preferred_element_type=jnp.float32).astype(jnp.bfloat16)
+        made = sum(
+            jnp.dot(
+                left[:, start : start + weights[i].shape[0]],
+                weights[i][...],
+                preferred_element_type=jnp.float32,
+            )
+            for i, (shard, start) in enumerate(places)
+            if shard == k
+        ).astype(jnp.bfloat16)
         at = pl.ds(pl.multiple_of((me[0] ^ k) * width, width), width)
         own_out[:, at] = made[:rows, :]
         other_out[:, at] = made[rows:, :]
@@ -319,7 +308,7 @@
 
 VMEM = pl.BlockSpec(memory_space=pltpu.VMEM)
 SMEM = pl.BlockSpec(memory_space=pltpu.SMEM)
-ANY = pl.BlockSpec(memory_space=pl.ANY)
+PROJECT = pltpu.CompilerParams(vmem_limit_bytes=16 << 20)
 LARGE = pltpu.CompilerParams(vmem_limit_bytes=60 << 20)
 SMALL = pltpu.CompilerParams(vmem_limit_bytes=16 << 20)
 
@@ -329,6 +318,14 @@
         pltpu.SMEM((members * capacity,), jnp.int32),
         pltpu.SMEM((members,), jnp.int32),
     ]
+
+
+def on_chip(array):
+    return pltpu.with_memory_space_constraint(array, pltpu.VMEM)
+
+
+def in_hbm(array):
+    return pltpu.with_memory_space_constraint(array, pltpu.HBM)
 
 
 def early_first(step):
@@ -382,7 +379,7 @@
             out_specs=pl.BlockSpec((half, KVH * block + STAT_ROWS, HD), lambda g: (0, 0, 0)),
             scratch_shapes=[pltpu.VMEM((STAT_ROWS, rows), jnp.float32)],
             compiler_params=pltpu.CompilerParams(
-                dimension_semantics=("arbitrary",), vmem_limit_bytes=58 << 20
+                dimension_semantics=("arbitrary",), vmem_limit_bytes=24 << 20
             ),
             cost_estimate=pl.CostEstimate(
                 flops=4 * rows * KVH * page * HD,
@@ -390,7 +387,7 @@
                 transcendentals=rows * KVH * page,
             ),
             name="attend",
-        )(incoming, keys, values)
+        )(incoming, in_hbm(keys), in_hbm(values))
 
     def merge(listed, returned, own):
         return pl.pallas_call(
@@ -459,15 +456,11 @@
     own_out, other_out = pl.pallas_call(
         functools.partial(project_kernel, half, tuple(places)),
         out_shape=[jax.ShapeDtypeStruct((row_total, half * width), jnp.bfloat16)] * 2,
-        in_specs=[VMEM] * 4 + [SMEM] + [ANY] * len(places),
+        in_specs=[VMEM] * 4 + [SMEM] + [VMEM] * len(places),
         out_specs=[VMEM, VMEM],
-        scratch_shapes=[
-            pltpu.VMEM((half, features, width), jnp.bfloat16),
-            pltpu.SemaphoreType.DMA((len(places),)),
-        ],
-        compiler_params=LARGE,
+        compiler_params=PROJECT,
         name="project",
-    )(own_a, own_b, other_a, other_b, (me % half).reshape(1), *gathered)
+    )(own_a, own_b, other_a, other_b, (me % half).reshape(1), *[on_chip(part) for part in gathered])
     received = mirrored(other_out)
     return pl.pallas_call(
         place_kernel,

time: 111 us -> 110 us (level)
  Pallas kernels: 38.9 us -> 35.5 us
  local copies, waits for them, and re-layouts: 5.82 us -> 7.98 us
    pallas_call x1, Pallas kernels: 6.72 us -> 4.21 us  [shards(): pl.pallas_call(functools.partial(project_kernel, half, tuple(places)), ou...]
    unnamed x31 -> x21, local copies, waits for them, and re-layouts: 3.77 us -> 5.92 us
where the time goes in v4:
time: 110 us; the launch traced here: 109 us
  Pallas kernels  35.5 us (32%)
  starting transfers between devices  34.3 us (31%)
  waiting for transfers between devices  31.5 us (29%)
  local copies, waits for them, and re-layouts  7.98 us (7%)
    ppermute x5, waiting for transfers between devices, mirrored(): lax.ppermute(array, 'seq', [(i, (i + half) % members) for i in range(memb...  23.9 us
    pallas_call x2, Pallas kernels, attend(): pl.pallas_call(attend_kernel, out_shape=jax.ShapeDtypeStruct((half, KVH *...  22.3 us
    all_to_all x4, starting transfers between devices, spread(): lax.all_to_all(array, 'seq', split_axis=0, concat_axis=0, tiled=True, axi...  19.7 us
    ppermute x13, starting transfers between devices, exchanged(): return lax.ppermute(array, 'seq', [(i, i ^ step) for i in range(members)])  8.91 us
    ppermute x13, waiting for transfers between devices, exchanged(): return lax.ppermute(array, 'seq', [(i, i ^ step) for i in range(members)])  6.41 us
    unnamed x21, local copies, waits for them, and re-layouts  5.92 us
    ppermute x5, starting transfers between devices, mirrored(): lax.ppermute(array, 'seq', [(i, (i + half) % members) for i in range(memb...  5.72 us
    pallas_call x1, Pallas kernels, shards(): pl.pallas_call(functools.partial(project_kernel, half, tuple(places)), ou...  4.21 us
  transfers between devices with their start and end apart: 22, of which 6 were waited for; matrix products, arithmetic and copies ran while one was open for 2% of the time, Pallas kernels for 26%

profile of v4, /device:TPU:0, one launch (start us, length us, event | category | flops | bytes accessed | tf_op | source)
XLA Modules:
  0.0 109.4 jit_solution(9927172149599681242)
XLA Ops:
  0.0 1.3 %copy.9.page_list = s32[8,3]{1,0:T(8,128)} copy(s32[8,3]{0,1:T(4,128)} %param.12) | data formatting | bytes 192 | tf_op args[5]
  1.3 2.2 %pack.2 = bf16[8,192,128]{2,1,0:T(8,128)(2,1)} custom-call(s32[1]{0:T(128)} %bitcast.1.base, s32[8,3]{1,0:T(8,128)} %copy.9.page_list, bf16[32,2048]{1,0:T(8,128)(2,1)} %refs_0_.2), custom_call_target="tpu_custom_call" | custom-call | tf_op jit(solution)/shard_map/pack/pallas_call | solution.py:354
  3.6 5.3 %all-to-all-start = ((bf16[8,192,128]{2,1,0:T(8,128)(2,1)}), bf16[8,192,128]{2,1,0:T(8,128)(2,1)S(1)}, u32[]{:S(2)}, u32[]{:S(2)}) async-start(bf16[8,192,128]{2,1,0:T(8,128)(2,1)} %pack.2), calls=%async_computation | async-start | bytes 786432 | tf_op jit(solution)/shard_map/all_to_all | solution.py:365
  8.9 2.6 %collective-permute-start.1 = (bf16[32,2048]{1,0:T(8,128)(2,1)}, bf16[32,2048]{1,0:T(8,128)(2,1)S(1)}, u32[]{:S(2)}, u32[]{:S(2)}) collective-permute-start(bf16[32,2048]{1,0:T(8,128)(2,1)} %refs_0_.2), channel_id=1, source_target_pairs={{0,8},{1,9},{2,10},{3,11},{4,12},{5,13},{6,14},{7,15},{8,0},{9,1},... | collective-permute-start | bytes 393224 | tf_op jit(solution)/shard_map/ppermute | solution.py:351
  11.8 5.4 %collective-permute-done.page_list = s32[8,3]{1,0:T(8,128)S(1)} collective-permute-done((s32[8,3]{1,0:T(8,128)}, s32[8,3]{1,0:T(8,128)S(1)}, u32[]{:S(2)}, u32[]{:S(2)}) %collective-permute-start) | collective-permute-done | bytes 128 | tf_op jit(solution)/shard_map/ppermute | solution.py:351
  17.2 1.9 %pack.3 = bf16[8,192,128]{2,1,0:T(8,128)(2,1)} custom-call(s32[1]{0:T(128)} %bitcast.1.base, s32[8,3]{1,0:T(8,128)S(1)} %collective-permute-done.page_list, bf16[32,2048]{1,0:T(8,128)(2,1)S(1)} %collective-permute-done.1.queries), custom_call_target="tpu_custom_call" | custom-call | tf_op jit(solution)/shard_map/pack/pallas_call | solution.py:354
  19.2 6.7 %all-to-all-start.2 = ((bf16[8,192,128]{2,1,0:T(8,128)(2,1)}), bf16[8,192,128]{2,1,0:T(8,128)(2,1)S(1)}, u32[]{:S(2)}, u32[]{:S(2)}) async-start(bf16[8,192,128]{2,1,0:T(8,128)(2,1)} %pack.3), calls=%async_computation.2 | async-start | bytes 786432 | tf_op jit(solution)/shard_map/all_to_all | solution.py:365
  25.9 2.1 %fusion = (bf16[1024,256]{1,0:T(8,128)(2,1)S(1)}, bf16[1024,256]{1,0:T(8,128)(2,1)}) fusion(bf16[2048,256]{1,0:T(8,128)(2,1)} %refs_0_.3), kind=kLoop, calls=%fused_computation | loop fusion | bytes 2097152 | tf_op jit(solution)/shard_map/slice | solution.py:437
  27.9 2.0 %collective-permute-start.11 = (bf16[1024,256]{1,0:T(8,128)(2,1)S(1)}, bf16[1024,256]{1,0:T(8,128)(2,1)S(1)}, u32[]{:S(2)}, u32[]{:S(2)}) collective-permute-start(bf16[1024,256]{1,0:T(8,128)(2,1)S(1)} %get-tuple-element.9), channel_id=1, source_target_pairs={{0,4},{1,5},{2,6},{3,7},{4,0},{5,1},{6,2},{7,3},{8,12},{9,13},{10,... | collective-permute-start | bytes 1572872 | tf_op jit(solution)/shard_map/ppermute | solution.py:434
  30.0 1.5 %collective-permute-start.7 = (bf16[1024,256]{1,0:T(8,128)(2,1)S(1)}, bf16[1024,256]{1,0:T(8,128)(2,1)}, u32[]{:S(2)}, u32[]{:S(2)}) collective-permute-start(bf16[1024,256]{1,0:T(8,128)(2,1)S(1)} %get-tuple-element.9), channel_id=1, source_target_pairs={{0,2},{1,3},{2,0},{3,1},{4,6},{5,7},{6,4},{7,5},{8,10},{9,11},{10,... | collective-permute-start | bytes 1572872 | tf_op jit(solution)/shard_map/ppermute | solution.py:434
  32.0 11.5 %attend.2 = bf16[8,208,128]{2,1,0:T(8,128)(2,1)} custom-call(bf16[8,192,128]{2,1,0:T(8,128)(2,1)S(1)} %all-to-all-done.queries, bf16[4096,512]{1,0:T(8,128)(2,1)} %keys.3, bf16[4096,512]{1,0:T(8,128)(2,1)} %values.3), custom_call_target="tpu_custom_call" | custom-call | flops 3221225472 | bytes 8388608 | tf_op jit(solution)/shard_map/attend/pallas_call | solution.py:370
  43.5 4.2 %all-to-all-start.1 = ((bf16[8,208,128]{2,1,0:T(8,128)(2,1)}), bf16[8,208,128]{2,1,0:T(8,128)(2,1)S(1)}, u32[]{:S(2)}, u32[]{:S(2)}) async-start(bf16[8,208,128]{2,1,0:T(8,128)(2,1)} %attend.2), calls=%async_computation.1 | async-start | bytes 851968 | tf_op jit(solution)/shard_map/all_to_all | solution.py:365
  48.4 1.6 %collective-permute-start.15 = (bf16[1024,256]{1,0:T(8,128)(2,1)}, bf16[1024,256]{1,0:T(8,128)(2,1)}, u32[]{:S(2)}, u32[]{:S(2)}) collective-permute-start(bf16[1024,256]{1,0:T(8,128)(2,1)} %collective-permute-done.7.refs_4_), channel_id=1, source_target_pairs={{0,4},{1,5},{2,6},{3,7},{4,0},{5,1},{6,2},{7,3},{8,12},{9,13},{10,... | collective-permute-start | bytes 1572872 | tf_op jit(solution)/shard_map/ppermute | solution.py:434
  50.1 6.4 %collective-permute-done.9.refs_6_ = bf16[1024,256]{1,0:T(8,128)(2,1)} collective-permute-done((bf16[1024,256]{1,0:T(8,128)(2,1)}, bf16[1024,256]{1,0:T(8,128)(2,1)}, u32[]{:S(2)}, u32[]{:S(2)}) %collective-permute-start.9) | collective-permute-done | bytes 524320 | tf_op jit(solution)/shard_map/ppermute | solution.py:434
  56.5 1.5 %collective-permute-start.13 = (bf16[1024,256]{1,0:T(8,128)(2,1)}, bf16[1024,256]{1,0:T(8,128)(2,1)}, u32[]{:S(2)}, u32[]{:S(2)}) collective-permute-start(bf16[1024,256]{1,0:T(8,128)(2,1)} %collective-permute-done.9.refs_6_), channel_id=1, source_target_pairs={{0,2},{1,3},{2,0},{3,1},{4,6},{5,7},{6,4},{7,5},{8,10},{9,11},{10,... | collective-permute-start | bytes 1572872 | tf_op jit(solution)/shard_map/ppermute | solution.py:434
  58.0 10.8 %attend.3 = bf16[8,208,128]{2,1,0:T(8,128)(2,1)S(1)} custom-call(bf16[8,192,128]{2,1,0:T(8,128)(2,1)S(1)} %all-to-all-done.2.queries, bf16[4096,512]{1,0:T(8,128)(2,1)} %keys.3, bf16[4096,512]{1,0:T(8,128)(2,1)} %values.3), custom_call_target="tpu_custom_call" | custom-call | flops 3221225472 | bytes 8388608 | tf_op jit(solution)/shard_map/attend/pallas_call | solution.py:370
  68.8 0.8 copy-done.6
  69.5 3.5 %all-to-all-start.3 = ((bf16[8,208,128]{2,1,0:T(8,128)(2,1)}), bf16[8,208,128]{2,1,0:T(8,128)(2,1)S(1)}, u32[]{:S(2)}, u32[]{:S(2)}) async-start(bf16[8,208,128]{2,1,0:T(8,128)(2,1)} %copy-done.6), calls=%async_computation.3 | async-start | bytes 851968 | tf_op jit(solution)/shard_map/all_to_all | solution.py:365
  74.1 0.9 copy-done.5
  75.0 2.4 %merge.2.own_a = bf16[528,128]{1,0:T(8,128)(2,1)S(1)} custom-call(s32[1]{0:T(128)} %bitcast.1.base, s32[8,3]{1,0:T(8,128)S(1)} %copy-done.7, bf16[32,2048]{1,0:T(8,128)(2,1)S(1)} %copy-done.5, bf16[32,512]{1,0:T(8,128)(2,1)S(1)} %copy-done.8, bf16[32,512]{1,0:T(8,128)(2,1)S(1)} %copy-done.9, bf16[8,208,128]{2,1,0:T(8,128)(2,1)S(1)} %all-to-all-done.1.refs_3_), custom_call_target="tpu_custom_call" | custom-call | tf_op jit(solution)/shard_map/merge/pallas_call | solution.py:393
  77.5 0.8 copy-done.3
  78.3 1.3 %collective-permute-start.3 = (bf16[528,128]{1,0:T(8,128)(2,1)S(1)}, bf16[528,128]{1,0:T(8,128)(2,1)S(1)}, u32[]{:S(2)}, u32[]{:S(2)}) collective-permute-start(bf16[528,128]{1,0:T(8,128)(2,1)S(1)} %merge.2.own_a), channel_id=1, source_target_pairs={{0,8},{1,9},{2,10},{3,11},{4,12},{5,13},{6,14},{7,15},{8,0},{9,1},... | collective-permute-start | bytes 405512 | tf_op jit(solution)/shard_map/ppermute | solution.py:351
  79.6 1.1 %all-to-all-done.3.refs_0_ = bf16[8,208,128]{2,1,0:T(8,128)(2,1)S(1)} async-done(((bf16[8,208,128]{2,1,0:T(8,128)(2,1)}), bf16[8,208,128]{2,1,0:T(8,128)(2,1)S(1)}, u32[]{:S(2)}, u32[]{:S(2)}) %all-to-all-start.3) | async-done | bytes 426016 | tf_op jit(solution)/shard_map/all_to_all | solution.py:365
  80.7 1.7 %merge.3.other_b = bf16[528,128]{1,0:T(8,128)(2,1)S(1)} custom-call(s32[1]{0:T(128)} %bitcast.1.base, s32[8,3]{1,0:T(8,128)S(1)} %collective-permute-done.page_list, bf16[8,208,128]{2,1,0:T(8,128)(2,1)S(1)} %all-to-all-done.3.refs_0_), custom_call_target="tpu_custom_call" | custom-call | tf_op jit(solution)/shard_map/merge/pallas_call | solution.py:393
  82.4 1.4 %collective-permute-start.2 = (bf16[528,128]{1,0:T(8,128)(2,1)S(1)}, bf16[528,128]{1,0:T(8,128)(2,1)S(1)}, u32[]{:S(2)}, u32[]{:S(2)}) collective-permute-start(bf16[528,128]{1,0:T(8,128)(2,1)S(1)} %merge.3.other_b), channel_id=1, source_target_pairs={{0,8},{1,9},{2,10},{3,11},{4,12},{5,13},{6,14},{7,15},{8,0},{9,1},... | collective-permute-start | bytes 405512 | tf_op jit(solution)/shard_map/ppermute | solution.py:351
  83.8 7.6 %collective-permute-done.3.other_a = bf16[528,128]{1,0:T(8,128)(2,1)S(1)} collective-permute-done((bf16[528,128]{1,0:T(8,128)(2,1)S(1)}, bf16[528,128]{1,0:T(8,128)(2,1)S(1)}, u32[]{:S(2)}, u32[]{:S(2)}) %collective-permute-start.3) | collective-permute-done | bytes 135200 | tf_op jit(solution)/shard_map/ppermute | solution.py:351
  91.5 2.3 %collective-permute-done.2.own_b = bf16[528,128]{1,0:T(8,128)(2,1)S(1)} collective-permute-done((bf16[528,128]{1,0:T(8,128)(2,1)S(1)}, bf16[528,128]{1,0:T(8,128)(2,1)S(1)}, u32[]{:S(2)}, u32[]{:S(2)}) %collective-permute-start.2) | collective-permute-done | bytes 135200 | tf_op jit(solution)/shard_map/ppermute | solution.py:351
  93.7 1.0 copy-done.2
  94.8 1.0 copy-done.4
  95.8 4.2 %project.1 = (bf16[32,2048]{1,0:T(8,128)(2,1)S(1)}, bf16[32,2048]{1,0:T(8,128)(2,1)S(1)}) custom-call(bf16[528,128]{1,0:T(8,128)(2,1)S(1)} %merge.2.own_a, bf16[528,128]{1,0:T(8,128)(2,1)S(1)} %collective-permute-done.2.own_b, bf16[528,128]{1,0:T(8,128)(2,1)S(1)} %collective-permute-done.3.other_a, bf16[528,128]{1,0:T(8,128)(2,1)S(1)} %merge.3.other_b, ...), custom_call_target="tpu_custom_call" | custom-call | tf_op jit(solution)/shard_map/project/pallas_call | solution.py:456
  100.1 8.6 %collective-permute-done.17.received = bf16[32,2048]{1,0:T(8,128)(2,1)S(1)} collective-permute-done((bf16[32,2048]{1,0:T(8,128)(2,1)S(1)}, bf16[32,2048]{1,0:T(8,128)(2,1)S(1)}, u32[]{:S(2)}, u32[]{:S(2)}) %collective-permute-start.17) | collective-permute-done | bytes 131104 | tf_op jit(solution)/shard_map/ppermute | solution.py:351
  108.7 0.7 place.1
  (42 shorter events, 2.8 us)
Async XLA Ops:
  3.6 15.6 %all-to-all-start = ((bf16[8,192,128]{2,1,0:T(8,128)(2,1)}), bf16[8,192,128]{2,1,0:T(8,128)(2,1)S(1)}, u32[]{:S(2)}, u32[]{:S(2)}) async-start(bf16[8,192,128]{2,1,0:T(8,128)(2,1)} %pack.2), calls=%async_computation | async-start | bytes 786432 | tf_op jit(solution)/shard_map/all_to_all | solution.py:365
  8.9 8.4 %collective-permute-start.1 = (bf16[32,2048]{1,0:T(8,128)(2,1)}, bf16[32,2048]{1,0:T(8,128)(2,1)S(1)}, u32[]{:S(2)}, u32[]{:S(2)}) collective-permute-start(bf16[32,2048]{1,0:T(8,128)(2,1)} %refs_0_.2), channel_id=1, source_target_pairs={{0,8},{1,9},{2,10},{3,11},{4,12},{5,13},{6,14},{7,15},{8,0},{9,1},... | collective-permute-start | bytes 393224 | tf_op jit(solution)/shard_map/ppermute | solution.py:351
  11.4 5.8 %collective-permute-start = (s32[8,3]{1,0:T(8,128)}, s32[8,3]{1,0:T(8,128)S(1)}, u32[]{:S(2)}, u32[]{:S(2)}) collective-permute-start(s32[8,3]{1,0:T(8,128)} %copy.9.page_list), channel_id=1, source_target_pairs={{0,8},{1,9},{2,10},{3,11},{4,12},{5,13},{6,14},{7,15},{8,0},{9,1},... | collective-permute-start | bytes 296 | tf_op jit(solution)/shard_map/ppermute | solution.py:351
  19.2 24.4 %all-to-all-start.2 = ((bf16[8,192,128]{2,1,0:T(8,128)(2,1)}), bf16[8,192,128]{2,1,0:T(8,128)(2,1)S(1)}, u32[]{:S(2)}, u32[]{:S(2)}) async-start(bf16[8,192,128]{2,1,0:T(8,128)(2,1)} %pack.3), calls=%async_computation.2 | async-start | bytes 786432 | tf_op jit(solution)/shard_map/all_to_all | solution.py:365
  27.9 19.8 %collective-permute-start.11 = (bf16[1024,256]{1,0:T(8,128)(2,1)S(1)}, bf16[1024,256]{1,0:T(8,128)(2,1)S(1)}, u32[]{:S(2)}, u32[]{:S(2)}) collective-permute-start(bf16[1024,256]{1,0:T(8,128)(2,1)S(1)} %get-tuple-element.9), channel_id=1, source_target_pairs={{0,4},{1,5},{2,6},{3,7},{4,0},{5,1},{6,2},{7,3},{8,12},{9,13},{10,... | collective-permute-start | bytes 1572872 | tf_op jit(solution)/shard_map/ppermute | solution.py:434
  30.0 18.4 %collective-permute-start.7 = (bf16[1024,256]{1,0:T(8,128)(2,1)S(1)}, bf16[1024,256]{1,0:T(8,128)(2,1)}, u32[]{:S(2)}, u32[]{:S(2)}) collective-permute-start(bf16[1024,256]{1,0:T(8,128)(2,1)S(1)} %get-tuple-element.9), channel_id=1, source_target_pairs={{0,2},{1,3},{2,0},{3,1},{4,6},{5,7},{6,4},{7,5},{8,10},{9,11},{10,... | collective-permute-start | bytes 1572872 | tf_op jit(solution)/shard_map/ppermute | solution.py:434
  31.4 18.6 %copy-start = (bf16[2048,256]{1,0:T(8,128)(2,1)S(1)}, bf16[2048,256]{1,0:T(8,128)(2,1)}, u32[]{:S(2)}) copy-start(bf16[2048,256]{1,0:T(8,128)(2,1)} %refs_0_.3) | copy-start | bytes 3145732
  31.4 25.0 %collective-permute-start.9 = (bf16[1024,256]{1,0:T(8,128)(2,1)}, bf16[1024,256]{1,0:T(8,128)(2,1)}, u32[]{:S(2)}, u32[]{:S(2)}) collective-permute-start(bf16[1024,256]{1,0:T(8,128)(2,1)} %get-tuple-element.10), channel_id=1, source_target_pairs={{0,4},{1,5},{2,6},{3,7},{4,0},{5,1},{6,2},{7,3},{8,12},{9,13},{10,... | collective-permute-start | bytes 1572872 | tf_op jit(solution)/shard_map/ppermute | solution.py:434
  32.0 24.5 %collective-permute-start.5 = (bf16[1024,256]{1,0:T(8,128)(2,1)}, bf16[1024,256]{1,0:T(8,128)(2,1)}, u32[]{:S(2)}, u32[]{:S(2)}) collective-permute-start(bf16[1024,256]{1,0:T(8,128)(2,1)} %get-tuple-element.10), channel_id=1, source_target_pairs={{0,2},{1,3},{2,0},{3,1},{4,6},{5,7},{6,4},{7,5},{8,10},{9,11},{10,... | collective-permute-start | bytes 1572872 | tf_op jit(solution)/shard_map/ppermute | solution.py:434
  43.5 26.0 %all-to-all-start.1 = ((bf16[8,208,128]{2,1,0:T(8,128)(2,1)}), bf16[8,208,128]{2,1,0:T(8,128)(2,1)S(1)}, u32[]{:S(2)}, u32[]{:S(2)}) async-start(bf16[8,208,128]{2,1,0:T(8,128)(2,1)} %attend.2), calls=%async_computation.1 | async-start | bytes 851968 | tf_op jit(solution)/shard_map/all_to_all | solution.py:365
  47.7 26.4 %copy-start.7 = (s32[8,3]{1,0:T(8,128)S(1)}, s32[8,3]{1,0:T(8,128)}, u32[]{:S(2)}) copy-start(s32[8,3]{1,0:T(8,128)} %copy.9.page_list) | copy-start | bytes 292
  47.7 26.4 %copy-start.8 = (bf16[32,512]{1,0:T(8,128)(2,1)S(1)}, bf16[32,512]{1,0:T(8,128)(2,1)}, u32[]{:S(2)}) copy-start(bf16[32,512]{1,0:T(8,128)(2,1)} %refs_1_.1) | copy-start | bytes 98308
  47.8 26.4 %copy-start.9 = (bf16[32,512]{1,0:T(8,128)(2,1)S(1)}, bf16[32,512]{1,0:T(8,128)(2,1)}, u32[]{:S(2)}) copy-start(bf16[32,512]{1,0:T(8,128)(2,1)} %refs_2_.1) | copy-start | bytes 98308
  47.8 21.0 %copy-start.1 = (bf16[1024,256]{1,0:T(8,128)(2,1)}, bf16[1024,256]{1,0:T(8,128)(2,1)S(1)}, u32[]{:S(2)}) copy-start(bf16[1024,256]{1,0:T(8,128)(2,1)S(1)} %collective-permute-done.11.refs_8_) | copy-start | bytes 1572868
  47.8 25.2 %collective-permute-start.12 = (bf16[1024,256]{1,0:T(8,128)(2,1)S(1)}, bf16[1024,256]{1,0:T(8,128)(2,1)}, u32[]{:S(2)}, u32[]{:S(2)}) collective-permute-start(bf16[1024,256]{1,0:T(8,128)(2,1)S(1)} %collective-permute-done.11.refs_8_), channel_id=1, source_target_pairs={{0,1},{1,0},{2,3},{3,2},{4,5},{5,4},{6,7},{7,6},{8,9},{9,8},{10,11... | collective-permute-start | bytes 1572872 | tf_op jit(solution)/shard_map/ppermute | solution.py:434
  48.4 25.1 %collective-permute-start.15 = (bf16[1024,256]{1,0:T(8,128)(2,1)}, bf16[1024,256]{1,0:T(8,128)(2,1)}, u32[]{:S(2)}, u32[]{:S(2)}) collective-permute-start(bf16[1024,256]{1,0:T(8,128)(2,1)} %collective-permute-done.7.refs_4_), channel_id=1, source_target_pairs={{0,4},{1,5},{2,6},{3,7},{4,0},{5,1},{6,2},{7,3},{8,12},{9,13},{10,... | collective-permute-start | bytes 1572872 | tf_op jit(solution)/shard_map/ppermute | solution.py:434
  50.0 33.8 %collective-permute-start.4 = (bf16[2048,256]{1,0:T(8,128)(2,1)S(1)}, bf16[2048,256]{1,0:T(8,128)(2,1)S(1)}, u32[]{:S(2)}, u32[]{:S(2)}) collective-permute-start(bf16[2048,256]{1,0:T(8,128)(2,1)S(1)} %copy-done), channel_id=1, source_target_pairs={{0,1},{1,0},{2,3},{3,2},{4,5},{5,4},{6,7},{7,6},{8,9},{9,8},{10,11... | collective-permute-start | bytes 3145736 | tf_op jit(solution)/shard_map/ppermute | solution.py:434
  56.5 17.1 %collective-permute-start.8 = (bf16[1024,256]{1,0:T(8,128)(2,1)}, bf16[1024,256]{1,0:T(8,128)(2,1)}, u32[]{:S(2)}, u32[]{:S(2)}) collective-permute-start(bf16[1024,256]{1,0:T(8,128)(2,1)} %collective-permute-done.7.refs_4_), channel_id=1, source_target_pairs={{0,1},{1,0},{2,3},{3,2},{4,5},{5,4},{6,7},{7,6},{8,9},{9,8},{10,11... | collective-permute-start | bytes 1572872 | tf_op jit(solution)/shard_map/ppermute | solution.py:434
  56.5 17.5 %collective-permute-start.13 = (bf16[1024,256]{1,0:T(8,128)(2,1)}, bf16[1024,256]{1,0:T(8,128)(2,1)}, u32[]{:S(2)}, u32[]{:S(2)}) collective-permute-start(bf16[1024,256]{1,0:T(8,128)(2,1)} %collective-permute-done.9.refs_6_), channel_id=1, source_target_pairs={{0,2},{1,3},{2,0},{3,1},{4,6},{5,7},{6,4},{7,5},{8,10},{9,11},{10,... | collective-permute-start | bytes 1572872 | tf_op jit(solution)/shard_map/ppermute | solution.py:434
  68.8 0.8 copy-start.6
  69.5 11.2 %all-to-all-start.3 = ((bf16[8,208,128]{2,1,0:T(8,128)(2,1)}), bf16[8,208,128]{2,1,0:T(8,128)(2,1)S(1)}, u32[]{:S(2)}, u32[]{:S(2)}) async-start(bf16[8,208,128]{2,1,0:T(8,128)(2,1)} %copy-done.6), calls=%async_computation.3 | async-start | bytes 851968 | tf_op jit(solution)/shard_map/all_to_all | solution.py:365
  73.0 4.5 %collective-permute-start.10 = (bf16[1024,256]{1,0:T(8,128)(2,1)}, bf16[1024,256]{1,0:T(8,128)(2,1)S(1)}, u32[]{:S(2)}, u32[]{:S(2)}) collective-permute-start(bf16[1024,256]{1,0:T(8,128)(2,1)} %collective-permute-done.9.refs_6_), channel_id=1, source_target_pairs={{0,1},{1,0},{2,3},{3,2},{4,5},{5,4},{6,7},{7,6},{8,9},{9,8},{10,11... | collective-permute-start | bytes 1572872 | tf_op jit(solution)/shard_map/ppermute | solution.py:434
  73.4 9.0 %collective-permute-start.6 = (bf16[1024,256]{1,0:T(8,128)(2,1)}, bf16[1024,256]{1,0:T(8,128)(2,1)}, u32[]{:S(2)}, u32[]{:S(2)}) collective-permute-start(bf16[1024,256]{1,0:T(8,128)(2,1)} %collective-permute-done.5.refs_2_), channel_id=1, source_target_pairs={{0,1},{1,0},{2,3},{3,2},{4,5},{5,4},{6,7},{7,6},{8,9},{9,8},{10,11... | collective-permute-start | bytes 1572872 | tf_op jit(solution)/shard_map/ppermute | solution.py:434
  73.6 17.8 %collective-permute-start.16 = (bf16[1024,256]{1,0:T(8,128)(2,1)}, bf16[1024,256]{1,0:T(8,128)(2,1)}, u32[]{:S(2)}, u32[]{:S(2)}) collective-permute-start(bf16[1024,256]{1,0:T(8,128)(2,1)} %collective-permute-done.15.refs_12_), channel_id=1, source_target_pairs={{0,1},{1,0},{2,3},{3,2},{4,5},{5,4},{6,7},{7,6},{8,9},{9,8},{10,11... | collective-permute-start | bytes 1572872 | tf_op jit(solution)/shard_map/ppermute | solution.py:434
  73.9 17.5 %collective-permute-start.14 = (bf16[1024,256]{1,0:T(8,128)(2,1)}, bf16[1024,256]{1,0:T(8,128)(2,1)}, u32[]{:S(2)}, u32[]{:S(2)}) collective-permute-start(bf16[1024,256]{1,0:T(8,128)(2,1)} %collective-permute-done.13.refs_10_), channel_id=1, source_target_pairs={{0,1},{1,0},{2,3},{3,2},{4,5},{5,4},{6,7},{7,6},{8,9},{9,8},{10,11... | collective-permute-start | bytes 1572872 | tf_op jit(solution)/shard_map/ppermute | solution.py:434
  74.1 0.9 copy-start.5
  77.5 0.8 copy-start.3
  78.3 13.2 %collective-permute-start.3 = (bf16[528,128]{1,0:T(8,128)(2,1)S(1)}, bf16[528,128]{1,0:T(8,128)(2,1)S(1)}, u32[]{:S(2)}, u32[]{:S(2)}) collective-permute-start(bf16[528,128]{1,0:T(8,128)(2,1)S(1)} %merge.2.own_a), channel_id=1, source_target_pairs={{0,8},{1,9},{2,10},{3,11},{4,12},{5,13},{6,14},{7,15},{8,0},{9,1},... | collective-permute-start | bytes 405512 | tf_op jit(solution)/shard_map/ppermute | solution.py:351
  82.4 11.3 %collective-permute-start.2 = (bf16[528,128]{1,0:T(8,128)(2,1)S(1)}, bf16[528,128]{1,0:T(8,128)(2,1)S(1)}, u32[]{:S(2)}, u32[]{:S(2)}) collective-permute-start(bf16[528,128]{1,0:T(8,128)(2,1)S(1)} %merge.3.other_b), channel_id=1, source_target_pairs={{0,8},{1,9},{2,10},{3,11},{4,12},{5,13},{6,14},{7,15},{8,0},{9,1},... | collective-permute-start | bytes 405512 | tf_op jit(solution)/shard_map/ppermute | solution.py:351
  93.7 1.0 copy-start.2
  94.8 1.0 copy-start.4
  100.0 8.6 %collective-permute-start.17 = (bf16[32,2048]{1,0:T(8,128)(2,1)S(1)}, bf16[32,2048]{1,0:T(8,128)(2,1)S(1)}, u32[]{:S(2)}, u32[]{:S(2)}) collective-permute-start(bf16[32,2048]{1,0:T(8,128)(2,1)S(1)} %get-tuple-element.8), channel_id=1, source_target_pairs={{0,8},{1,9},{2,10},{3,11},{4,12},{5,13},{6,14},{7,15},{8,0},{9,1},... | collective-permute-start | bytes 393224 | tf_op jit(solution)/shard_map/ppermute | solution.py:351

commit v5 on v4

--- a/solution.py
+++ b/solution.py
@@ -25,59 +25,51 @@
     return lax.broadcasted_iota(jnp.int32, shape, axis)
 
 
-def fill_slots(page_list, base, members, capacity, source, count):
-    tiles, width = page_list.shape
-
-    def clear(i, carry):
-        source[i] = -1
-        return carry
-
-    lax.fori_loop(0, members * capacity, clear, 0)
-
-    def clear_count(i, carry):
-        count[i] = 0
-        return carry
-
-    lax.fori_loop(0, members, clear_count, 0)
-    for tile in range(tiles):
-        for item in range(width):
-            page = page_list[tile, item] - base
-
-            @pl.when((page >= 0) & (page < members))
-            def _():
-                slot = count[page]
-                source[page * capacity + slot] = tile
-                count[page] = slot + 1
-
-
-def pack_kernel(members, capacity, base, page_list, queries, packed, source, count):
-    tiles = page_list.shape[0]
+def slot_codes(listed, base, members, capacity, tile):
+    width, tiles = listed.shape
+    entry = [[listed[k : k + 1, t : t + 1] for t in range(tiles)] for k in range(width)]
+    codes = []
+    for k in range(width):
+        page = jnp.zeros_like(tile)
+        for t in range(tiles):
+            page = jnp.where(tile == t, entry[k][t], page)
+        slot = jnp.zeros_like(tile)
+        for t in range(tiles):
+            earlier = tile > t
+            for other in range(width):
+                slot = slot + jnp.where(earlier & (page == entry[other][t]), 1, 0)
+        page = page - base
+        inside = (page >= 0) & (page < members)
+        codes.append(jnp.where(inside, page * capacity + slot, -1))
+    return codes
+
+
+def pack_kernel(members, capacity, base, listed, queries, packed):
+    tiles = listed.shape[1]
     rows = queries.shape[0]
     tile_rows = rows // tiles
     slot_rows = capacity * tile_rows
     block = GROUP * slot_rows
-    fill_slots(page_list, base[0], members, capacity, source, count)
-    row = iota((block, GROUP * rows), 0)
-    col = iota((block, GROUP * rows), 1)
+    tall = GROUP * rows
+    codes = slot_codes(
+        listed, base[0], members, capacity, iota((8, tall), 1) % rows // tile_rows
+    )
+    row = iota((block, tall), 0)
+    col = iota((block, tall), 1)
     fixed = (row // slot_rows == col // rows) & (row % tile_rows == col % tile_rows)
-    slot = row % slot_rows // tile_rows
-    tile = col % rows // tile_rows
+    slot = jnp.where(fixed, row % slot_rows // tile_rows, -2 - members * capacity)
     pieces = []
     for page in range(members):
-        wanted = jnp.full((block, GROUP * rows), -1, jnp.int32)
-        for k in range(capacity):
-            wanted = jnp.where(slot == k, source[page * capacity + k], wanted)
-        pieces.append((fixed & (tile == wanted)).astype(jnp.bfloat16))
+        here = slot + page * capacity
+        hit = codes[0][:1, :] == here
+        for code in codes[1:]:
+            hit = hit | (code[:1, :] == here)
+        pieces.append(jnp.where(hit, 1.0, 0.0).astype(jnp.bfloat16))
     chosen = jnp.concatenate(pieces, axis=0)
     for group in range(KVH):
-        stacked = jnp.concatenate(
-            [
-                queries[:, (group * GROUP + j) * HD : (group * GROUP + j + 1) * HD]
-                for j in range(GROUP)
-            ],
-            axis=0,
-        )
-        sent = jnp.dot(chosen, stacked, preferred_element_type=jnp.float32).astype(jnp.bfloat16)
+        sent = jnp.dot(
+            chosen, stacked_heads(queries, group), preferred_element_type=jnp.float32
+        ).astype(jnp.bfloat16)
         packed[:, group * block : (group + 1) * block, :] = sent.reshape(members, block, HD)
 
 
@@ -179,25 +171,32 @@
     return peak * SCALE2, total, mixed
 
 
-def merge_kernel(members, capacity, with_own, base, page_list, *refs):
+def merge_kernel(members, capacity, with_own, base, listed, *refs):
     own_refs = refs[:3] if with_own else ()
-    returned, merged, source, count = refs[len(own_refs) :]
-    tiles = page_list.shape[0]
+    returned, merged = refs[len(own_refs) :]
+    tiles = listed.shape[1]
     tall = (merged.shape[0] - STAT_ROWS) // KVH
     rows = tall // GROUP
     tile_rows = rows // tiles
     slot_rows = capacity * tile_rows
     block = GROUP * slot_rows
     width = members * block
-    fill_slots(page_list, base[0], members, capacity, source, count)
+    across = iota((8, tall), 1)
+    codes = slot_codes(listed, base[0], members, capacity, across % rows // tile_rows)
+    turned = jnp.full((8, tall), -1, jnp.int32)
+    for k, code in enumerate(codes):
+        code = (code * GROUP + across // rows) * tile_rows + across % tile_rows
+        turned = jnp.where(iota((8, tall), 0) == k, code, turned)
+    turned = jnp.concatenate(
+        [turned.astype(jnp.float32), jnp.zeros((LANES - 8, tall), jnp.float32)], axis=0
+    ).T.astype(jnp.int32)
     lane = iota((8, width), 1)
-    lane_slot = lane // block * capacity + lane % slot_rows // tile_rows
-    wanted = jnp.full((8, width), -1, jnp.int32)
-    for slot in range(members * capacity):
-        wanted = jnp.where(lane_slot == slot, source[slot], wanted)
-    lane_code = (wanted * tile_rows + lane % tile_rows) + (lane % block // slot_rows) * rows
-    lane_code = jnp.where(wanted < 0, -1, lane_code)[:1, :]
-    bias = jnp.where(iota((tall, width), 0) == lane_code, 0.0, -jnp.inf)
+    lane_code = lane // block * capacity + lane % slot_rows // tile_rows
+    lane_code = (lane_code * GROUP + lane % block // slot_rows) * tile_rows + lane % tile_rows
+    hit = turned[:, :1] == lane_code[:1, :]
+    for k in range(1, len(codes)):
+        hit = hit | (turned[:, k : k + 1] == lane_code[:1, :])
+    bias = jnp.where(hit, 0.0, -jnp.inf)
     stat_pieces = [
         returned[member, KVH * block :, :].astype(jnp.float32)[:, :block]
         for member in range(members)
@@ -313,13 +312,6 @@
 SMALL = pltpu.CompilerParams(vmem_limit_bytes=16 << 20)
 
 
-def slot_scratch(members, capacity):
-    return [
-        pltpu.SMEM((members * capacity,), jnp.int32),
-        pltpu.SMEM((members,), jnp.int32),
-    ]
-
-
 def on_chip(array):
     return pltpu.with_memory_space_constraint(array, pltpu.VMEM)
 
@@ -354,9 +346,8 @@
         return pl.pallas_call(
             functools.partial(pack_kernel, half, capacity),
             out_shape=jax.ShapeDtypeStruct((half, KVH * block, HD), jnp.bfloat16),
-            in_specs=[SMEM, SMEM, VMEM],
+            in_specs=[SMEM, VMEM, VMEM],
             out_specs=VMEM,
-            scratch_shapes=slot_scratch(half, capacity),
             compiler_params=params,
             name="pack",
         )(base, listed, tiles)
@@ -393,16 +384,16 @@
         return pl.pallas_call(
             functools.partial(merge_kernel, half, capacity, bool(own)),
             out_shape=jax.ShapeDtypeStruct((KVH * tall + STAT_ROWS, HD), jnp.bfloat16),
-            in_specs=[SMEM, SMEM] + [VMEM] * (len(own) + 1),
+            in_specs=[SMEM] + [VMEM] * (len(own) + 2),
             out_specs=VMEM,
-            scratch_shapes=slot_scratch(half, capacity),
             compiler_params=SMALL,
             name="merge",
         )(base, listed, *own, returned)
 
+    own_list = page_list.T
     other_queries = mirrored(queries)
-    other_list = mirrored(page_list)
-    packed_near = pack(queries, page_list, LARGE)
+    other_list = mirrored(own_list)
+    packed_near = pack(queries, own_list, LARGE)
     near = spread(packed_near)
     packed_far = pack(other_queries, other_list, SMALL)
     far = spread(packed_far)
@@ -410,7 +401,7 @@
     near_back = spread(near_partial)
     far_partial = attend(far)
     far_back = spread(far_partial)
-    own_a = merge(page_list, near_back, (queries, new_keys, new_values))
+    own_a = merge(own_list, near_back, (queries, new_keys, new_values))
     other_b = merge(other_list, far_back, ())
     other_a = mirrored(own_a)
     own_b = mirrored(other_b)

time: 110 us -> 107 us (0.973)
  Pallas kernels: 35.5 us -> 33.4 us
  waiting for transfers between devices: 31.5 us -> 32.9 us
  local copies, waits for them, and re-layouts: 7.98 us -> 6.64 us
    all_to_all x4, waiting for transfers between devices: 1.16 us -> 2.53 us  [spread(): lax.all_to_all(array, 'seq', split_axis=0, concat_axis=0, tiled=True, axi...]
    unnamed x21 -> x20, local copies, waits for them, and re-layouts: 5.92 us -> 4.57 us
    pallas_call x2, Pallas kernels: 4.09 us -> 2.87 us  [merge(): pl.pallas_call(functools.partial(merge_kernel, half, capacity, bool(own))...]
  transfers between devices with their start and end apart: 22 -> 22, of which waited for: 6 -> 7; matrix products, arithmetic and copies ran while one was open for 2% -> 2% of each run, Pallas kernels for 26% -> 25%
where the time goes in v5:
time: 107 us
  starting transfers between devices  33.5 us (31%)
  Pallas kernels  33.4 us (31%)
  waiting for transfers between devices  32.9 us (31%)
  local copies, waits for them, and re-layouts  6.64 us (6%)
    ppermute x5, waiting for transfers between devices, mirrored(): lax.ppermute(array, 'seq', [(i, (i + half) % members) for i in range(memb...  23.9 us
    pallas_call x2, Pallas kernels, attend(): pl.pallas_call(attend_kernel, out_shape=jax.ShapeDtypeStruct((half, KVH *...  22.3 us
    all_to_all x4, starting transfers between devices, spread(): lax.all_to_all(array, 'seq', split_axis=0, concat_axis=0, tiled=True, axi...  18.9 us
    ppermute x13, starting transfers between devices, exchanged(): return lax.ppermute(array, 'seq', [(i, i ^ step) for i in range(members)])  8.91 us
    ppermute x13, waiting for transfers between devices, exchanged(): return lax.ppermute(array, 'seq', [(i, i ^ step) for i in range(members)])  6.41 us
    ppermute x5, starting transfers between devices, mirrored(): lax.ppermute(array, 'seq', [(i, (i + half) % members) for i in range(memb...  5.63 us
    unnamed x20, local copies, waits for them, and re-layouts  4.57 us
    pallas_call x1, Pallas kernels, shards(): pl.pallas_call(functools.partial(project_kernel, half, tuple(places)), ou...  4.22 us
  transfers between devices with their start and end apart: 22, of which 7 were waited for; matrix products, arithmetic and copies ran while one was open for 2% of the time, Pallas kernels for 25%

profile of v5, /device:TPU:0, one launch (start us, length us, event | category | flops | bytes accessed | tf_op | source)
XLA Modules:
  0.0 106.5 jit_solution(8468895844683485953)
XLA Ops:
  0.0 2.1 %pack.2 = bf16[8,192,128]{2,1,0:T(8,128)(2,1)} custom-call(s32[1]{0:T(128)} %bitcast.1.base, s32[3,8]{1,0:T(4,128)} %bitcast.4, bf16[32,2048]{1,0:T(8,128)(2,1)} %refs_0_.2), custom_call_target="tpu_custom_call" | custom-call | tf_op jit(solution)/shard_map/pack/pallas_call | solution.py:346
  2.1 5.3 %all-to-all-start = ((bf16[8,192,128]{2,1,0:T(8,128)(2,1)}), bf16[8,192,128]{2,1,0:T(8,128)(2,1)S(1)}, u32[]{:S(2)}, u32[]{:S(2)}) async-start(bf16[8,192,128]{2,1,0:T(8,128)(2,1)} %pack.2), calls=%async_computation | async-start | bytes 786432 | tf_op jit(solution)/shard_map/all_to_all | solution.py:356
  7.4 2.6 %collective-permute-start.1 = (bf16[32,2048]{1,0:T(8,128)(2,1)}, bf16[32,2048]{1,0:T(8,128)(2,1)S(1)}, u32[]{:S(2)}, u32[]{:S(2)}) collective-permute-start(bf16[32,2048]{1,0:T(8,128)(2,1)} %refs_0_.2), channel_id=1, source_target_pairs={{0,8},{1,9},{2,10},{3,11},{4,12},{5,13},{6,14},{7,15},{8,0},{9,1},... | collective-permute-start | bytes 393224 | tf_op jit(solution)/shard_map/ppermute | solution.py:343
  10.3 5.4 %collective-permute-done.listed = s32[3,8]{1,0:T(4,128)S(1)} collective-permute-done((s32[3,8]{1,0:T(4,128)}, s32[3,8]{1,0:T(4,128)S(1)}, u32[]{:S(2)}, u32[]{:S(2)}) %collective-permute-start) | collective-permute-done | bytes 128 | tf_op jit(solution)/shard_map/ppermute | solution.py:343
  15.7 1.2 %pack.3 = bf16[8,192,128]{2,1,0:T(8,128)(2,1)} custom-call(s32[1]{0:T(128)} %bitcast.1.base, s32[3,8]{1,0:T(4,128)S(1)} %collective-permute-done.listed, bf16[32,2048]{1,0:T(8,128)(2,1)S(1)} %collective-permute-done.1.queries), custom_call_target="tpu_custom_call" | custom-call | tf_op jit(solution)/shard_map/pack/pallas_call | solution.py:346
  16.9 0.8 all-to-all-done.queries
  17.6 6.0 %all-to-all-start.2 = ((bf16[8,192,128]{2,1,0:T(8,128)(2,1)}), bf16[8,192,128]{2,1,0:T(8,128)(2,1)S(1)}, u32[]{:S(2)}, u32[]{:S(2)}) async-start(bf16[8,192,128]{2,1,0:T(8,128)(2,1)} %pack.3), calls=%async_computation.2 | async-start | bytes 786432 | tf_op jit(solution)/shard_map/all_to_all | solution.py:356
  23.6 2.1 %fusion = (bf16[1024,256]{1,0:T(8,128)(2,1)S(1)}, bf16[1024,256]{1,0:T(8,128)(2,1)}) fusion(bf16[2048,256]{1,0:T(8,128)(2,1)} %refs_0_.3), kind=kLoop, calls=%fused_computation | loop fusion | bytes 2097152 | tf_op jit(solution)/shard_map/slice | solution.py:428
  25.7 2.0 %collective-permute-start.11 = (bf16[1024,256]{1,0:T(8,128)(2,1)S(1)}, bf16[1024,256]{1,0:T(8,128)(2,1)S(1)}, u32[]{:S(2)}, u32[]{:S(2)}) collective-permute-start(bf16[1024,256]{1,0:T(8,128)(2,1)S(1)} %get-tuple-element.9), channel_id=1, source_target_pairs={{0,4},{1,5},{2,6},{3,7},{4,0},{5,1},{6,2},{7,3},{8,12},{9,13},{10,... | collective-permute-start | bytes 1572872 | tf_op jit(solution)/shard_map/ppermute | solution.py:425
  27.7 1.5 %collective-permute-start.7 = (bf16[1024,256]{1,0:T(8,128)(2,1)S(1)}, bf16[1024,256]{1,0:T(8,128)(2,1)}, u32[]{:S(2)}, u32[]{:S(2)}) collective-permute-start(bf16[1024,256]{1,0:T(8,128)(2,1)S(1)} %get-tuple-element.9), channel_id=1, source_target_pairs={{0,2},{1,3},{2,0},{3,1},{4,6},{5,7},{6,4},{7,5},{8,10},{9,11},{10,... | collective-permute-start | bytes 1572872 | tf_op jit(solution)/shard_map/ppermute | solution.py:425
  29.7 11.5 %attend.2 = bf16[8,208,128]{2,1,0:T(8,128)(2,1)} custom-call(bf16[8,192,128]{2,1,0:T(8,128)(2,1)S(1)} %all-to-all-done.queries, bf16[4096,512]{1,0:T(8,128)(2,1)} %keys.3, bf16[4096,512]{1,0:T(8,128)(2,1)} %values.3), custom_call_target="tpu_custom_call" | custom-call | flops 3221225472 | bytes 8388608 | tf_op jit(solution)/shard_map/attend/pallas_call | solution.py:361
  41.3 4.2 %all-to-all-start.1 = ((bf16[8,208,128]{2,1,0:T(8,128)(2,1)}), bf16[8,208,128]{2,1,0:T(8,128)(2,1)S(1)}, u32[]{:S(2)}, u32[]{:S(2)}) async-start(bf16[8,208,128]{2,1,0:T(8,128)(2,1)} %attend.2), calls=%async_computation.1 | async-start | bytes 851968 | tf_op jit(solution)/shard_map/all_to_all | solution.py:356
  46.1 1.6 %collective-permute-start.15 = (bf16[1024,256]{1,0:T(8,128)(2,1)}, bf16[1024,256]{1,0:T(8,128)(2,1)}, u32[]{:S(2)}, u32[]{:S(2)}) collective-permute-start(bf16[1024,256]{1,0:T(8,128)(2,1)} %collective-permute-done.7.refs_4_), channel_id=1, source_target_pairs={{0,4},{1,5},{2,6},{3,7},{4,0},{5,1},{6,2},{7,3},{8,12},{9,13},{10,... | collective-permute-start | bytes 1572872 | tf_op jit(solution)/shard_map/ppermute | solution.py:425
  47.8 6.4 %collective-permute-done.9.refs_6_ = bf16[1024,256]{1,0:T(8,128)(2,1)} collective-permute-done((bf16[1024,256]{1,0:T(8,128)(2,1)}, bf16[1024,256]{1,0:T(8,128)(2,1)}, u32[]{:S(2)}, u32[]{:S(2)}) %collective-permute-start.9) | collective-permute-done | bytes 524320 | tf_op jit(solution)/shard_map/ppermute | solution.py:425
  54.2 1.5 %collective-permute-start.13 = (bf16[1024,256]{1,0:T(8,128)(2,1)}, bf16[1024,256]{1,0:T(8,128)(2,1)}, u32[]{:S(2)}, u32[]{:S(2)}) collective-permute-start(bf16[1024,256]{1,0:T(8,128)(2,1)} %collective-permute-done.9.refs_6_), channel_id=1, source_target_pairs={{0,2},{1,3},{2,0},{3,1},{4,6},{5,7},{6,4},{7,5},{8,10},{9,11},{10,... | collective-permute-start | bytes 1572872 | tf_op jit(solution)/shard_map/ppermute | solution.py:425
  55.7 10.8 %attend.3 = bf16[8,208,128]{2,1,0:T(8,128)(2,1)S(1)} custom-call(bf16[8,192,128]{2,1,0:T(8,128)(2,1)S(1)} %all-to-all-done.2.queries, bf16[4096,512]{1,0:T(8,128)(2,1)} %keys.3, bf16[4096,512]{1,0:T(8,128)(2,1)} %values.3), custom_call_target="tpu_custom_call" | custom-call | flops 3221225472 | bytes 8388608 | tf_op jit(solution)/shard_map/attend/pallas_call | solution.py:361
  66.5 0.8 copy-done.6
  67.3 3.5 %all-to-all-start.3 = ((bf16[8,208,128]{2,1,0:T(8,128)(2,1)}), bf16[8,208,128]{2,1,0:T(8,128)(2,1)S(1)}, u32[]{:S(2)}, u32[]{:S(2)}) async-start(bf16[8,208,128]{2,1,0:T(8,128)(2,1)} %copy-done.6), calls=%async_computation.3 | async-start | bytes 851968 | tf_op jit(solution)/shard_map/all_to_all | solution.py:356
  71.9 0.9 copy-done.5
  72.8 1.8 %merge.2.own_a = bf16[528,128]{1,0:T(8,128)(2,1)S(1)} custom-call(s32[1]{0:T(128)} %bitcast.1.base, s32[3,8]{1,0:T(4,128)S(1)} %bitcast.6, bf16[32,2048]{1,0:T(8,128)(2,1)S(1)} %copy-done.5, bf16[32,512]{1,0:T(8,128)(2,1)S(1)} %copy-done.7, bf16[32,512]{1,0:T(8,128)(2,1)S(1)} %copy-done.8, bf16[8,208,128]{2,1,0:T(8,128)(2,1)S(1)} %all-to-all-done.1.refs_3_), custom_call_target="tpu_custom_call" | custom-call | tf_op jit(solution)/shard_map/merge/pallas_call | solution.py:384
  74.6 0.8 copy-done.3
  75.4 1.3 %collective-permute-start.3 = (bf16[528,128]{1,0:T(8,128)(2,1)S(1)}, bf16[528,128]{1,0:T(8,128)(2,1)S(1)}, u32[]{:S(2)}, u32[]{:S(2)}) collective-permute-start(bf16[528,128]{1,0:T(8,128)(2,1)S(1)} %merge.2.own_a), channel_id=1, source_target_pairs={{0,8},{1,9},{2,10},{3,11},{4,12},{5,13},{6,14},{7,15},{8,0},{9,1},... | collective-permute-start | bytes 405512 | tf_op jit(solution)/shard_map/ppermute | solution.py:343
  76.7 1.8 %all-to-all-done.3.refs_0_ = bf16[8,208,128]{2,1,0:T(8,128)(2,1)S(1)} async-done(((bf16[8,208,128]{2,1,0:T(8,128)(2,1)}), bf16[8,208,128]{2,1,0:T(8,128)(2,1)S(1)}, u32[]{:S(2)}, u32[]{:S(2)}) %all-to-all-start.3) | async-done | bytes 426016 | tf_op jit(solution)/shard_map/all_to_all | solution.py:356
  78.5 1.0 merge.3.other_b
  79.5 1.4 %collective-permute-start.2 = (bf16[528,128]{1,0:T(8,128)(2,1)S(1)}, bf16[528,128]{1,0:T(8,128)(2,1)S(1)}, u32[]{:S(2)}, u32[]{:S(2)}) collective-permute-start(bf16[528,128]{1,0:T(8,128)(2,1)S(1)} %merge.3.other_b), channel_id=1, source_target_pairs={{0,8},{1,9},{2,10},{3,11},{4,12},{5,13},{6,14},{7,15},{8,0},{9,1},... | collective-permute-start | bytes 405512 | tf_op jit(solution)/shard_map/ppermute | solution.py:343
  80.9 7.7 %collective-permute-done.3.other_a = bf16[528,128]{1,0:T(8,128)(2,1)S(1)} collective-permute-done((bf16[528,128]{1,0:T(8,128)(2,1)S(1)}, bf16[528,128]{1,0:T(8,128)(2,1)S(1)}, u32[]{:S(2)}, u32[]{:S(2)}) %collective-permute-start.3) | collective-permute-done | bytes 135200 | tf_op jit(solution)/shard_map/ppermute | solution.py:343
  88.6 2.3 %collective-permute-done.2.own_b = bf16[528,128]{1,0:T(8,128)(2,1)S(1)} collective-permute-done((bf16[528,128]{1,0:T(8,128)(2,1)S(1)}, bf16[528,128]{1,0:T(8,128)(2,1)S(1)}, u32[]{:S(2)}, u32[]{:S(2)}) %collective-permute-start.2) | collective-permute-done | bytes 135200 | tf_op jit(solution)/shard_map/ppermute | solution.py:343
  90.8 1.0 copy-done.2
  91.9 1.0 copy-done.4
  92.9 4.2 %project.1 = (bf16[32,2048]{1,0:T(8,128)(2,1)S(1)}, bf16[32,2048]{1,0:T(8,128)(2,1)S(1)}) custom-call(bf16[528,128]{1,0:T(8,128)(2,1)S(1)} %merge.2.own_a, bf16[528,128]{1,0:T(8,128)(2,1)S(1)} %collective-permute-done.2.own_b, bf16[528,128]{1,0:T(8,128)(2,1)S(1)} %collective-permute-done.3.other_a, bf16[528,128]{1,0:T(8,128)(2,1)S(1)} %merge.3.other_b, ...), custom_call_target="tpu_custom_call" | custom-call | tf_op jit(solution)/shard_map/project/pallas_call | solution.py:447
  97.2 8.6 %collective-permute-done.17.received = bf16[32,2048]{1,0:T(8,128)(2,1)S(1)} collective-permute-done((bf16[32,2048]{1,0:T(8,128)(2,1)S(1)}, bf16[32,2048]{1,0:T(8,128)(2,1)S(1)}, u32[]{:S(2)}, u32[]{:S(2)}) %collective-permute-start.17) | collective-permute-done | bytes 131104 | tf_op jit(solution)/shard_map/ppermute | solution.py:343
  105.8 0.7 place.1
  (41 shorter events, 2.8 us)
Async XLA Ops:
  2.1 15.5 %all-to-all-start = ((bf16[8,192,128]{2,1,0:T(8,128)(2,1)}), bf16[8,192,128]{2,1,0:T(8,128)(2,1)S(1)}, u32[]{:S(2)}, u32[]{:S(2)}) async-start(bf16[8,192,128]{2,1,0:T(8,128)(2,1)} %pack.2), calls=%async_computation | async-start | bytes 786432 | tf_op jit(solution)/shard_map/all_to_all | solution.py:356
  7.4 8.3 %collective-permute-start.1 = (bf16[32,2048]{1,0:T(8,128)(2,1)}, bf16[32,2048]{1,0:T(8,128)(2,1)S(1)}, u32[]{:S(2)}, u32[]{:S(2)}) collective-permute-start(bf16[32,2048]{1,0:T(8,128)(2,1)} %refs_0_.2), channel_id=1, source_target_pairs={{0,8},{1,9},{2,10},{3,11},{4,12},{5,13},{6,14},{7,15},{8,0},{9,1},... | collective-permute-start | bytes 393224 | tf_op jit(solution)/shard_map/ppermute | solution.py:343
  10.0 5.7 %collective-permute-start = (s32[3,8]{1,0:T(4,128)}, s32[3,8]{1,0:T(4,128)S(1)}, u32[]{:S(2)}, u32[]{:S(2)}) collective-permute-start(s32[3,8]{1,0:T(4,128)} %bitcast.5), channel_id=1, source_target_pairs={{0,8},{1,9},{2,10},{3,11},{4,12},{5,13},{6,14},{7,15},{8,0},{9,1},... | collective-permute-start | bytes 296 | tf_op jit(solution)/shard_map/ppermute | solution.py:343
  17.6 23.7 %all-to-all-start.2 = ((bf16[8,192,128]{2,1,0:T(8,128)(2,1)}), bf16[8,192,128]{2,1,0:T(8,128)(2,1)S(1)}, u32[]{:S(2)}, u32[]{:S(2)}) async-start(bf16[8,192,128]{2,1,0:T(8,128)(2,1)} %pack.3), calls=%async_computation.2 | async-start | bytes 786432 | tf_op jit(solution)/shard_map/all_to_all | solution.py:356
  25.7 19.8 %collective-permute-start.11 = (bf16[1024,256]{1,0:T(8,128)(2,1)S(1)}, bf16[1024,256]{1,0:T(8,128)(2,1)S(1)}, u32[]{:S(2)}, u32[]{:S(2)}) collective-permute-start(bf16[1024,256]{1,0:T(8,128)(2,1)S(1)} %get-tuple-element.9), channel_id=1, source_target_pairs={{0,4},{1,5},{2,6},{3,7},{4,0},{5,1},{6,2},{7,3},{8,12},{9,13},{10,... | collective-permute-start | bytes 1572872 | tf_op jit(solution)/shard_map/ppermute | solution.py:425
  27.7 18.4 %collective-permute-start.7 = (bf16[1024,256]{1,0:T(8,128)(2,1)S(1)}, bf16[1024,256]{1,0:T(8,128)(2,1)}, u32[]{:S(2)}, u32[]{:S(2)}) collective-permute-start(bf16[1024,256]{1,0:T(8,128)(2,1)S(1)} %get-tuple-element.9), channel_id=1, source_target_pairs={{0,2},{1,3},{2,0},{3,1},{4,6},{5,7},{6,4},{7,5},{8,10},{9,11},{10,... | collective-permute-start | bytes 1572872 | tf_op jit(solution)/shard_map/ppermute | solution.py:425
  29.2 18.6 %copy-start = (bf16[2048,256]{1,0:T(8,128)(2,1)S(1)}, bf16[2048,256]{1,0:T(8,128)(2,1)}, u32[]{:S(2)}) copy-start(bf16[2048,256]{1,0:T(8,128)(2,1)} %refs_0_.3) | copy-start | bytes 3145732
  29.2 25.0 %collective-permute-start.9 = (bf16[1024,256]{1,0:T(8,128)(2,1)}, bf16[1024,256]{1,0:T(8,128)(2,1)}, u32[]{:S(2)}, u32[]{:S(2)}) collective-permute-start(bf16[1024,256]{1,0:T(8,128)(2,1)} %get-tuple-element.10), channel_id=1, source_target_pairs={{0,4},{1,5},{2,6},{3,7},{4,0},{5,1},{6,2},{7,3},{8,12},{9,13},{10,... | collective-permute-start | bytes 1572872 | tf_op jit(solution)/shard_map/ppermute | solution.py:425
  29.7 24.5 %collective-permute-start.5 = (bf16[1024,256]{1,0:T(8,128)(2,1)}, bf16[1024,256]{1,0:T(8,128)(2,1)}, u32[]{:S(2)}, u32[]{:S(2)}) collective-permute-start(bf16[1024,256]{1,0:T(8,128)(2,1)} %get-tuple-element.10), channel_id=1, source_target_pairs={{0,2},{1,3},{2,0},{3,1},{4,6},{5,7},{6,4},{7,5},{8,10},{9,11},{10,... | collective-permute-start | bytes 1572872 | tf_op jit(solution)/shard_map/ppermute | solution.py:425
  41.3 26.0 %all-to-all-start.1 = ((bf16[8,208,128]{2,1,0:T(8,128)(2,1)}), bf16[8,208,128]{2,1,0:T(8,128)(2,1)S(1)}, u32[]{:S(2)}, u32[]{:S(2)}) async-start(bf16[8,208,128]{2,1,0:T(8,128)(2,1)} %attend.2), calls=%async_computation.1 | async-start | bytes 851968 | tf_op jit(solution)/shard_map/all_to_all | solution.py:356
  45.5 26.4 %copy-start.7 = (bf16[32,512]{1,0:T(8,128)(2,1)S(1)}, bf16[32,512]{1,0:T(8,128)(2,1)}, u32[]{:S(2)}) copy-start(bf16[32,512]{1,0:T(8,128)(2,1)} %refs_1_.1) | copy-start | bytes 98308
  45.5 26.4 %copy-start.8 = (bf16[32,512]{1,0:T(8,128)(2,1)S(1)}, bf16[32,512]{1,0:T(8,128)(2,1)}, u32[]{:S(2)}) copy-start(bf16[32,512]{1,0:T(8,128)(2,1)} %refs_2_.1) | copy-start | bytes 98308
  45.5 26.4 %copy-start.9 = (s32[8,3]{0,1:T(4,128)S(1)}, s32[8,3]{0,1:T(4,128)}, u32[]{:S(2)}) copy-start(s32[8,3]{0,1:T(4,128)} %param.12) | copy-start | bytes 292
  45.5 21.0 %copy-start.1 = (bf16[1024,256]{1,0:T(8,128)(2,1)}, bf16[1024,256]{1,0:T(8,128)(2,1)S(1)}, u32[]{:S(2)}) copy-start(bf16[1024,256]{1,0:T(8,128)(2,1)S(1)} %collective-permute-done.11.refs_8_) | copy-start | bytes 1572868
  45.5 25.2 %collective-permute-start.12 = (bf16[1024,256]{1,0:T(8,128)(2,1)S(1)}, bf16[1024,256]{1,0:T(8,128)(2,1)}, u32[]{:S(2)}, u32[]{:S(2)}) collective-permute-start(bf16[1024,256]{1,0:T(8,128)(2,1)S(1)} %collective-permute-done.11.refs_8_), channel_id=1, source_target_pairs={{0,1},{1,0},{2,3},{3,2},{4,5},{5,4},{6,7},{7,6},{8,9},{9,8},{10,11... | collective-permute-start | bytes 1572872 | tf_op jit(solution)/shard_map/ppermute | solution.py:425
  46.1 25.1 %collective-permute-start.15 = (bf16[1024,256]{1,0:T(8,128)(2,1)}, bf16[1024,256]{1,0:T(8,128)(2,1)}, u32[]{:S(2)}, u32[]{:S(2)}) collective-permute-start(bf16[1024,256]{1,0:T(8,128)(2,1)} %collective-permute-done.7.refs_4_), channel_id=1, source_target_pairs={{0,4},{1,5},{2,6},{3,7},{4,0},{5,1},{6,2},{7,3},{8,12},{9,13},{10,... | collective-permute-start | bytes 1572872 | tf_op jit(solution)/shard_map/ppermute | solution.py:425
  47.7 33.2 %collective-permute-start.4 = (bf16[2048,256]{1,0:T(8,128)(2,1)S(1)}, bf16[2048,256]{1,0:T(8,128)(2,1)S(1)}, u32[]{:S(2)}, u32[]{:S(2)}) collective-permute-start(bf16[2048,256]{1,0:T(8,128)(2,1)S(1)} %copy-done), channel_id=1, source_target_pairs={{0,1},{1,0},{2,3},{3,2},{4,5},{5,4},{6,7},{7,6},{8,9},{9,8},{10,11... | collective-permute-start | bytes 3145736 | tf_op jit(solution)/shard_map/ppermute | solution.py:425
  54.2 17.1 %collective-permute-start.8 = (bf16[1024,256]{1,0:T(8,128)(2,1)}, bf16[1024,256]{1,0:T(8,128)(2,1)}, u32[]{:S(2)}, u32[]{:S(2)}) collective-permute-start(bf16[1024,256]{1,0:T(8,128)(2,1)} %collective-permute-done.7.refs_4_), channel_id=1, source_target_pairs={{0,1},{1,0},{2,3},{3,2},{4,5},{5,4},{6,7},{7,6},{8,9},{9,8},{10,11... | collective-permute-start | bytes 1572872 | tf_op jit(solution)/shard_map/ppermute | solution.py:425
  54.2 17.5 %collective-permute-start.13 = (bf16[1024,256]{1,0:T(8,128)(2,1)}, bf16[1024,256]{1,0:T(8,128)(2,1)}, u32[]{:S(2)}, u32[]{:S(2)}) collective-permute-start(bf16[1024,256]{1,0:T(8,128)(2,1)} %collective-permute-done.9.refs_6_), channel_id=1, source_target_pairs={{0,2},{1,3},{2,0},{3,1},{4,6},{5,7},{6,4},{7,5},{8,10},{9,11},{10,... | collective-permute-start | bytes 1572872 | tf_op jit(solution)/shard_map/ppermute | solution.py:425
  66.5 0.8 copy-start.6
  67.3 11.2 %all-to-all-start.3 = ((bf16[8,208,128]{2,1,0:T(8,128)(2,1)}), bf16[8,208,128]{2,1,0:T(8,128)(2,1)S(1)}, u32[]{:S(2)}, u32[]{:S(2)}) async-start(bf16[8,208,128]{2,1,0:T(8,128)(2,1)} %copy-done.6), calls=%async_computation.3 | async-start | bytes 851968 | tf_op jit(solution)/shard_map/all_to_all | solution.py:356
  70.8 3.8 %collective-permute-start.10 = (bf16[1024,256]{1,0:T(8,128)(2,1)}, bf16[1024,256]{1,0:T(8,128)(2,1)S(1)}, u32[]{:S(2)}, u32[]{:S(2)}) collective-permute-start(bf16[1024,256]{1,0:T(8,128)(2,1)} %collective-permute-done.9.refs_6_), channel_id=1, source_target_pairs={{0,1},{1,0},{2,3},{3,2},{4,5},{5,4},{6,7},{7,6},{8,9},{9,8},{10,11... | collective-permute-start | bytes 1572872 | tf_op jit(solution)/shard_map/ppermute | solution.py:425
  71.2 8.4 %collective-permute-start.6 = (bf16[1024,256]{1,0:T(8,128)(2,1)}, bf16[1024,256]{1,0:T(8,128)(2,1)}, u32[]{:S(2)}, u32[]{:S(2)}) collective-permute-start(bf16[1024,256]{1,0:T(8,128)(2,1)} %collective-permute-done.5.refs_2_), channel_id=1, source_target_pairs={{0,1},{1,0},{2,3},{3,2},{4,5},{5,4},{6,7},{7,6},{8,9},{9,8},{10,11... | collective-permute-start | bytes 1572872 | tf_op jit(solution)/shard_map/ppermute | solution.py:425
  71.4 17.2 %collective-permute-start.16 = (bf16[1024,256]{1,0:T(8,128)(2,1)}, bf16[1024,256]{1,0:T(8,128)(2,1)}, u32[]{:S(2)}, u32[]{:S(2)}) collective-permute-start(bf16[1024,256]{1,0:T(8,128)(2,1)} %collective-permute-done.15.refs_12_), channel_id=1, source_target_pairs={{0,1},{1,0},{2,3},{3,2},{4,5},{5,4},{6,7},{7,6},{8,9},{9,8},{10,11... | collective-permute-start | bytes 1572872 | tf_op jit(solution)/shard_map/ppermute | solution.py:425
  71.7 16.9 %collective-permute-start.14 = (bf16[1024,256]{1,0:T(8,128)(2,1)}, bf16[1024,256]{1,0:T(8,128)(2,1)}, u32[]{:S(2)}, u32[]{:S(2)}) collective-permute-start(bf16[1024,256]{1,0:T(8,128)(2,1)} %collective-permute-done.13.refs_10_), channel_id=1, source_target_pairs={{0,1},{1,0},{2,3},{3,2},{4,5},{5,4},{6,7},{7,6},{8,9},{9,8},{10,11... | collective-permute-start | bytes 1572872 | tf_op jit(solution)/shard_map/ppermute | solution.py:425
  71.9 0.9 copy-start.5
  74.6 0.8 copy-start.3
  75.4 13.2 %collective-permute-start.3 = (bf16[528,128]{1,0:T(8,128)(2,1)S(1)}, bf16[528,128]{1,0:T(8,128)(2,1)S(1)}, u32[]{:S(2)}, u32[]{:S(2)}) collective-permute-start(bf16[528,128]{1,0:T(8,128)(2,1)S(1)} %merge.2.own_a), channel_id=1, source_target_pairs={{0,8},{1,9},{2,10},{3,11},{4,12},{5,13},{6,14},{7,15},{8,0},{9,1},... | collective-permute-start | bytes 405512 | tf_op jit(solution)/shard_map/ppermute | solution.py:343
  79.5 11.3 %collective-permute-start.2 = (bf16[528,128]{1,0:T(8,128)(2,1)S(1)}, bf16[528,128]{1,0:T(8,128)(2,1)S(1)}, u32[]{:S(2)}, u32[]{:S(2)}) collective-permute-start(bf16[528,128]{1,0:T(8,128)(2,1)S(1)} %merge.3.other_b), channel_id=1, source_target_pairs={{0,8},{1,9},{2,10},{3,11},{4,12},{5,13},{6,14},{7,15},{8,0},{9,1},... | collective-permute-start | bytes 405512 | tf_op jit(solution)/shard_map/ppermute | solution.py:343
  90.8 1.0 copy-start.2
  91.9 1.0 copy-start.4
  97.1 8.6 %collective-permute-start.17 = (bf16[32,2048]{1,0:T(8,128)(2,1)S(1)}, bf16[32,2048]{1,0:T(8,128)(2,1)S(1)}, u32[]{:S(2)}, u32[]{:S(2)}) collective-permute-start(bf16[32,2048]{1,0:T(8,128)(2,1)S(1)} %get-tuple-element.8), channel_id=1, source_target_pairs={{0,8},{1,9},{2,10},{3,11},{4,12},{5,13},{6,14},{7,15},{8,0},{9,1},... | collective-permute-start | bytes 393224 | tf_op jit(solution)/shard_map/ppermute | solution.py:343

commit v6 on v5

--- a/solution.py
+++ b/solution.py
@@ -275,26 +275,19 @@
     attended[...] = combine(tall, first, second)
 
 
-def project_kernel(count, places, own_a, own_b, other_a, other_b, me, *refs):
-    weights = refs[: len(places)]
-    own_out, other_out = refs[len(places) :]
+def project_kernel(own_a, own_b, other_a, other_b, places, *refs):
+    weights = refs[:-2]
+    own_out, other_out = refs[-2:]
     width = weights[0].shape[1]
     tall = (own_a.shape[0] - STAT_ROWS) // KVH
     rows = tall // GROUP
     left = jnp.concatenate(
         [combine(tall, own_a, own_b), combine(tall, other_a, other_b)], axis=0
     )
-    for k in range(count):
-        made = sum(
-            jnp.dot(
-                left[:, start : start + weights[i].shape[0]],
-                weights[i][...],
-                preferred_element_type=jnp.float32,
-            )
-            for i, (shard, start) in enumerate(places)
-            if shard == k
-        ).astype(jnp.bfloat16)
-        at = pl.ds(pl.multiple_of((me[0] ^ k) * width, width), width)
+    for i, weight in enumerate(weights):
+        made = jnp.dot(left, weight[...], preferred_element_type=jnp.float32)
+        made = made.astype(jnp.bfloat16)
+        at = pl.ds(pl.multiple_of(places[i] * width, width), width)
         own_out[:, at] = made[:rows, :]
         other_out[:, at] = made[rows:, :]
 
@@ -318,10 +311,6 @@
 
 def in_hbm(array):
     return pltpu.with_memory_space_constraint(array, pltpu.HBM)
-
-
-def early_first(step):
-    return (1, 0) if step == 2 else (0, 1)
 
 
 def shards(queries, new_keys, new_values, keys, values, page_list, out_weight):
@@ -421,37 +410,41 @@
             preferred_element_type=jnp.float32,
         ).astype(jnp.bfloat16)
 
-    def exchanged(array, step):
-        return lax.ppermute(array, "seq", [(i, i ^ step) for i in range(members)])
-
-    middle = features // 2
-    halves_of = [out_weight[:middle, :], out_weight[middle:, :]]
-    pieces = {0: [out_weight]}
-    for step in range(2, half, 2):
-        low = step & -step
-        if low == step:
-            pieces[step] = [None, None]
-            for i in early_first(step):
-                pieces[step][i] = exchanged(halves_of[i], step)
-    for step in range(2, half, 2):
-        low = step & -step
-        if low != step:
-            first_piece = exchanged(pieces[step ^ low][0], low)
-            pieces[step] = [first_piece, exchanged(pieces[low][1], step ^ low)]
+    def exchanged(array, even_step, odd_step):
+        return lax.ppermute(
+            array,
+            "seq",
+            [(i, i ^ (odd_step if i & 1 else even_step)) for i in range(members)],
+        )
+
+    steps = [(0, 0)]
+    arrays = [out_weight]
+    if half == 8:
+        arrays.append(exchanged(out_weight, 2, 4))
+        arrays.append(exchanged(out_weight, 4, 2))
+        arrays.append(exchanged(arrays[1], 4, 2))
+        steps += [(2, 4), (4, 2), (6, 6)]
+    else:
+        for step in range(2, half, 2):
+            arrays.append(exchanged(out_weight, step, step))
+            steps.append((step, step))
     gathered = []
     places = []
-    for step, parts in pieces.items():
-        for i, part in enumerate(parts):
-            gathered += [part, exchanged(part, 1)]
-            places += [(step, i * middle), (step + 1, i * middle)]
+    for array, (even, odd) in zip(arrays, steps):
+        gathered += [array, exchanged(array, 1, 1)]
+        places += [(even, odd), (odd ^ 1, even ^ 1)]
+    odd_core = me % 2
+    places = jnp.stack(
+        [(me % half) ^ (even + odd_core * (odd - even)) for even, odd in places]
+    ).astype(jnp.int32)
     own_out, other_out = pl.pallas_call(
-        functools.partial(project_kernel, half, tuple(places)),
+        project_kernel,
         out_shape=[jax.ShapeDtypeStruct((row_total, half * width), jnp.bfloat16)] * 2,
-        in_specs=[VMEM] * 4 + [SMEM] + [VMEM] * len(places),
+        in_specs=[VMEM] * 4 + [SMEM] + [VMEM] * half,
         out_specs=[VMEM, VMEM],
         compiler_params=PROJECT,
         name="project",
-    )(own_a, own_b, other_a, other_b, (me % half).reshape(1), *[on_chip(part) for part in gathered])
+    )(own_a, own_b, other_a, other_b, places, *[on_chip(part) for part in gathered])
     received = mirrored(other_out)
     return pl.pallas_call(
         place_kernel,

time: 107 us -> 108 us (level)
  waiting for transfers between devices: 32.9 us -> 47.4 us
  starting transfers between devices: 33.5 us -> 25.7 us
  local copies, waits for them, and re-layouts: 6.64 us -> 0.87 us
    all_to_all x4, waiting for transfers between devices: 2.53 us -> 11.9 us  [spread(): lax.all_to_all(array, 'seq', split_axis=0, concat_axis=0, tiled=True, axi...]
    ppermute x13 -> x7, waiting for transfers between devices: 6.41 us -> 13.8 us  [exchanged(): lax.ppermute(array, 'seq', [(i, i ^ (odd_step if i & 1 else even_step)) f...]
    unnamed x20 -> x12, local copies, waits for them, and re-layouts: 4.57 us -> 0.79 us
    ppermute x13 -> x7, starting transfers between devices: 8.91 us -> 5.9 us  [exchanged(): lax.ppermute(array, 'seq', [(i, i ^ (odd_step if i & 1 else even_step)) f...]
    all_to_all x4, starting transfers between devices: 18.9 us -> 16.3 us  [spread(): lax.all_to_all(array, 'seq', split_axis=0, concat_axis=0, tiled=True, axi...]
    ppermute x5, waiting for transfers between devices: 23.9 us -> 21.7 us  [mirrored(): lax.ppermute(array, 'seq', [(i, (i + half) % members) for i in range(memb...]
    ppermute x5, starting transfers between devices: 5.63 us -> 3.49 us  [mirrored(): lax.ppermute(array, 'seq', [(i, (i + half) % members) for i in range(memb...]
    slice x1 -> x0, local copies, waits for them, and re-layouts: 2.07 us -> none  [shards(): halves_of = [out_weight[:middle, :], out_weight[middle:, :]]]
  transfers between devices with their start and end apart: 22 -> 16, of which waited for: 7 -> 8; matrix products, arithmetic and copies ran while one was open for 2% -> 0% of each run, Pallas kernels for 25% -> 26%
where the time goes in v6:
time: 108 us
  waiting for transfers between devices  47.4 us (44%)
  Pallas kernels  33.8 us (31%)
  starting transfers between devices  25.7 us (24%)
    pallas_call x2, Pallas kernels, attend(): pl.pallas_call(attend_kernel, out_shape=jax.ShapeDtypeStruct((half, KVH *...  22.3 us
    ppermute x5, waiting for transfers between devices, mirrored(): lax.ppermute(array, 'seq', [(i, (i + half) % members) for i in range(memb...  21.7 us
    all_to_all x4, starting transfers between devices, spread(): lax.all_to_all(array, 'seq', split_axis=0, concat_axis=0, tiled=True, axi...  16.3 us
    ppermute x7, waiting for transfers between devices, exchanged(): lax.ppermute(array, 'seq', [(i, i ^ (odd_step if i & 1 else even_step)) f...  13.8 us
    all_to_all x4, waiting for transfers between devices, spread(): lax.all_to_all(array, 'seq', split_axis=0, concat_axis=0, tiled=True, axi...  11.9 us
    ppermute x7, starting transfers between devices, exchanged(): lax.ppermute(array, 'seq', [(i, i ^ (odd_step if i & 1 else even_step)) f...  5.9 us
    pallas_call x1, Pallas kernels, shards(): pl.pallas_call(project_kernel, out_shape=[jax.ShapeDtypeStruct((row_total...  4.58 us
    ppermute x5, starting transfers between devices, mirrored(): lax.ppermute(array, 'seq', [(i, (i + half) % members) for i in range(memb...  3.49 us
  transfers between devices with their start and end apart: 16, of which 8 were waited for; matrix products, arithmetic and copies ran while one was open for 0% of the time, Pallas kernels for 26%

profile of v6, /device:TPU:0, one launch (start us, length us, event | category | flops | bytes accessed | tf_op | source)
XLA Modules:
  0.0 107.9 jit_solution(2800428104562378841)
XLA Ops:
  0.0 3.0 %collective-permute-start.5 = (bf16[2048,256]{1,0:T(8,128)(2,1)}, bf16[2048,256]{1,0:T(8,128)(2,1)S(1)}, u32[]{:S(2)}, u32[]{:S(2)}) collective-permute-start(bf16[2048,256]{1,0:T(8,128)(2,1)} %refs_0_.3), channel_id=1, source_target_pairs={{0,2},{1,5},{2,0},{3,7},{4,6},{5,1},{6,4},{7,3},{8,10},{9,13},{10,... | collective-permute-start | bytes 3145736 | tf_op jit(solution)/shard_map/ppermute | solution.py:414
  3.0 2.1 %pack.2 = bf16[8,192,128]{2,1,0:T(8,128)(2,1)} custom-call(s32[1]{0:T(128)} %bitcast.1.base, s32[3,8]{1,0:T(4,128)} %bitcast.11, bf16[32,2048]{1,0:T(8,128)(2,1)} %refs_0_.2), custom_call_target="tpu_custom_call" | custom-call | tf_op jit(solution)/shard_map/pack/pallas_call | solution.py:335
  5.1 3.5 %all-to-all-start = ((bf16[8,192,128]{2,1,0:T(8,128)(2,1)}), bf16[8,192,128]{2,1,0:T(8,128)(2,1)S(1)}, u32[]{:S(2)}, u32[]{:S(2)}) async-start(bf16[8,192,128]{2,1,0:T(8,128)(2,1)} %pack.2), calls=%async_computation | async-start | bytes 786432 | tf_op jit(solution)/shard_map/all_to_all | solution.py:345
  8.5 2.7 %collective-permute-start.1 = (bf16[32,2048]{1,0:T(8,128)(2,1)}, bf16[32,2048]{1,0:T(8,128)(2,1)S(1)}, u32[]{:S(2)}, u32[]{:S(2)}) collective-permute-start(bf16[32,2048]{1,0:T(8,128)(2,1)} %refs_0_.2), channel_id=1, source_target_pairs={{0,8},{1,9},{2,10},{3,11},{4,12},{5,13},{6,14},{7,15},{8,0},{9,1},... | collective-permute-start | bytes 393224 | tf_op jit(solution)/shard_map/ppermute | solution.py:332
  11.2 0.3 collective-permute-start
  11.5 5.4 %collective-permute-done.listed = s32[3,8]{1,0:T(4,128)S(1)} collective-permute-done((s32[3,8]{1,0:T(4,128)}, s32[3,8]{1,0:T(4,128)S(1)}, u32[]{:S(2)}, u32[]{:S(2)}) %collective-permute-start) | collective-permute-done | bytes 128 | tf_op jit(solution)/shard_map/ppermute | solution.py:332
  16.9 1.2 %pack.3 = bf16[8,192,128]{2,1,0:T(8,128)(2,1)} custom-call(s32[1]{0:T(128)} %bitcast.1.base, s32[3,8]{1,0:T(4,128)S(1)} %collective-permute-done.listed, bf16[32,2048]{1,0:T(8,128)(2,1)S(1)} %collective-permute-done.1.queries), custom_call_target="tpu_custom_call" | custom-call | tf_op jit(solution)/shard_map/pack/pallas_call | solution.py:335
  18.1 4.8 %all-to-all-done.queries = bf16[8,192,128]{2,1,0:T(8,128)(2,1)S(1)} async-done(((bf16[8,192,128]{2,1,0:T(8,128)(2,1)}), bf16[8,192,128]{2,1,0:T(8,128)(2,1)S(1)}, u32[]{:S(2)}, u32[]{:S(2)}) %all-to-all-start) | async-done | bytes 393248 | tf_op jit(solution)/shard_map/all_to_all | solution.py:345
  22.8 5.0 %all-to-all-start.2 = ((bf16[8,192,128]{2,1,0:T(8,128)(2,1)}), bf16[8,192,128]{2,1,0:T(8,128)(2,1)S(1)}, u32[]{:S(2)}, u32[]{:S(2)}) async-start(bf16[8,192,128]{2,1,0:T(8,128)(2,1)} %pack.3), calls=%async_computation.2 | async-start | bytes 786432 | tf_op jit(solution)/shard_map/all_to_all | solution.py:345
  27.9 2.0 %collective-permute-start.7 = (bf16[2048,256]{1,0:T(8,128)(2,1)}, bf16[2048,256]{1,0:T(8,128)(2,1)}, u32[]{:S(2)}, u32[]{:S(2)}) collective-permute-start(bf16[2048,256]{1,0:T(8,128)(2,1)} %refs_0_.3), channel_id=1, source_target_pairs={{0,4},{1,3},{2,6},{3,1},{4,0},{5,7},{6,2},{7,5},{8,12},{9,11},{10,... | collective-permute-start | bytes 3145736 | tf_op jit(solution)/shard_map/ppermute | solution.py:414
  29.9 0.1 collective-permute-start.9
  30.0 11.5 %attend.2 = bf16[8,208,128]{2,1,0:T(8,128)(2,1)} custom-call(bf16[8,192,128]{2,1,0:T(8,128)(2,1)S(1)} %all-to-all-done.queries, bf16[4096,512]{1,0:T(8,128)(2,1)} %keys.3, bf16[4096,512]{1,0:T(8,128)(2,1)} %values.3), custom_call_target="tpu_custom_call" | custom-call | flops 3221225472 | bytes 8388608 | tf_op jit(solution)/shard_map/attend/pallas_call | solution.py:350
  41.5 4.1 %all-to-all-start.1 = ((bf16[8,208,128]{2,1,0:T(8,128)(2,1)}), bf16[8,208,128]{2,1,0:T(8,128)(2,1)S(1)}, u32[]{:S(2)}, u32[]{:S(2)}) async-start(bf16[8,208,128]{2,1,0:T(8,128)(2,1)} %attend.2), calls=%async_computation.1 | async-start | bytes 851968 | tf_op jit(solution)/shard_map/all_to_all | solution.py:345
  45.7 0.6 collective-permute-start.4
  46.2 0.1 collective-permute-start.6
  46.3 0.3 collective-permute-done.7.refs_4_
  46.6 0.1 collective-permute-start.8
  46.7 13.4 %collective-permute-done.9.refs_6_ = bf16[2048,256]{1,0:T(8,128)(2,1)} collective-permute-done((bf16[2048,256]{1,0:T(8,128)(2,1)S(1)}, bf16[2048,256]{1,0:T(8,128)(2,1)}, u32[]{:S(2)}, u32[]{:S(2)}) %collective-permute-start.9) | collective-permute-done | bytes 1048608 | tf_op jit(solution)/shard_map/ppermute | solution.py:414
  60.2 10.8 %attend.3 = bf16[8,208,128]{2,1,0:T(8,128)(2,1)S(1)} custom-call(bf16[8,192,128]{2,1,0:T(8,128)(2,1)S(1)} %all-to-all-done.2.queries, bf16[4096,512]{1,0:T(8,128)(2,1)} %keys.3, bf16[4096,512]{1,0:T(8,128)(2,1)} %values.3), custom_call_target="tpu_custom_call" | custom-call | flops 3221225472 | bytes 8388608 | tf_op jit(solution)/shard_map/attend/pallas_call | solution.py:350
  71.0 0.8 copy-done.2
  71.8 3.7 %all-to-all-start.3 = ((bf16[8,208,128]{2,1,0:T(8,128)(2,1)}), bf16[8,208,128]{2,1,0:T(8,128)(2,1)S(1)}, u32[]{:S(2)}, u32[]{:S(2)}) async-start(bf16[8,208,128]{2,1,0:T(8,128)(2,1)} %copy-done.2), calls=%async_computation.3 | async-start | bytes 851968 | tf_op jit(solution)/shard_map/all_to_all | solution.py:345
  75.5 1.8 %merge.2.own_a = bf16[528,128]{1,0:T(8,128)(2,1)S(1)} custom-call(s32[1]{0:T(128)} %bitcast.1.base, s32[3,8]{1,0:T(4,128)S(1)} %bitcast.13, bf16[32,2048]{1,0:T(8,128)(2,1)S(1)} %copy-done.1, bf16[32,512]{1,0:T(8,128)(2,1)S(1)} %copy-done.3, bf16[32,512]{1,0:T(8,128)(2,1)S(1)} %copy-done.4, bf16[8,208,128]{2,1,0:T(8,128)(2,1)S(1)} %all-to-all-done.1.refs_3_), custom_call_target="tpu_custom_call" | custom-call | tf_op jit(solution)/shard_map/merge/pallas_call | solution.py:373
  77.4 0.4 collective-permute-start.3
  77.7 7.2 %all-to-all-done.3.refs_0_ = bf16[8,208,128]{2,1,0:T(8,128)(2,1)S(1)} async-done(((bf16[8,208,128]{2,1,0:T(8,128)(2,1)}), bf16[8,208,128]{2,1,0:T(8,128)(2,1)S(1)}, u32[]{:S(2)}, u32[]{:S(2)}) %all-to-all-start.3) | async-done | bytes 426016 | tf_op jit(solution)/shard_map/all_to_all | solution.py:345
  84.9 1.0 merge.3.other_b
  85.9 0.1 collective-permute-start.2
  86.0 0.1 stack.35.places
  86.1 1.1 %collective-permute-done.3.other_a = bf16[528,128]{1,0:T(8,128)(2,1)S(1)} collective-permute-done((bf16[528,128]{1,0:T(8,128)(2,1)S(1)}, bf16[528,128]{1,0:T(8,128)(2,1)S(1)}, u32[]{:S(2)}, u32[]{:S(2)}) %collective-permute-start.3) | collective-permute-done | bytes 135200 | tf_op jit(solution)/shard_map/ppermute | solution.py:332
  87.3 6.8 %collective-permute-done.2.own_b = bf16[528,128]{1,0:T(8,128)(2,1)S(1)} collective-permute-done((bf16[528,128]{1,0:T(8,128)(2,1)S(1)}, bf16[528,128]{1,0:T(8,128)(2,1)S(1)}, u32[]{:S(2)}, u32[]{:S(2)}) %collective-permute-start.2) | collective-permute-done | bytes 135200 | tf_op jit(solution)/shard_map/ppermute | solution.py:332
  94.1 4.6 %project.1 = (bf16[32,2048]{1,0:T(8,128)(2,1)S(1)}, bf16[32,2048]{1,0:T(8,128)(2,1)S(1)}) custom-call(bf16[528,128]{1,0:T(8,128)(2,1)S(1)} %merge.2.own_a, bf16[528,128]{1,0:T(8,128)(2,1)S(1)} %collective-permute-done.2.own_b, bf16[528,128]{1,0:T(8,128)(2,1)S(1)} %collective-permute-done.3.other_a, bf16[528,128]{1,0:T(8,128)(2,1)S(1)} %merge.3.other_b, ...), custom_call_target="tpu_custom_call" | custom-call | tf_op jit(solution)/shard_map/project/pallas_call | solution.py:440
  98.8 8.4 %collective-permute-done.11.received = bf16[32,2048]{1,0:T(8,128)(2,1)S(1)} collective-permute-done((bf16[32,2048]{1,0:T(8,128)(2,1)S(1)}, bf16[32,2048]{1,0:T(8,128)(2,1)S(1)}, u32[]{:S(2)}, u32[]{:S(2)}) %collective-permute-start.11) | collective-permute-done | bytes 131104 | tf_op jit(solution)/shard_map/ppermute | solution.py:332
  107.2 0.7 place.1
  (21 shorter events, 0.2 us)
Async XLA Ops:
  0.0 29.9 %collective-permute-start.5 = (bf16[2048,256]{1,0:T(8,128)(2,1)}, bf16[2048,256]{1,0:T(8,128)(2,1)S(1)}, u32[]{:S(2)}, u32[]{:S(2)}) collective-permute-start(bf16[2048,256]{1,0:T(8,128)(2,1)} %refs_0_.3), channel_id=1, source_target_pairs={{0,2},{1,5},{2,0},{3,7},{4,6},{5,1},{6,4},{7,3},{8,10},{9,13},{10,... | collective-permute-start | bytes 3145736 | tf_op jit(solution)/shard_map/ppermute | solution.py:414
  5.1 17.8 %all-to-all-start = ((bf16[8,192,128]{2,1,0:T(8,128)(2,1)}), bf16[8,192,128]{2,1,0:T(8,128)(2,1)S(1)}, u32[]{:S(2)}, u32[]{:S(2)}) async-start(bf16[8,192,128]{2,1,0:T(8,128)(2,1)} %pack.2), calls=%async_computation | async-start | bytes 786432 | tf_op jit(solution)/shard_map/all_to_all | solution.py:345
  8.5 8.4 %collective-permute-start.1 = (bf16[32,2048]{1,0:T(8,128)(2,1)}, bf16[32,2048]{1,0:T(8,128)(2,1)S(1)}, u32[]{:S(2)}, u32[]{:S(2)}) collective-permute-start(bf16[32,2048]{1,0:T(8,128)(2,1)} %refs_0_.2), channel_id=1, source_target_pairs={{0,8},{1,9},{2,10},{3,11},{4,12},{5,13},{6,14},{7,15},{8,0},{9,1},... | collective-permute-start | bytes 393224 | tf_op jit(solution)/shard_map/ppermute | solution.py:332
  11.2 5.7 %collective-permute-start = (s32[3,8]{1,0:T(4,128)}, s32[3,8]{1,0:T(4,128)S(1)}, u32[]{:S(2)}, u32[]{:S(2)}) collective-permute-start(s32[3,8]{1,0:T(4,128)} %bitcast.12), channel_id=1, source_target_pairs={{0,8},{1,9},{2,10},{3,11},{4,12},{5,13},{6,14},{7,15},{8,0},{9,1},... | collective-permute-start | bytes 296 | tf_op jit(solution)/shard_map/ppermute | solution.py:332
  22.8 18.6 %all-to-all-start.2 = ((bf16[8,192,128]{2,1,0:T(8,128)(2,1)}), bf16[8,192,128]{2,1,0:T(8,128)(2,1)S(1)}, u32[]{:S(2)}, u32[]{:S(2)}) async-start(bf16[8,192,128]{2,1,0:T(8,128)(2,1)} %pack.3), calls=%async_computation.2 | async-start | bytes 786432 | tf_op jit(solution)/shard_map/all_to_all | solution.py:345
  27.8 17.8 %copy-start = (bf16[2048,256]{1,0:T(8,128)(2,1)S(1)}, bf16[2048,256]{1,0:T(8,128)(2,1)}, u32[]{:S(2)}) copy-start(bf16[2048,256]{1,0:T(8,128)(2,1)} %refs_0_.3) | copy-start | bytes 3145732
  27.9 18.8 %collective-permute-start.7 = (bf16[2048,256]{1,0:T(8,128)(2,1)}, bf16[2048,256]{1,0:T(8,128)(2,1)}, u32[]{:S(2)}, u32[]{:S(2)}) collective-permute-start(bf16[2048,256]{1,0:T(8,128)(2,1)} %refs_0_.3), channel_id=1, source_target_pairs={{0,4},{1,3},{2,6},{3,1},{4,0},{5,7},{6,2},{7,5},{8,12},{9,11},{10,... | collective-permute-start | bytes 3145736 | tf_op jit(solution)/shard_map/ppermute | solution.py:414
  29.9 30.3 %collective-permute-start.9 = (bf16[2048,256]{1,0:T(8,128)(2,1)S(1)}, bf16[2048,256]{1,0:T(8,128)(2,1)}, u32[]{:S(2)}, u32[]{:S(2)}) collective-permute-start(bf16[2048,256]{1,0:T(8,128)(2,1)S(1)} %collective-permute-done.5.refs_2_), channel_id=1, source_target_pairs={{0,4},{1,3},{2,6},{3,1},{4,0},{5,7},{6,2},{7,5},{8,12},{9,11},{10,... | collective-permute-start | bytes 3145736 | tf_op jit(solution)/shard_map/ppermute | solution.py:414
  41.5 30.3 %all-to-all-start.1 = ((bf16[8,208,128]{2,1,0:T(8,128)(2,1)}), bf16[8,208,128]{2,1,0:T(8,128)(2,1)S(1)}, u32[]{:S(2)}, u32[]{:S(2)}) async-start(bf16[8,208,128]{2,1,0:T(8,128)(2,1)} %attend.2), calls=%async_computation.1 | async-start | bytes 851968 | tf_op jit(solution)/shard_map/all_to_all | solution.py:345
  45.6 29.9 %copy-start.1 = (bf16[32,2048]{1,0:T(8,128)(2,1)S(1)}, bf16[32,2048]{1,0:T(8,128)(2,1)}, u32[]{:S(2)}) copy-start(bf16[32,2048]{1,0:T(8,128)(2,1)} %refs_0_.2) | copy-start | bytes 393220
  45.6 29.9 %copy-start.3 = (bf16[32,512]{1,0:T(8,128)(2,1)S(1)}, bf16[32,512]{1,0:T(8,128)(2,1)}, u32[]{:S(2)}) copy-start(bf16[32,512]{1,0:T(8,128)(2,1)} %refs_1_.1) | copy-start | bytes 98308
  45.7 29.9 %copy-start.4 = (bf16[32,512]{1,0:T(8,128)(2,1)S(1)}, bf16[32,512]{1,0:T(8,128)(2,1)}, u32[]{:S(2)}) copy-start(bf16[32,512]{1,0:T(8,128)(2,1)} %refs_2_.1) | copy-start | bytes 98308
  45.7 29.9 %copy-start.5 = (s32[8,3]{0,1:T(4,128)S(1)}, s32[8,3]{0,1:T(4,128)}, u32[]{:S(2)}) copy-start(s32[8,3]{0,1:T(4,128)} %param.12) | copy-start | bytes 292
  45.7 40.3 %collective-permute-start.4 = (bf16[2048,256]{1,0:T(8,128)(2,1)S(1)}, bf16[2048,256]{1,0:T(8,128)(2,1)}, u32[]{:S(2)}, u32[]{:S(2)}) collective-permute-start(bf16[2048,256]{1,0:T(8,128)(2,1)S(1)} %copy-done), channel_id=1, source_target_pairs={{0,1},{1,0},{2,3},{3,2},{4,5},{5,4},{6,7},{7,6},{8,9},{9,8},{10,11... | collective-permute-start | bytes 3145736 | tf_op jit(solution)/shard_map/ppermute | solution.py:414
  46.2 47.9 %collective-permute-start.6 = (bf16[2048,256]{1,0:T(8,128)(2,1)S(1)}, bf16[2048,256]{1,0:T(8,128)(2,1)}, u32[]{:S(2)}, u32[]{:S(2)}) collective-permute-start(bf16[2048,256]{1,0:T(8,128)(2,1)S(1)} %collective-permute-done.5.refs_2_), channel_id=1, source_target_pairs={{0,1},{1,0},{2,3},{3,2},{4,5},{5,4},{6,7},{7,6},{8,9},{9,8},{10,11... | collective-permute-start | bytes 3145736 | tf_op jit(solution)/shard_map/ppermute | solution.py:414
  46.6 47.5 %collective-permute-start.8 = (bf16[2048,256]{1,0:T(8,128)(2,1)}, bf16[2048,256]{1,0:T(8,128)(2,1)}, u32[]{:S(2)}, u32[]{:S(2)}) collective-permute-start(bf16[2048,256]{1,0:T(8,128)(2,1)} %collective-permute-done.7.refs_4_), channel_id=1, source_target_pairs={{0,1},{1,0},{2,3},{3,2},{4,5},{5,4},{6,7},{7,6},{8,9},{9,8},{10,11... | collective-permute-start | bytes 3145736 | tf_op jit(solution)/shard_map/ppermute | solution.py:414
  60.2 34.0 %collective-permute-start.10 = (bf16[2048,256]{1,0:T(8,128)(2,1)}, bf16[2048,256]{1,0:T(8,128)(2,1)}, u32[]{:S(2)}, u32[]{:S(2)}) collective-permute-start(bf16[2048,256]{1,0:T(8,128)(2,1)} %collective-permute-done.9.refs_6_), channel_id=1, source_target_pairs={{0,1},{1,0},{2,3},{3,2},{4,5},{5,4},{6,7},{7,6},{8,9},{9,8},{10,11... | collective-permute-start | bytes 3145736 | tf_op jit(solution)/shard_map/ppermute | solution.py:414
  71.0 0.8 copy-start.2
  71.8 13.1 %all-to-all-start.3 = ((bf16[8,208,128]{2,1,0:T(8,128)(2,1)}), bf16[8,208,128]{2,1,0:T(8,128)(2,1)S(1)}, u32[]{:S(2)}, u32[]{:S(2)}) async-start(bf16[8,208,128]{2,1,0:T(8,128)(2,1)} %copy-done.2), calls=%async_computation.3 | async-start | bytes 851968 | tf_op jit(solution)/shard_map/all_to_all | solution.py:345
  77.4 9.9 %collective-permute-start.3 = (bf16[528,128]{1,0:T(8,128)(2,1)S(1)}, bf16[528,128]{1,0:T(8,128)(2,1)S(1)}, u32[]{:S(2)}, u32[]{:S(2)}) collective-permute-start(bf16[528,128]{1,0:T(8,128)(2,1)S(1)} %merge.2.own_a), channel_id=1, source_target_pairs={{0,8},{1,9},{2,10},{3,11},{4,12},{5,13},{6,14},{7,15},{8,0},{9,1},... | collective-permute-start | bytes 405512 | tf_op jit(solution)/shard_map/ppermute | solution.py:332
  85.9 8.2 %collective-permute-start.2 = (bf16[528,128]{1,0:T(8,128)(2,1)S(1)}, bf16[528,128]{1,0:T(8,128)(2,1)S(1)}, u32[]{:S(2)}, u32[]{:S(2)}) collective-permute-start(bf16[528,128]{1,0:T(8,128)(2,1)S(1)} %merge.3.other_b), channel_id=1, source_target_pairs={{0,8},{1,9},{2,10},{3,11},{4,12},{5,13},{6,14},{7,15},{8,0},{9,1},... | collective-permute-start | bytes 405512 | tf_op jit(solution)/shard_map/ppermute | solution.py:332
  98.7 8.5 %collective-permute-start.11 = (bf16[32,2048]{1,0:T(8,128)(2,1)S(1)}, bf16[32,2048]{1,0:T(8,128)(2,1)S(1)}, u32[]{:S(2)}, u32[]{:S(2)}) collective-permute-start(bf16[32,2048]{1,0:T(8,128)(2,1)S(1)} %get-tuple-element.8), channel_id=1, source_target_pairs={{0,8},{1,9},{2,10},{3,11},{4,12},{5,13},{6,14},{7,15},{8,0},{9,1},... | collective-permute-start | bytes 393224 | tf_op jit(solution)/shard_map/ppermute | solution.py:332

commit v7 on v6

--- a/solution.py
+++ b/solution.py
@@ -275,21 +275,14 @@
     attended[...] = combine(tall, first, second)
 
 
-def project_kernel(own_a, own_b, other_a, other_b, places, *refs):
-    weights = refs[:-2]
-    own_out, other_out = refs[-2:]
+def project_kernel(first, second, places, *refs):
+    weights, out = refs[:-1], refs[-1]
     width = weights[0].shape[1]
-    tall = (own_a.shape[0] - STAT_ROWS) // KVH
-    rows = tall // GROUP
-    left = jnp.concatenate(
-        [combine(tall, own_a, own_b), combine(tall, other_a, other_b)], axis=0
-    )
+    left = combine((first.shape[0] - STAT_ROWS) // KVH, first, second)
     for i, weight in enumerate(weights):
         made = jnp.dot(left, weight[...], preferred_element_type=jnp.float32)
-        made = made.astype(jnp.bfloat16)
         at = pl.ds(pl.multiple_of(places[i] * width, width), width)
-        own_out[:, at] = made[:rows, :]
-        other_out[:, at] = made[rows:, :]
+        out[:, at] = made.astype(jnp.bfloat16)
 
 
 def place_kernel(first, own, received, out):
@@ -389,7 +382,7 @@
     near_partial = attend(near)
     near_back = spread(near_partial)
     far_partial = attend(far)
-    far_back = spread(far_partial)
+    far_back = on_chip(spread(far_partial))
     own_a = merge(own_list, near_back, (queries, new_keys, new_values))
     other_b = merge(other_list, far_back, ())
     other_a = mirrored(own_a)
@@ -437,15 +430,21 @@
     places = jnp.stack(
         [(me % half) ^ (even + odd_core * (odd - even)) for even, odd in places]
     ).astype(jnp.int32)
-    own_out, other_out = pl.pallas_call(
-        project_kernel,
-        out_shape=[jax.ShapeDtypeStruct((row_total, half * width), jnp.bfloat16)] * 2,
-        in_specs=[VMEM] * 4 + [SMEM] + [VMEM] * half,
-        out_specs=[VMEM, VMEM],
-        compiler_params=PROJECT,
-        name="project",
-    )(own_a, own_b, other_a, other_b, places, *[on_chip(part) for part in gathered])
+    gathered = [on_chip(part) for part in gathered]
+
+    def project(first, second):
+        return pl.pallas_call(
+            project_kernel,
+            out_shape=jax.ShapeDtypeStruct((row_total, half * width), jnp.bfloat16),
+            in_specs=[VMEM] * 2 + [SMEM] + [VMEM] * half,
+            out_specs=VMEM,
+            compiler_params=PROJECT,
+            name="project",
+        )(first, second, places, *gathered)
+
+    other_out = project(other_a, other_b)
     received = mirrored(other_out)
+    own_out = project(own_a, own_b)
     return pl.pallas_call(
         place_kernel,
         out_shape=jax.ShapeDtypeStruct((row_total, members * width), jnp.bfloat16),

time: 108 us -> 106 us (0.981)
  waiting for transfers between devices: 47.4 us -> 33 us
  Pallas kernels: 33.8 us -> 38.9 us
  local copies, waits for them, and re-layouts: 0.87 us -> 5.13 us
  starting transfers between devices: 25.7 us -> 28 us
    ppermute x5, waiting for transfers between devices: 21.7 us -> 11 us  [mirrored(): lax.ppermute(array, 'seq', [(i, (i + half) % members) for i in range(memb...]
    unnamed x12 -> x22, local copies, waits for them, and re-layouts: 0.79 us -> 5.04 us
    pallas_call x1 -> x2, Pallas kernels: 4.58 us -> 8.4 us  [project(): pl.pallas_call(project_kernel, out_shape=jax.ShapeDtypeStruct((row_total,...]
    ppermute x7, waiting for transfers between devices: 13.8 us -> 11.7 us  [exchanged(): lax.ppermute(array, 'seq', [(i, i ^ (odd_step if i & 1 else even_step)) f...]
    pallas_call x2, Pallas kernels: 2.87 us -> 4.88 us  [merge(): pl.pallas_call(functools.partial(merge_kernel, half, capacity, bool(own))...]
    all_to_all x4, waiting for transfers between devices: 11.9 us -> 10.2 us  [spread(): lax.all_to_all(array, 'seq', split_axis=0, concat_axis=0, tiled=True, axi...]
    ppermute x5, starting transfers between devices: 3.49 us -> 5.05 us  [mirrored(): lax.ppermute(array, 'seq', [(i, (i + half) % members) for i in range(memb...]
  transfers between devices with their start and end apart: 16 -> 16, of which waited for: 8 -> 6; matrix products, arithmetic and copies ran while one was open for 0% -> 0% of each run, Pallas kernels for 26% -> 36%
where the time goes in v7:
time: 106 us; the launch traced here: 105 us
  Pallas kernels  38.9 us (37%)
  waiting for transfers between devices  33 us (31%)
  starting transfers between devices  28 us (26%)
  local copies, waits for them, and re-layouts  5.13 us (5%)
    pallas_call x2, Pallas kernels, attend(): pl.pallas_call(attend_kernel, out_shape=jax.ShapeDtypeStruct((half, KVH *...  21.6 us
    all_to_all x4, starting transfers between devices, spread(): lax.all_to_all(array, 'seq', split_axis=0, concat_axis=0, tiled=True, axi...  16.7 us
    ppermute x7, waiting for transfers between devices, exchanged(): lax.ppermute(array, 'seq', [(i, i ^ (odd_step if i & 1 else even_step)) f...  11.7 us
    ppermute x5, waiting for transfers between devices, mirrored(): lax.ppermute(array, 'seq', [(i, (i + half) % members) for i in range(memb...  11 us
    all_to_all x4, waiting for transfers between devices, spread(): lax.all_to_all(array, 'seq', split_axis=0, concat_axis=0, tiled=True, axi...  10.2 us
    pallas_call x2, Pallas kernels, project(): pl.pallas_call(project_kernel, out_shape=jax.ShapeDtypeStruct((row_total,...  8.4 us
    ppermute x7, starting transfers between devices, exchanged(): lax.ppermute(array, 'seq', [(i, i ^ (odd_step if i & 1 else even_step)) f...  6.23 us
    ppermute x5, starting transfers between devices, mirrored(): lax.ppermute(array, 'seq', [(i, (i + half) % members) for i in range(memb...  5.05 us
  transfers between devices with their start and end apart: 16, of which 6 were waited for; matrix products, arithmetic and copies ran while one was open for 0% of the time, Pallas kernels for 36%

profile of v7, /device:TPU:0, one launch (start us, length us, event | category | flops | bytes accessed | tf_op | source)
XLA Modules:
  0.0 105.1 jit_solution(4201899698887594512)
XLA Ops:
  0.0 3.0 %collective-permute-start.4 = (bf16[2048,256]{1,0:T(8,128)(2,1)}, bf16[2048,256]{1,0:T(8,128)(2,1)S(1)}, u32[]{:S(2)}, u32[]{:S(2)}) collective-permute-start(bf16[2048,256]{1,0:T(8,128)(2,1)} %refs_0_.5), channel_id=1, source_target_pairs={{0,2},{1,5},{2,0},{3,7},{4,6},{5,1},{6,4},{7,3},{8,10},{9,13},{10,... | collective-permute-start | bytes 3145736 | tf_op jit(solution)/shard_map/ppermute | solution.py:407
  3.0 2.1 %pack.2 = bf16[8,192,128]{2,1,0:T(8,128)(2,1)} custom-call(s32[1]{0:T(128)} %bitcast.1.base, s32[3,8]{1,0:T(4,128)} %bitcast.11, bf16[32,2048]{1,0:T(8,128)(2,1)} %refs_0_.3), custom_call_target="tpu_custom_call" | custom-call | tf_op jit(solution)/shard_map/pack/pallas_call | solution.py:328
  5.1 3.5 %all-to-all-start = ((bf16[8,192,128]{2,1,0:T(8,128)(2,1)}), bf16[8,192,128]{2,1,0:T(8,128)(2,1)S(1)}, u32[]{:S(2)}, u32[]{:S(2)}) async-start(bf16[8,192,128]{2,1,0:T(8,128)(2,1)} %pack.2), calls=%async_computation | async-start | bytes 786432 | tf_op jit(solution)/shard_map/all_to_all | solution.py:338
  8.6 2.7 %collective-permute-start.1 = (bf16[32,2048]{1,0:T(8,128)(2,1)}, bf16[32,2048]{1,0:T(8,128)(2,1)S(1)}, u32[]{:S(2)}, u32[]{:S(2)}) collective-permute-start(bf16[32,2048]{1,0:T(8,128)(2,1)} %refs_0_.3), channel_id=1, source_target_pairs={{0,8},{1,9},{2,10},{3,11},{4,12},{5,13},{6,14},{7,15},{8,0},{9,1},... | collective-permute-start | bytes 393224 | tf_op jit(solution)/shard_map/ppermute | solution.py:325
  11.5 5.4 %collective-permute-done.listed = s32[3,8]{1,0:T(4,128)S(1)} collective-permute-done((s32[3,8]{1,0:T(4,128)}, s32[3,8]{1,0:T(4,128)S(1)}, u32[]{:S(2)}, u32[]{:S(2)}) %collective-permute-start) | collective-permute-done | bytes 128 | tf_op jit(solution)/shard_map/ppermute | solution.py:325
  16.9 1.2 %pack.3 = bf16[8,192,128]{2,1,0:T(8,128)(2,1)} custom-call(s32[1]{0:T(128)} %bitcast.1.base, s32[3,8]{1,0:T(4,128)S(1)} %collective-permute-done.listed, bf16[32,2048]{1,0:T(8,128)(2,1)S(1)} %collective-permute-done.1.queries), custom_call_target="tpu_custom_call" | custom-call | tf_op jit(solution)/shard_map/pack/pallas_call | solution.py:328
  18.1 4.8 %all-to-all-done.queries = bf16[8,192,128]{2,1,0:T(8,128)(2,1)S(1)} async-done(((bf16[8,192,128]{2,1,0:T(8,128)(2,1)}), bf16[8,192,128]{2,1,0:T(8,128)(2,1)S(1)}, u32[]{:S(2)}, u32[]{:S(2)}) %all-to-all-start) | async-done | bytes 393248 | tf_op jit(solution)/shard_map/all_to_all | solution.py:338
  22.8 0.8 copy-done.6
  23.6 5.0 %all-to-all-start.2 = ((bf16[8,192,128]{2,1,0:T(8,128)(2,1)}), bf16[8,192,128]{2,1,0:T(8,128)(2,1)S(1)}, u32[]{:S(2)}, u32[]{:S(2)}) async-start(bf16[8,192,128]{2,1,0:T(8,128)(2,1)} %pack.3), calls=%async_computation.2 | async-start | bytes 786432 | tf_op jit(solution)/shard_map/all_to_all | solution.py:338
  28.6 2.0 %collective-permute-start.6 = (bf16[2048,256]{1,0:T(8,128)(2,1)}, bf16[2048,256]{1,0:T(8,128)(2,1)S(1)}, u32[]{:S(2)}, u32[]{:S(2)}) collective-permute-start(bf16[2048,256]{1,0:T(8,128)(2,1)} %refs_0_.5), channel_id=1, source_target_pairs={{0,4},{1,3},{2,6},{3,1},{4,0},{5,7},{6,2},{7,5},{8,12},{9,11},{10,... | collective-permute-start | bytes 3145736 | tf_op jit(solution)/shard_map/ppermute | solution.py:407
  30.7 1.0 copy-done.7
  31.7 10.8 %attend.2 = bf16[8,208,128]{2,1,0:T(8,128)(2,1)S(1)} custom-call(bf16[8,192,128]{2,1,0:T(8,128)(2,1)S(1)} %copy-done.7, bf16[4096,512]{1,0:T(8,128)(2,1)} %keys.3, bf16[4096,512]{1,0:T(8,128)(2,1)} %values.3), custom_call_target="tpu_custom_call" | custom-call | flops 3221225472 | bytes 8388608 | tf_op jit(solution)/shard_map/attend/pallas_call | solution.py:343
  42.5 0.8 copy-done.2
  43.3 0.8 copy-done.4
  44.0 4.1 %all-to-all-start.1 = ((bf16[8,208,128]{2,1,0:T(8,128)(2,1)}), bf16[8,208,128]{2,1,0:T(8,128)(2,1)}, u32[]{:S(2)}, u32[]{:S(2)}) async-start(bf16[8,208,128]{2,1,0:T(8,128)(2,1)} %copy-done.2), calls=%async_computation.1 | async-start | bytes 851968 | tf_op jit(solution)/shard_map/all_to_all | solution.py:338
  48.2 0.6 collective-permute-start.3
  48.8 0.4 collective-permute-start.7
  49.2 11.7 %collective-permute-done.8.refs_6_ = bf16[2048,256]{1,0:T(8,128)(2,1)} collective-permute-done((bf16[2048,256]{1,0:T(8,128)(2,1)S(1)}, bf16[2048,256]{1,0:T(8,128)(2,1)}, u32[]{:S(2)}, u32[]{:S(2)}) %collective-permute-start.8) | collective-permute-done | bytes 1048608 | tf_op jit(solution)/shard_map/ppermute | solution.py:407
  61.0 1.0 copy-done.5
  62.0 10.8 %attend.3 = bf16[8,208,128]{2,1,0:T(8,128)(2,1)S(1)} custom-call(bf16[8,192,128]{2,1,0:T(8,128)(2,1)S(1)} %copy-done.5, bf16[4096,512]{1,0:T(8,128)(2,1)} %keys.3, bf16[4096,512]{1,0:T(8,128)(2,1)} %values.3), custom_call_target="tpu_custom_call" | custom-call | flops 3221225472 | bytes 8388608 | tf_op jit(solution)/shard_map/attend/pallas_call | solution.py:343
  72.8 0.8 copy-done.3
  73.6 4.1 %all-to-all-start.3 = ((bf16[8,208,128]{2,1,0:T(8,128)(2,1)}), bf16[8,208,128]{2,1,0:T(8,128)(2,1)}, u32[]{:S(2)}, u32[]{:S(2)}) async-start(bf16[8,208,128]{2,1,0:T(8,128)(2,1)} %copy-done.3), calls=%async_computation.3 | async-start | bytes 851968 | tf_op jit(solution)/shard_map/all_to_all | solution.py:338
  77.7 2.8 %merge.2.first = bf16[528,128]{1,0:T(8,128)(2,1)S(1)} custom-call(s32[1]{0:T(128)} %bitcast.1.base, s32[3,8]{1,0:T(4,128)S(1)} %bitcast.13, bf16[32,2048]{1,0:T(8,128)(2,1)S(1)} %copy-done.1, bf16[32,512]{1,0:T(8,128)(2,1)S(1)} %copy-done.8, bf16[32,512]{1,0:T(8,128)(2,1)S(1)} %copy-done.9, bf16[8,208,128]{2,1,0:T(8,128)(2,1)} %all-to-all-done.1.refs_3_), custom_call_target="tpu_custom_call" | custom-call | tf_op jit(solution)/shard_map/merge/pallas_call | solution.py:366
  80.6 0.6 collective-permute-start.10
  81.1 5.5 %all-to-all-done.3.refs_0_ = bf16[8,208,128]{2,1,0:T(8,128)(2,1)} async-done(((bf16[8,208,128]{2,1,0:T(8,128)(2,1)}), bf16[8,208,128]{2,1,0:T(8,128)(2,1)}, u32[]{:S(2)}, u32[]{:S(2)}) %all-to-all-start.3) | async-done | bytes 426016 | tf_op jit(solution)/shard_map/all_to_all | solution.py:338
  86.6 2.1 %merge.3.second = bf16[528,128]{1,0:T(8,128)(2,1)S(1)} custom-call(s32[1]{0:T(128)} %bitcast.1.base, s32[3,8]{1,0:T(4,128)S(1)} %collective-permute-done.listed, bf16[8,208,128]{2,1,0:T(8,128)(2,1)} %all-to-all-done.3.refs_0_), custom_call_target="tpu_custom_call" | custom-call | tf_op jit(solution)/shard_map/merge/pallas_call | solution.py:366
  88.9 1.6 %collective-permute-done.10.first = bf16[528,128]{1,0:T(8,128)(2,1)} collective-permute-done((bf16[528,128]{1,0:T(8,128)(2,1)S(1)}, bf16[528,128]{1,0:T(8,128)(2,1)}, u32[]{:S(2)}, u32[]{:S(2)}) %collective-permute-start.10) | collective-permute-done | bytes 135200 | tf_op jit(solution)/shard_map/ppermute | solution.py:325
  90.5 4.2 %project.3 = bf16[32,2048]{1,0:T(8,128)(2,1)S(1)} custom-call(bf16[528,128]{1,0:T(8,128)(2,1)} %collective-permute-done.10.first, bf16[528,128]{1,0:T(8,128)(2,1)S(1)} %merge.3.second, s32[8]{0:T(128)S(1)} %stack.35.places, bf16[2048,256]{1,0:T(8,128)(2,1)S(1)} %copy-done, bf16[2048,256]{1,0:T(8,128)(2,1)} %collective-permute-done.3.refs_1_, ...), custom_call_target="tpu_custom_call" | custom-call | tf_op jit(solution)/shard_map/project/pallas_call | solution.py:436
  94.7 1.4 %collective-permute-start.11 = (bf16[32,2048]{1,0:T(8,128)(2,1)S(1)}, bf16[32,2048]{1,0:T(8,128)(2,1)S(1)}, u32[]{:S(2)}, u32[]{:S(2)}) collective-permute-start(bf16[32,2048]{1,0:T(8,128)(2,1)S(1)} %project.3), channel_id=1, source_target_pairs={{0,8},{1,9},{2,10},{3,11},{4,12},{5,13},{6,14},{7,15},{8,0},{9,1},... | collective-permute-start | bytes 393224 | tf_op jit(solution)/shard_map/ppermute | solution.py:325
  96.1 4.1 %collective-permute-done.2.second = bf16[528,128]{1,0:T(8,128)(2,1)S(1)} collective-permute-done((bf16[528,128]{1,0:T(8,128)(2,1)S(1)}, bf16[528,128]{1,0:T(8,128)(2,1)S(1)}, u32[]{:S(2)}, u32[]{:S(2)}) %collective-permute-start.2) | collective-permute-done | bytes 135200 | tf_op jit(solution)/shard_map/ppermute | solution.py:325
  100.2 4.2 %project.2.own = bf16[32,2048]{1,0:T(8,128)(2,1)S(1)} custom-call(bf16[528,128]{1,0:T(8,128)(2,1)S(1)} %merge.2.first, bf16[528,128]{1,0:T(8,128)(2,1)S(1)} %collective-permute-done.2.second, s32[8]{0:T(128)S(1)} %stack.35.places, bf16[2048,256]{1,0:T(8,128)(2,1)S(1)} %copy-done, bf16[2048,256]{1,0:T(8,128)(2,1)} %collective-permute-done.3.refs_1_, ...), custom_call_target="tpu_custom_call" | custom-call | tf_op jit(solution)/shard_map/project/pallas_call | solution.py:436
  104.4 0.7 place.1
  (32 shorter events, 0.8 us)
Async XLA Ops:
  0.0 30.6 %collective-permute-start.4 = (bf16[2048,256]{1,0:T(8,128)(2,1)}, bf16[2048,256]{1,0:T(8,128)(2,1)S(1)}, u32[]{:S(2)}, u32[]{:S(2)}) collective-permute-start(bf16[2048,256]{1,0:T(8,128)(2,1)} %refs_0_.5), channel_id=1, source_target_pairs={{0,2},{1,5},{2,0},{3,7},{4,6},{5,1},{6,4},{7,3},{8,10},{9,13},{10,... | collective-permute-start | bytes 3145736 | tf_op jit(solution)/shard_map/ppermute | solution.py:407
  5.1 17.7 %all-to-all-start = ((bf16[8,192,128]{2,1,0:T(8,128)(2,1)}), bf16[8,192,128]{2,1,0:T(8,128)(2,1)S(1)}, u32[]{:S(2)}, u32[]{:S(2)}) async-start(bf16[8,192,128]{2,1,0:T(8,128)(2,1)} %pack.2), calls=%async_computation | async-start | bytes 786432 | tf_op jit(solution)/shard_map/all_to_all | solution.py:338
  8.6 8.4 %collective-permute-start.1 = (bf16[32,2048]{1,0:T(8,128)(2,1)}, bf16[32,2048]{1,0:T(8,128)(2,1)S(1)}, u32[]{:S(2)}, u32[]{:S(2)}) collective-permute-start(bf16[32,2048]{1,0:T(8,128)(2,1)} %refs_0_.3), channel_id=1, source_target_pairs={{0,8},{1,9},{2,10},{3,11},{4,12},{5,13},{6,14},{7,15},{8,0},{9,1},... | collective-permute-start | bytes 393224 | tf_op jit(solution)/shard_map/ppermute | solution.py:325
  11.2 5.7 %collective-permute-start = (s32[3,8]{1,0:T(4,128)}, s32[3,8]{1,0:T(4,128)S(1)}, u32[]{:S(2)}, u32[]{:S(2)}) collective-permute-start(s32[3,8]{1,0:T(4,128)} %bitcast.12), channel_id=1, source_target_pairs={{0,8},{1,9},{2,10},{3,11},{4,12},{5,13},{6,14},{7,15},{8,0},{9,1},... | collective-permute-start | bytes 296 | tf_op jit(solution)/shard_map/ppermute | solution.py:325
  22.8 0.8 copy-start.6
  23.6 19.7 %all-to-all-start.2 = ((bf16[8,192,128]{2,1,0:T(8,128)(2,1)}), bf16[8,192,128]{2,1,0:T(8,128)(2,1)S(1)}, u32[]{:S(2)}, u32[]{:S(2)}) async-start(bf16[8,192,128]{2,1,0:T(8,128)(2,1)} %pack.3), calls=%async_computation.2 | async-start | bytes 786432 | tf_op jit(solution)/shard_map/all_to_all | solution.py:338
  28.6 19.6 %copy-start = (bf16[2048,256]{1,0:T(8,128)(2,1)S(1)}, bf16[2048,256]{1,0:T(8,128)(2,1)}, u32[]{:S(2)}) copy-start(bf16[2048,256]{1,0:T(8,128)(2,1)} %refs_0_.5) | copy-start | bytes 3145732
  28.6 20.2 %collective-permute-start.6 = (bf16[2048,256]{1,0:T(8,128)(2,1)}, bf16[2048,256]{1,0:T(8,128)(2,1)S(1)}, u32[]{:S(2)}, u32[]{:S(2)}) collective-permute-start(bf16[2048,256]{1,0:T(8,128)(2,1)} %refs_0_.5), channel_id=1, source_target_pairs={{0,4},{1,3},{2,6},{3,1},{4,0},{5,7},{6,2},{7,5},{8,12},{9,11},{10,... | collective-permute-start | bytes 3145736 | tf_op jit(solution)/shard_map/ppermute | solution.py:407
  30.6 30.3 %collective-permute-start.8 = (bf16[2048,256]{1,0:T(8,128)(2,1)S(1)}, bf16[2048,256]{1,0:T(8,128)(2,1)}, u32[]{:S(2)}, u32[]{:S(2)}) collective-permute-start(bf16[2048,256]{1,0:T(8,128)(2,1)S(1)} %collective-permute-done.4.refs_2_), channel_id=1, source_target_pairs={{0,4},{1,3},{2,6},{3,1},{4,0},{5,7},{6,2},{7,5},{8,12},{9,11},{10,... | collective-permute-start | bytes 3145736 | tf_op jit(solution)/shard_map/ppermute | solution.py:407
  30.7 1.0 copy-start.7
  42.5 0.8 copy-start.2
  43.3 0.8 copy-start.4
  43.3 34.4 %copy-start.10 = (s32[8,3]{0,1:T(4,128)S(1)}, s32[8,3]{0,1:T(4,128)}, u32[]{:S(2)}) copy-start(s32[8,3]{0,1:T(4,128)} %param.12) | copy-start | bytes 292
  44.0 29.5 %all-to-all-start.1 = ((bf16[8,208,128]{2,1,0:T(8,128)(2,1)}), bf16[8,208,128]{2,1,0:T(8,128)(2,1)}, u32[]{:S(2)}, u32[]{:S(2)}) async-start(bf16[8,208,128]{2,1,0:T(8,128)(2,1)} %copy-done.2), calls=%async_computation.1 | async-start | bytes 851968 | tf_op jit(solution)/shard_map/all_to_all | solution.py:338
  48.2 29.5 %copy-start.1 = (bf16[32,2048]{1,0:T(8,128)(2,1)S(1)}, bf16[32,2048]{1,0:T(8,128)(2,1)}, u32[]{:S(2)}) copy-start(bf16[32,2048]{1,0:T(8,128)(2,1)} %refs_0_.3) | copy-start | bytes 393220
  48.2 40.5 %collective-permute-start.3 = (bf16[2048,256]{1,0:T(8,128)(2,1)S(1)}, bf16[2048,256]{1,0:T(8,128)(2,1)}, u32[]{:S(2)}, u32[]{:S(2)}) collective-permute-start(bf16[2048,256]{1,0:T(8,128)(2,1)S(1)} %copy-done), channel_id=1, source_target_pairs={{0,1},{1,0},{2,3},{3,2},{4,5},{5,4},{6,7},{7,6},{8,9},{9,8},{10,11... | collective-permute-start | bytes 3145736 | tf_op jit(solution)/shard_map/ppermute | solution.py:407
  48.7 41.7 %collective-permute-start.5 = (bf16[2048,256]{1,0:T(8,128)(2,1)S(1)}, bf16[2048,256]{1,0:T(8,128)(2,1)}, u32[]{:S(2)}, u32[]{:S(2)}) collective-permute-start(bf16[2048,256]{1,0:T(8,128)(2,1)S(1)} %collective-permute-done.4.refs_2_), channel_id=1, source_target_pairs={{0,1},{1,0},{2,3},{3,2},{4,5},{5,4},{6,7},{7,6},{8,9},{9,8},{10,11... | collective-permute-start | bytes 3145736 | tf_op jit(solution)/shard_map/ppermute | solution.py:407
  48.8 41.6 %collective-permute-start.7 = (bf16[2048,256]{1,0:T(8,128)(2,1)S(1)}, bf16[2048,256]{1,0:T(8,128)(2,1)}, u32[]{:S(2)}, u32[]{:S(2)}) collective-permute-start(bf16[2048,256]{1,0:T(8,128)(2,1)S(1)} %collective-permute-done.6.refs_4_), channel_id=1, source_target_pairs={{0,1},{1,0},{2,3},{3,2},{4,5},{5,4},{6,7},{7,6},{8,9},{9,8},{10,11... | collective-permute-start | bytes 3145736 | tf_op jit(solution)/shard_map/ppermute | solution.py:407
  60.9 29.6 %collective-permute-start.9 = (bf16[2048,256]{1,0:T(8,128)(2,1)}, bf16[2048,256]{1,0:T(8,128)(2,1)}, u32[]{:S(2)}, u32[]{:S(2)}) collective-permute-start(bf16[2048,256]{1,0:T(8,128)(2,1)} %collective-permute-done.8.refs_6_), channel_id=1, source_target_pairs={{0,1},{1,0},{2,3},{3,2},{4,5},{5,4},{6,7},{7,6},{8,9},{9,8},{10,11... | collective-permute-start | bytes 3145736 | tf_op jit(solution)/shard_map/ppermute | solution.py:407
  61.0 1.0 copy-start.5
  62.0 15.7 %copy-start.8 = (bf16[32,512]{1,0:T(8,128)(2,1)S(1)}, bf16[32,512]{1,0:T(8,128)(2,1)}, u32[]{:S(2)}) copy-start(bf16[32,512]{1,0:T(8,128)(2,1)} %refs_1_.1) | copy-start | bytes 98308
  62.0 15.7 %copy-start.9 = (bf16[32,512]{1,0:T(8,128)(2,1)S(1)}, bf16[32,512]{1,0:T(8,128)(2,1)}, u32[]{:S(2)}) copy-start(bf16[32,512]{1,0:T(8,128)(2,1)} %refs_2_.1) | copy-start | bytes 98308
  72.8 0.8 copy-start.3
  73.6 13.1 %all-to-all-start.3 = ((bf16[8,208,128]{2,1,0:T(8,128)(2,1)}), bf16[8,208,128]{2,1,0:T(8,128)(2,1)}, u32[]{:S(2)}, u32[]{:S(2)}) async-start(bf16[8,208,128]{2,1,0:T(8,128)(2,1)} %copy-done.3), calls=%async_computation.3 | async-start | bytes 851968 | tf_op jit(solution)/shard_map/all_to_all | solution.py:338
  80.6 9.9 %collective-permute-start.10 = (bf16[528,128]{1,0:T(8,128)(2,1)S(1)}, bf16[528,128]{1,0:T(8,128)(2,1)}, u32[]{:S(2)}, u32[]{:S(2)}) collective-permute-start(bf16[528,128]{1,0:T(8,128)(2,1)S(1)} %merge.2.first), channel_id=1, source_target_pairs={{0,8},{1,9},{2,10},{3,11},{4,12},{5,13},{6,14},{7,15},{8,0},{9,1},... | collective-permute-start | bytes 405512 | tf_op jit(solution)/shard_map/ppermute | solution.py:325
  88.7 11.5 %collective-permute-start.2 = (bf16[528,128]{1,0:T(8,128)(2,1)S(1)}, bf16[528,128]{1,0:T(8,128)(2,1)S(1)}, u32[]{:S(2)}, u32[]{:S(2)}) collective-permute-start(bf16[528,128]{1,0:T(8,128)(2,1)S(1)} %merge.3.second), channel_id=1, source_target_pairs={{0,8},{1,9},{2,10},{3,11},{4,12},{5,13},{6,14},{7,15},{8,0},{9,1},... | collective-permute-start | bytes 405512 | tf_op jit(solution)/shard_map/ppermute | solution.py:325
  94.7 9.7 %collective-permute-start.11 = (bf16[32,2048]{1,0:T(8,128)(2,1)S(1)}, bf16[32,2048]{1,0:T(8,128)(2,1)S(1)}, u32[]{:S(2)}, u32[]{:S(2)}) collective-permute-start(bf16[32,2048]{1,0:T(8,128)(2,1)S(1)} %project.3), channel_id=1, source_target_pairs={{0,8},{1,9},{2,10},{3,11},{4,12},{5,13},{6,14},{7,15},{8,0},{9,1},... | collective-permute-start | bytes 393224 | tf_op jit(solution)/shard_map/ppermute | solution.py:325
